TPU v7x, 128 devices: a whole 4x4x4 slice. The times are simulated.
128 devices in a mesh: grp: 8 (over y, x_lo), bal: 16 (over x_hi, z, core).
Axes of the slice: x: 4 (x_hi: 2, x_lo: 2; x = x_hi * 2 + x_lo), y: 4, z: 4, core: 2. Of those that a mesh axis runs over, the one named last changes fastest.
Arguments:
- events: bfloat16 [8, 8192, 512], P('grp', 'bal'), may hold values from -6 to 6
- cotangent: bfloat16 [8, 8192, 512], P('grp', 'bal'), may hold values from -6 to 6
- lengths: int32 [8, 16], P('grp'), may hold values from 1 to 16, as said below
- gain_in: float32 [512], replicated, may hold values from 0.1 to 1.9
- w_proj: bfloat16 [512, 2048], replicated, may hold values from -0.25 to 0.25
- gain_attn: float32 [512], replicated, may hold values from 0.1 to 1.9
- w_out: bfloat16 [512, 512], replicated, may hold values from -0.25 to 0.25
Outputs:
- d_x: bfloat16 [8, 8192, 512], P('grp', 'bal')
- grad_proj: float32 [512, 2048], replicated
- grad_out: float32 [512, 512], replicated
- grad_gain_in: float32 [512], replicated
- grad_gain_attn: float32 [512], replicated
Inputs may be any that keep to these rules, and one draw needn't show every extreme that they name: A group's 16 lengths count blocks of 64 events and sum to 128; in every group one length equals 16.
All inputs are finite; a program needn't handle non-finite values.
Results may differ from a plain program's by a relative error of at most 0.013.
Values may be sent and summed in bfloat16 or wider, within the bound.
No kernel may reach another device: no remote copies, remote signals or barrier semaphores. Data moves between devices by JAX's collectives and lax.ppermute only.
A program may use at most 256 MiB of HBM per device.

v0:
```python
import math

import jax
import jax.numpy as jnp
from jax import lax
from jax.sharding import PartitionSpec as P

HEADS = 8
BLOCK = 64
LEN_BLK = 16


epsilon = 1e-06


def norm_rows(values):
    mean_value = jnp.mean(values, axis=-1, keepdims=True)
    centred = values - mean_value
    rstd = lax.rsqrt(jnp.mean(centred * centred, axis=-1, keepdims=True) + epsilon)
    return (centred * rstd, rstd)


def silu_slope(values):
    sigma = jax.nn.sigmoid(values)
    return sigma * (1.0 + values * (1.0 - sigma))


def norm_back(grad, normed, rstd):
    return rstd * (
        grad
        - jnp.mean(grad, axis=-1, keepdims=True)
        - normed * jnp.mean(grad * normed, axis=-1, keepdims=True)
    )


def contract_rows(left, right):
    return lax.dot_general(
        left, right, (((0,), (0,)), ((), ())), preferred_element_type=jnp.float32
    )


def contract_cols(left, right):
    return lax.dot_general(
        left, right, (((1,), (1,)), ((), ())), preferred_element_type=jnp.float32
    )


def project_rows(rows, gain_in, w_proj):
    normed, rstd_in = norm_rows(rows.astype(jnp.float32))
    scaled = (normed * gain_in).astype(jnp.bfloat16)
    hidden = jnp.dot(scaled, w_proj, preferred_element_type=jnp.float32)
    active = jax.nn.silu(hidden).astype(jnp.bfloat16)
    return (normed, rstd_in, scaled, hidden, active)


def output_rows(attn, upper, grads_out, gain_attn, w_out):
    normed, rstd = norm_rows(attn.astype(jnp.float32))
    upper_wide = upper.astype(jnp.float32)
    mixed = (normed * gain_attn * upper_wide).astype(jnp.bfloat16)
    d_mixed = contract_cols(grads_out, w_out)
    d_upper = d_mixed * normed * gain_attn
    d_attn = norm_back(d_mixed * gain_attn * upper_wide, normed, rstd).astype(jnp.bfloat16)
    out_term = contract_rows(mixed, grads_out)
    gain_term = jnp.sum(d_mixed * normed * upper_wide, axis=0)
    return (d_upper, d_attn, out_term, gain_term)


def input_rows(grads_out, d_act, hidden, normed, rstd_in, scaled, gain_in, w_proj):
    d_hidden = (d_act * silu_slope(hidden)).astype(jnp.bfloat16)
    proj_term = contract_rows(scaled, d_hidden)
    d_scaled = contract_cols(d_hidden, w_proj)
    d_rows = (
        grads_out.astype(jnp.float32) + norm_back(d_scaled * gain_in, normed, rstd_in)
    ).astype(jnp.bfloat16)
    gain_term = jnp.sum(d_scaled * normed, axis=0)
    return (d_rows, proj_term, gain_term)


def attend_forward(query, keys, values, allowed):
    head_width = query.shape[1] // HEADS
    scale = head_width ** (-0.5)
    outputs = []
    for head in range(HEADS):
        columns = slice(head * head_width, (head + 1) * head_width)
        scores = contract_cols(query[:, columns], keys[:, columns]) * scale
        weights = (jax.nn.silu(scores) * allowed).astype(jnp.bfloat16)
        outputs.append(jnp.dot(weights, values[:, columns], preferred_element_type=jnp.float32))
    return jnp.concatenate(outputs, axis=1).astype(jnp.bfloat16)


def attend_backward(query, keys, values, grad_attn, allowed):
    head_width = query.shape[1] // HEADS
    scale = head_width ** (-0.5)
    grads_query, grads_keys, grads_values = ([], [], [])
    for head in range(HEADS):
        columns = slice(head * head_width, (head + 1) * head_width)
        query_head = query[:, columns]
        key_head = keys[:, columns]
        grad_head = grad_attn[:, columns]
        scores = contract_cols(query_head, key_head) * scale
        weights = (jax.nn.silu(scores) * allowed).astype(jnp.bfloat16)
        grad_weights = contract_cols(grad_head, values[:, columns])
        grad_scores = (grad_weights * silu_slope(scores) * allowed).astype(jnp.bfloat16)
        grads_values.append(contract_rows(weights, grad_head).astype(jnp.bfloat16))
        grads_query.append(
            (jnp.dot(grad_scores, key_head, preferred_element_type=jnp.float32) * scale).astype(
                jnp.bfloat16
            )
        )
        grads_keys.append((contract_rows(grad_scores, query_head) * scale).astype(jnp.bfloat16))
    return (
        jnp.concatenate(grads_query, axis=1),
        jnp.concatenate(grads_keys, axis=1),
        jnp.concatenate(grads_values, axis=1),
    )


def lookup(table, positions):
    entries = jnp.arange(table.shape[0], dtype=jnp.int32)
    picked = jnp.where(entries[None, :] == positions[:, None], table[None, :], 0)
    return jnp.sum(picked, axis=1)


def regroup(table, rows):
    blocks = rows.reshape(table.shape[1], -1)
    moved = jnp.dot(table, blocks, preferred_element_type=jnp.float32)
    return moved.astype(jnp.bfloat16).reshape(-1, rows.shape[1])


def pack_histories(seq_lengths):

    def advance(state, length_now):
        device_rank, held_blocks = state
        fresh = held_blocks + length_now > LEN_BLK
        device_rank = device_rank + fresh.astype(jnp.int32)
        held_blocks = jnp.where(fresh, 0, held_blocks) + length_now
        return ((device_rank, held_blocks), device_rank)

    start_state = (jnp.int32(0), jnp.int32(0))
    final_state, ranks = lax.scan(advance, start_state, seq_lengths)
    return ranks


def held_tiles_map(tile_fn, live_tiles, inputs, tile_rows):
    count = inputs[0].shape[0] // tile_rows
    pieces = tuple((array.reshape((count, tile_rows) + array.shape[1:]) for array in inputs))

    def blank_fn(parts):
        return jax.tree.map(jnp.zeros_like, tile_fn(parts))

    def each_tile(item):
        position, parts = item
        return lax.cond(position < live_tiles, tile_fn, blank_fn, parts)

    return lax.map(each_tile, (jnp.arange(count, dtype=jnp.int32), pieces))


def flatten_tiles(array):
    return array.reshape((-1,) + array.shape[2:])


def whole_layer(rows, grads_out, allowed, live_tiles, tile_rows, gain_in, w_proj, gain_attn, w_out):
    width = rows.shape[1]
    first = held_tiles_map(
        lambda parts: project_rows(parts[0], gain_in, w_proj), live_tiles, (rows,), tile_rows
    )
    normed, rstd_in, scaled, hidden, active = jax.tree.map(flatten_tiles, first)
    upper = active[:, :width]
    values = active[:, width : 2 * width]
    query = active[:, 2 * width : 3 * width]
    keys = active[:, 3 * width :]
    attn = attend_forward(query, keys, values, allowed)
    second = held_tiles_map(
        lambda parts: output_rows(parts[0], parts[1], parts[2], gain_attn, w_out),
        live_tiles,
        (attn, upper, grads_out),
        tile_rows,
    )
    d_upper = flatten_tiles(second[0])
    d_attn = flatten_tiles(second[1])
    out_term = jnp.sum(second[2], axis=0)
    gain_attn_term = jnp.sum(second[3], axis=0)
    d_query, d_keys, d_values = attend_backward(query, keys, values, d_attn, allowed)
    d_act = jnp.concatenate(
        [
            d_upper,
            d_values.astype(jnp.float32),
            d_query.astype(jnp.float32),
            d_keys.astype(jnp.float32),
        ],
        axis=1,
    )
    third = held_tiles_map(
        lambda parts: input_rows(
            parts[0], parts[1], parts[2], parts[3], parts[4], parts[5], gain_in, w_proj
        ),
        live_tiles,
        (grads_out, d_act, hidden, normed, rstd_in, scaled),
        tile_rows,
    )
    d_rows = flatten_tiles(third[0])
    proj_term = jnp.sum(third[1], axis=0)
    gain_in_term = jnp.sum(third[2], axis=0)
    return (d_rows, (proj_term, out_term, gain_in_term, gain_attn_term))


def per_device(events, cotangent, lengths, gain_in, w_proj, gain_attn, w_out):
    peers = lax.axis_size("bal")
    own_index = lax.axis_index("bal")
    local_rows = events[0]
    local_grads = cotangent[0]
    local_blocks = local_rows.shape[0] // BLOCK
    slots = LEN_BLK // peers
    seq_lengths = lengths[0]
    targets = pack_histories(seq_lengths)
    ends = jnp.cumsum(seq_lengths)
    device_ids = jnp.arange(peers, dtype=jnp.int32)
    range_starts = jnp.sum(
        jnp.where(targets[None, :] < device_ids[:, None], seq_lengths[None, :], 0), axis=1
    )
    range_sizes = jnp.sum(
        jnp.where(targets[None, :] == device_ids[:, None], seq_lengths[None, :], 0), axis=1
    )
    flat_blocks = own_index + peers * jnp.arange(local_blocks, dtype=jnp.int32)
    owner_seq = jnp.sum((ends[None, :] <= flat_blocks[:, None]).astype(jnp.int32), axis=1)
    owner = lookup(targets, owner_seq)
    slot_index = (flat_blocks - lookup(range_starts, owner)) // peers
    slot_ids = jnp.arange(peers * slots, dtype=jnp.int32)
    send_table = (slot_ids[:, None] == (owner * slots + slot_index)[None, :]).astype(jnp.bfloat16)
    mine_start = lookup(range_starts, own_index[None])[0]
    mine_size = lookup(range_sizes, own_index[None])[0]
    block_order = jnp.arange(LEN_BLK, dtype=jnp.int32)
    from_slot = (mine_start + block_order) % peers * slots + block_order // peers
    take_table = (from_slot[:, None] == slot_ids[None, :]).astype(jnp.bfloat16)
    return_table = jnp.transpose(take_table)
    home_table = jnp.transpose(send_table)
    block_seq = jnp.sum(
        (ends[None, :] <= (mine_start + block_order)[:, None]).astype(jnp.int32), axis=1
    )
    block_seq = jnp.where(block_order < mine_size, block_seq, -1)
    row_seq = jnp.repeat(block_seq, BLOCK)
    positions = jnp.arange(LEN_BLK * BLOCK, dtype=jnp.int32)
    allowed = (
        (row_seq[:, None] == row_seq[None, :])
        & (row_seq[:, None] >= 0)
        & (positions[None, :] <= positions[:, None])
    ).astype(jnp.float32)
    tile_blocks = math.gcd(LEN_BLK, max(1, 256 // BLOCK))
    live_tiles = (mine_size + tile_blocks - 1) // tile_blocks
    got_rows, got_grads = (
        lax.all_to_all(
            regroup(send_table, local_rows), "bal", split_axis=0, concat_axis=0, tiled=True
        ),
        lax.all_to_all(
            regroup(send_table, local_grads), "bal", split_axis=0, concat_axis=0, tiled=True
        ),
    )
    held_rows = regroup(take_table, got_rows)
    held_grads = regroup(take_table, got_grads)
    d_held, terms = whole_layer(
        held_rows,
        held_grads,
        allowed,
        live_tiles,
        tile_blocks * BLOCK,
        gain_in,
        w_proj,
        gain_attn,
        w_out,
    )
    came_back = lax.all_to_all(
        regroup(return_table, d_held), "bal", split_axis=0, concat_axis=0, tiled=True
    )
    d_rows = regroup(home_table, came_back)
    sums = lax.psum((terms[0], terms[1], terms[2], terms[3]), ("grp", "bal"))
    divisor = float(lax.axis_size("grp") * peers)
    return (
        d_rows[None],
        sums[0] / divisor,
        sums[1] / divisor,
        sums[2] / divisor,
        sums[3] / divisor,
    )


def solution(mesh):
    placed = (P("grp", "bal", None), P("grp", "bal", None), P("grp", None), P(), P(), P(), P())
    return jax.shard_map(
        per_device,
        mesh=mesh,
        in_specs=placed,
        out_specs=(P("grp", "bal", None), P(), P(), P(), P()),
        check_vma=False,
    )
```

profile of v0, /device:TPU:1, one launch (start us, length us, event | category | flops | bytes accessed | tf_op | source)
XLA Modules:
  0.0 637.0 jit_solution(15162623421532527161)
XLA Ops:
  7.2 42.6 %while.66 = (s32[]{:T(128)}, s32[]{:T(128)}, s32[]{:T(128)}, s32[16]{0:T(128)S(1)}, s32[16]{0:T(128)}) while((s32[]{:T(128)}, s32[]{:T(128)}, s32[]{:T(128)}, s32[16]{0:T(128)S(1)}, s32[16]{0:T(128)}) %tuple.198), condition=%wide.region_3.4_spmd.clone, body=%wide.region_2.3_spmd.sunk.clone | while | flops 8 | bytes 148 | solution.py:140
  55.1 9.3 %all-to-all-start.1 = ((bf16[16,64,512]{2,1,0:T(8,128)(2,1)}), bf16[16,64,512]{2,1,0:T(8,128)(2,1)S(1)}, u32[]{:S(2)}, u32[]{:S(2)}) async-start(bf16[16,64,512]{2,1,0:T(8,128)(2,1)} %bitcast.70), calls=%async_computation.1 | async-start | bytes 2097152 | tf_op jit(solution)/shard_map/all_to_all | solution.py:251
  70.0 11.6 %all-to-all-done.1 = bf16[16,64,512]{2,1,0:T(8,128)(2,1)S(1)} async-done(((bf16[16,64,512]{2,1,0:T(8,128)(2,1)}), bf16[16,64,512]{2,1,0:T(8,128)(2,1)S(1)}, u32[]{:S(2)}, u32[]{:S(2)}) %all-to-all-start.1) | async-done | bytes 1048608 | tf_op jit(solution)/shard_map/all_to_all | solution.py:251
  81.6 5.0 all-to-all-start
  91.9 70.2 %while.67 = (s32[]{:T(128)}, f32[4,256,512]{2,1,0:T(8,128)}, f32[4,256,1]{1,2,0:T(1,128)}, bf16[4,256,512]{2,1,0:T(8,128)(2,1)}, f32[4,256,2048]{2,1,0:T(8,128)}...) while((s32[]{:T(128)}, f32[4,256,512]{2,1,0:T(8,128)}, ...), condition=%wide.region_16.17_spmd.clone, body=%wide.region_11.16_spmd.sunk.clone | while | flops 541589760 | bytes 17060060 | solution.py:155
  93.2 9.2 %conditional.9 = (f32[1,256,512]{2,1,0:T(8,128)S(1)}, f32[1,256,1]{1,2,0:T(1,128)}, bf16[1,256,512]{2,1,0:T(8,128)(2,1)S(1)}, f32[1,256,2048]{2,1,0:T(8,128)}, bf16[1,256,2048]{2,1,0:T(8,128)(2,1)S(1)}) conditional(s32[]{:T(128)} %convert_element_type.475, () %tuple.157, (bf16[4,256,512]{2,1,0:T(8,128)(2,1)}, s32[]{:T(128)}, f32[512]{0:T(512)S(1)}, ...), branch_computations={%region_12.12_spmd, %region_13.15_spmd} | conditional | flops 541589760 | bytes 9190964 | solution.py:153
  96.0 3.1 fusion.8
  102.4 3.2 constant_dynamic-update-slice_fusion.33
  110.8 9.2 %conditional.9 = (f32[1,256,512]{2,1,0:T(8,128)S(1)}, f32[1,256,1]{1,2,0:T(1,128)}, bf16[1,256,512]{2,1,0:T(8,128)(2,1)S(1)}, f32[1,256,2048]{2,1,0:T(8,128)}, bf16[1,256,2048]{2,1,0:T(8,128)(2,1)S(1)}) conditional(s32[]{:T(128)} %convert_element_type.475, () %tuple.157, (bf16[4,256,512]{2,1,0:T(8,128)(2,1)}, s32[]{:T(128)}, f32[512]{0:T(512)S(1)}, ...), branch_computations={%region_12.12_spmd, %region_13.15_spmd} | conditional | flops 541589760 | bytes 9190964 | solution.py:153
  113.6 3.1 fusion.8
  120.0 3.1 constant_dynamic-update-slice_fusion.33
  128.4 9.2 %conditional.9 = (f32[1,256,512]{2,1,0:T(8,128)S(1)}, f32[1,256,1]{1,2,0:T(1,128)}, bf16[1,256,512]{2,1,0:T(8,128)(2,1)S(1)}, f32[1,256,2048]{2,1,0:T(8,128)}, bf16[1,256,2048]{2,1,0:T(8,128)(2,1)S(1)}) conditional(s32[]{:T(128)} %convert_element_type.475, () %tuple.157, (bf16[4,256,512]{2,1,0:T(8,128)(2,1)}, s32[]{:T(128)}, f32[512]{0:T(512)S(1)}, ...), branch_computations={%region_12.12_spmd, %region_13.15_spmd} | conditional | flops 541589760 | bytes 9190964 | solution.py:153
  131.2 3.1 fusion.8
  137.6 3.2 constant_dynamic-update-slice_fusion.33
  145.9 9.2 %conditional.9 = (f32[1,256,512]{2,1,0:T(8,128)S(1)}, f32[1,256,1]{1,2,0:T(1,128)}, bf16[1,256,512]{2,1,0:T(8,128)(2,1)S(1)}, f32[1,256,2048]{2,1,0:T(8,128)}, bf16[1,256,2048]{2,1,0:T(8,128)(2,1)S(1)}) conditional(s32[]{:T(128)} %convert_element_type.475, () %tuple.157, (bf16[4,256,512]{2,1,0:T(8,128)(2,1)}, s32[]{:T(128)}, f32[512]{0:T(512)S(1)}, ...), branch_computations={%region_12.12_spmd, %region_13.15_spmd} | conditional | flops 541589760 | bytes 9190964 | solution.py:153
  148.8 3.1 fusion.8
  155.2 3.1 constant_dynamic-update-slice_fusion.33
  162.2 3.7 fusion.113
  165.9 3.7 fusion.120
  169.6 3.7 fusion.127
  173.3 3.9 fusion.134
  177.2 3.7 fusion.141
  180.9 3.8 fusion.148
  186.4 19.1 %select_convert_fusion.8 = (bf16[1024,1024]{1,0:T(8,128)(2,1)S(1)}, bf16[1024,1024]{1,0:T(8,128)(2,1)}, bf16[1024,1024]{1,0:T(8,128)(2,1)}, bf16[1024,1024]{1,0:...) fusion(pred[1024]{0:T(1024)(128)(4,1)S(1)} %broadcast_compare_f, ...), kind=kOutput, calls=%fused_computation.122 | convolution fusion | flops 197132288 | bytes 50865152 | tf_op jit(solution)/shard_map/dot_general | solution.py:43
  237.3 35.1 %while.68 = (s32[]{:T(128)}, f32[4,256,512]{2,1,0:T(8,128)}, bf16[4,256,512]{2,1,0:T(8,128)(2,1)}, f32[4,512,512]{2,1,0:T(8,128)}, f32[4,512]{1,0:T(4,128)S(1)},...) while((s32[]{:T(128)}, f32[4,256,512]{2,1,0:T(8,128)}, ...), condition=%wide.region_25.26_spmd.clone, body=%wide.region_17.25_spmd.sunk.clone | while | flops 273415936 | bytes 9736943 | solution.py:155
  238.5 4.9 conditional.10
  247.3 4.9 conditional.10
  256.1 4.9 conditional.10
  264.8 4.9 conditional.10
  282.7 5.2 select_convert_fusion.1
  288.0 4.9 select_convert_fusion.2
  292.9 4.8 select_convert_fusion.3
  297.7 4.9 select_convert_fusion.4
  302.6 4.8 select_convert_fusion.5
  307.4 4.9 select_convert_fusion.6
  312.3 4.8 select_convert_fusion.7
  317.2 4.9 select_convert_fusion
  329.9 2.4 fusion.76
  338.4 2.4 fusion.74
  347.5 2.5 fusion.72
  372.0 5.6 pad_maximum_fusion
  377.8 67.9 %while.69 = (s32[]{:T(128)}, bf16[4,256,512]{2,1,0:T(8,128)(2,1)S(1)}, f32[4,512,2048]{2,1,0:T(8,128)}, f32[4,512]{1,0:T(4,128)S(1)}, s32[4]{0:T(128)S(1)}, /*in...) while((s32[]{:T(128)}, ...), condition=%wide.region_32.33_spmd.clone, body=%wide.region_26.32_spmd.sunk.clone | while | flops 1085013504 | bytes 26500880 | solution.py:155
  379.3 10.9 %conditional.11 = (bf16[1,256,512]{2,1,0:T(8,128)(2,1)S(1)}, f32[1,512,2048]{2,1,0:T(8,128)}, f32[1,512]{1,0:T(1,128)S(1)}) conditional(s32[]{:T(128)} %convert_element_type.477, () %tuple.167, (bf16[4,256,512]{2,1,0:T(8,128)(2,1)}, s32[]{:T(128)}, f32[4,256,1]{1,2,0:T(1,128)}, f32[4,256,2048]{2,1,0:T(8,128)}, f32[4,256,2048]{2,1,0:T(8,128)}, ...), branch_computations={%region_27.27_spmd, %region_28.31_spmd} | conditional | flops 1085013504 | bytes 17583136 | solution.py:153
  379.3 3.4 fusion.62
  384.7 5.5 convolution_bitcast_fusion.1
  390.2 4.6 constant_dynamic-update-slice_fusion.39
  396.1 10.9 %conditional.11 = (bf16[1,256,512]{2,1,0:T(8,128)(2,1)S(1)}, f32[1,512,2048]{2,1,0:T(8,128)}, f32[1,512]{1,0:T(1,128)S(1)}) conditional(s32[]{:T(128)} %convert_element_type.477, () %tuple.167, (bf16[4,256,512]{2,1,0:T(8,128)(2,1)}, s32[]{:T(128)}, f32[4,256,1]{1,2,0:T(1,128)}, f32[4,256,2048]{2,1,0:T(8,128)}, f32[4,256,2048]{2,1,0:T(8,128)}, ...), branch_computations={%region_27.27_spmd, %region_28.31_spmd} | conditional | flops 1085013504 | bytes 17583136 | solution.py:153
  396.2 3.4 fusion.62
  401.6 5.5 convolution_bitcast_fusion.1
  407.1 4.7 constant_dynamic-update-slice_fusion.39
  413.1 11.0 %conditional.11 = (bf16[1,256,512]{2,1,0:T(8,128)(2,1)S(1)}, f32[1,512,2048]{2,1,0:T(8,128)}, f32[1,512]{1,0:T(1,128)S(1)}) conditional(s32[]{:T(128)} %convert_element_type.477, () %tuple.167, (bf16[4,256,512]{2,1,0:T(8,128)(2,1)}, s32[]{:T(128)}, f32[4,256,1]{1,2,0:T(1,128)}, f32[4,256,2048]{2,1,0:T(8,128)}, f32[4,256,2048]{2,1,0:T(8,128)}, ...), branch_computations={%region_27.27_spmd, %region_28.31_spmd} | conditional | flops 1085013504 | bytes 17583136 | solution.py:153
  413.1 3.4 fusion.62
  418.5 5.5 convolution_bitcast_fusion.1
  424.0 4.7 constant_dynamic-update-slice_fusion.39
  430.0 11.0 %conditional.11 = (bf16[1,256,512]{2,1,0:T(8,128)(2,1)S(1)}, f32[1,512,2048]{2,1,0:T(8,128)}, f32[1,512]{1,0:T(1,128)S(1)}) conditional(s32[]{:T(128)} %convert_element_type.477, () %tuple.167, (bf16[4,256,512]{2,1,0:T(8,128)(2,1)}, s32[]{:T(128)}, f32[4,256,1]{1,2,0:T(1,128)}, f32[4,256,2048]{2,1,0:T(8,128)}, f32[4,256,2048]{2,1,0:T(8,128)}, ...), branch_computations={%region_27.27_spmd, %region_28.31_spmd} | conditional | flops 1085013504 | bytes 17583136 | solution.py:153
  430.0 3.4 fusion.62
  435.5 5.5 convolution_bitcast_fusion.1
  441.0 4.6 constant_dynamic-update-slice_fusion.39
  445.7 10.1 %reduce_sum.224 = f32[512,2048]{1,0:T(8,128)} reduce(f32[4,512,2048]{2,1,0:T(8,128)} %get-tuple-element.445, f32[]{:T(128)} %constant.270.clone.1), dimensions={0}, to_apply=%region_33.34 | reduce | flops 3145728 | bytes 20971524 | tf_op jit(solution)/shard_map/reduce_sum | solution.py:202
  455.8 3.8 reduce_sum.225
  462.0 4.9 all-to-all-start.2
  466.9 74.6 %all-reduce = (f32[512]{0:T(512)S(1)}, f32[512]{0:T(512)S(1)}) all-reduce(f32[512]{0:T(512)S(1)} %reduce_sum.226, f32[512]{0:T(512)S(1)} %reduce_sum.227), channel_id=1, replica_groups=mesh['grp'=8,'bal'=16] {'grp','bal'}, use_global_device_ids=true, to_apply=%region_38.39 | all-reduce | flops 1024 | bytes 8192 | tf_op jit(solution)/shard_map/psum | solution.py:275
  544.6 79.3 %all-reduce.4.cloned.1.call-done = (f32[512,2048]{1,0:T(8,128)}, f32[512,512]{1,0:T(8,128)}) async-done(((f32[512,2048]{1,0:T(8,128)}, f32[512,512]{1,0:T(8,128)}), (f32[512,2048]{1,0:T(8,128)}, f32[512,512]{1,0:T(8,128)})) %all-reduce.4.cloned.1.call-update) | async-done | bytes 5242896 | tf_op jit(solution)/shard_map/psum | solution.py:275
  623.9 4.9 broadcast_multiply_fusion.6
  (372 shorter events, 214.9 us)
Async XLA Ops:
  7.2 60.8 %copy-start.36 = (bf16[1,512,512]{2,1,0:T(8,128)(2,1)S(1)}, bf16[1,512,512]{2,1,0:T(8,128)(2,1)}, u32[]{:S(2)}) copy-start(bf16[1,512,512]{2,1,0:T(8,128)(2,1)} %param.22) | copy-start | bytes 1572868
  52.0 16.6 %copy-start.40 = (s32[8]{0:T(128)}, s32[8]{0:T(128)S(1)}, u32[]{:S(2)}) copy-start(s32[8]{0:T(128)S(1)} %fusion.169) | copy-start | bytes 100
  55.1 26.5 %all-to-all-start.1 = ((bf16[16,64,512]{2,1,0:T(8,128)(2,1)}), bf16[16,64,512]{2,1,0:T(8,128)(2,1)S(1)}, u32[]{:S(2)}, u32[]{:S(2)}) async-start(bf16[16,64,512]{2,1,0:T(8,128)(2,1)} %bitcast.70), calls=%async_computation.1 | async-start | bytes 2097152 | tf_op jit(solution)/shard_map/all_to_all | solution.py:251
  67.0 163.3 %copy-start.42 = (s32[16]{0:T(128)}, s32[16]{0:T(128)S(1)}, u32[]{:S(2)}) copy-start(s32[16]{0:T(128)S(1)} %get-tuple-element.578) | copy-start | bytes 196
  81.6 147.0 %all-to-all-start = ((bf16[16,64,512]{2,1,0:T(8,128)(2,1)}), bf16[16,64,512]{2,1,0:T(8,128)(2,1)}, u32[]{:S(2)}, u32[]{:S(2)}) async-start(bf16[16,64,512]{2,1,0:T(8,128)(2,1)} %bitcast.66), calls=%async_computation | async-start | bytes 2097152 | tf_op jit(solution)/shard_map/all_to_all | solution.py:254
  86.6 537.4 %all-reduce.4.cloned.1.call-start = ((), (), s32[]{:S(2)}) async-start(), calls=%async_computation.3 | async-start | bytes 10485760 | tf_op jit(solution)/shard_map/psum | solution.py:275
  87.2 4.8 copy-start
  87.2 4.8 copy-start.30
  186.4 19.1 %copy-start.15 = (f32[1024,1024]{1,0:T(8,128)}, f32[1024,1024]{1,0:T(8,128)S(1)}, u32[]{:S(2)}) copy-start(f32[1024,1024]{1,0:T(8,128)S(1)} %fusion.155) | copy-start | bytes 12582916
  205.5 7.7 %copy-start.8 = (bf16[1024,1024]{1,0:T(8,128)(2,1)}, bf16[1024,1024]{1,0:T(8,128)(2,1)S(1)}, u32[]{:S(2)}) copy-start(bf16[1024,1024]{1,0:T(8,128)(2,1)S(1)} %get-tuple-element.573) | copy-start | bytes 6291460
  205.5 7.7 %copy-start.10 = (bf16[1024,1024]{1,0:T(8,128)(2,1)}, bf16[1024,1024]{1,0:T(8,128)(2,1)S(1)}, u32[]{:S(2)}) copy-start(bf16[1024,1024]{1,0:T(8,128)(2,1)S(1)} %get-tuple-element.574) | copy-start | bytes 6291460
  205.5 7.7 %copy-start.6 = (bf16[1024,1024]{1,0:T(8,128)(2,1)}, bf16[1024,1024]{1,0:T(8,128)(2,1)S(1)}, u32[]{:S(2)}) copy-start(bf16[1024,1024]{1,0:T(8,128)(2,1)S(1)} %get-tuple-element.572) | copy-start | bytes 6291460
  205.5 9.4 %copy-start.12 = (bf16[1024,1024]{1,0:T(8,128)(2,1)}, bf16[1024,1024]{1,0:T(8,128)(2,1)S(1)}, u32[]{:S(2)}) copy-start(bf16[1024,1024]{1,0:T(8,128)(2,1)S(1)} %get-tuple-element.575) | copy-start | bytes 6291460
  205.5 9.4 %copy-start.13 = (bf16[1024,1024]{1,0:T(8,128)(2,1)}, bf16[1024,1024]{1,0:T(8,128)(2,1)S(1)}, u32[]{:S(2)}) copy-start(bf16[1024,1024]{1,0:T(8,128)(2,1)S(1)} %get-tuple-element.569) | copy-start | bytes 6291460
  205.5 20.4 %copy-start.2 = (bf16[1024,1024]{1,0:T(8,128)(2,1)}, bf16[1024,1024]{1,0:T(8,128)(2,1)S(1)}, u32[]{:S(2)}) copy-start(bf16[1024,1024]{1,0:T(8,128)(2,1)S(1)} %get-tuple-element.576) | copy-start | bytes 6291460
  227.7 4.5 copy-start.23
  227.7 4.5 copy-start.24
  230.8 6.4 %copy-start.37 = (f32[512]{0:T(512)S(1)}, f32[512]{0:T(512)}, u32[]{:S(2)}) copy-start(f32[512]{0:T(512)} %param.26) | copy-start | bytes 6148
  272.4 5.3 copy-start.38
  272.4 2.4 copy-start.14
  272.4 4.6 copy-start.11
  274.7 2.9 copy-start.9
  277.0 1.6 copy-start.7
  277.7 1.8 copy-start.5
  278.6 1.7 copy-start.4
  279.4 1.7 copy-start.3
  280.4 2.3 copy-start.22
  282.7 5.2 copy-start.21
  288.0 4.9 copy-start.20
  292.9 4.8 copy-start.19
  297.7 4.9 copy-start.18
  302.6 4.8 copy-start.17
  307.4 4.9 copy-start.16
  312.3 4.8 copy-start.44
  359.1 4.9 copy-start.32
  359.1 5.1 copy-start.33
  359.1 5.2 copy-start.34
  359.1 5.4 copy-start.35
  366.7 2.2 copy-start.26
  366.7 2.4 copy-start.27
  366.8 2.6 copy-start.28
  366.8 2.8 copy-start.29
  372.0 5.8 copy-start.1
  372.0 5.8 copy-start.31
  459.6 0.6 copy-start.43
  459.6 7.3 %copy-start.39 = (f32[4,512]{1,0:T(4,128)S(1)}, f32[4,512]{1,0:T(4,128)}, u32[]{:S(2)}) copy-start(f32[4,512]{1,0:T(4,128)} %copy-done.38) | copy-start | bytes 24580
  460.2 83.1 %copy-start.41 = (s32[8]{0:T(128)S(1)}, s32[8]{0:T(128)}, u32[]{:S(2)}) copy-start(s32[8]{0:T(128)} %copy-done.40) | copy-start | bytes 100
  462.0 80.6 %all-to-all-start.2 = ((bf16[16,64,512]{2,1,0:T(8,128)(2,1)}), bf16[16,64,512]{2,1,0:T(8,128)(2,1)S(1)}, u32[]{:S(2)}, u32[]{:S(2)}) async-start(bf16[16,64,512]{2,1,0:T(8,128)(2,1)} %bitcast.74), calls=%async_computation.2 | async-start | bytes 2097152 | tf_op jit(solution)/shard_map/all_to_all | solution.py:271
  623.9 4.9 copy-start.25
Sparse Core Ops, SparseCore 0:
  459.7 164.1 all-reduce.3
where the time goes:
time: 644 us; the launch traced here: 637 us
  matrix products  205 us (32%)
  local copies, waits for them, and re-layouts  132 us (20%)
  waiting for transfers between devices  90.9 us (14%)
  blocking collectives  74.6 us (12%)
  other arithmetic  70.4 us (11%)
  loops' own time  29.7 us (5%)
  starting transfers between devices  19.2 us (3%)
  between operations  16 us (2%)
    dot_general x24, matrix products, contract_cols(): lax.dot_general(left, right, (((1,), (1,)), ((), ())), preferred_element_...  103 us
    psum x1, waiting for transfers between devices, per_device(): sums = lax.psum((terms[0], terms[1], terms[2], terms[3]), ('grp', 'bal'))  79.3 us
    psum x1, blocking collectives, per_device(): sums = lax.psum((terms[0], terms[1], terms[2], terms[3]), ('grp', 'bal'))  74.6 us
    dynamic_update_slice x48, local copies, waits for them, and re-layouts, held_tiles_map(): return lax.map(each_tile, (jnp.arange(count, dtype=jnp.int32), pieces))  57.7 us
    dot_general x24, matrix products, contract_rows(): lax.dot_general(left, right, (((0,), (0,)), ((), ())), preferred_element_...  51.2 us
    another operation x1, loops' own time, pack_histories(): final_state, ranks = lax.scan(advance, start_state, seq_lengths)  20.9 us
    dynamic_slice x16, local copies, waits for them, and re-layouts, pack_histories(): final_state, ranks = lax.scan(advance, start_state, seq_lengths)  19.9 us
    dot_general x8, matrix products, attend_backward(): jnp.dot(grad_scores, key_head, preferred_element_type=jnp.float32) * scale  19.2 us
  transfers between devices with their start and end apart: 4, of which 2 were waited for; matrix products, arithmetic and copies ran while one was open for 23% of the time, Pallas kernels for 0%

commit v1 on v0

v1 whole, which is shorter than its diff:
```python
import jax
import jax.numpy as jnp
from jax import lax
from jax.experimental import pallas as pl
from jax.experimental.pallas import tpu as pltpu
from jax.sharding import Mesh, PartitionSpec as P

D = 512
HEADS = 8
BLOCK = 64
LEN_BLK = 16
SEQ = 16
PEERS = 16
LOCAL = 8
TILE = 256
TILES = 4
ROWS = 1024
LANES = 128
PAIRS = 4
PART = 88
HALF = 64 * PART
EPS = 1e-06
DEVICES = 128
BF = jnp.bfloat16
F32 = jnp.float32
VMEM_LIMIT = 56 * 1024 * 1024

SMEM_SPEC = pl.BlockSpec(memory_space=pltpu.SMEM)
ANY_SPEC = pl.BlockSpec(memory_space=pl.ANY)
VMEM_SPEC = pl.BlockSpec(memory_space=pltpu.VMEM)


def dot(left, right):
    return lax.dot_general(left, right, (((1,), (0,)), ((), ())), preferred_element_type=F32)


def dot_cols(left, right):
    return lax.dot_general(left, right, (((1,), (1,)), ((), ())), preferred_element_type=F32)


def dot_rows(left, right):
    return lax.dot_general(left, right, (((0,), (0,)), ((), ())), preferred_element_type=F32)


def packing(len_ref):
    starts, sizes, ranks = [], [], []
    start = jnp.int32(0)
    rank = jnp.int32(0)
    held = jnp.int32(0)
    for i in range(SEQ):
        size = len_ref[i]
        fresh = held + size > LEN_BLK
        rank = jnp.where(fresh, rank + 1, rank)
        held = jnp.where(fresh, size, held + size)
        starts.append(start)
        sizes.append(size)
        ranks.append(rank)
        start = start + size
    return starts, sizes, ranks


def owners(len_ref, own):
    starts, _, ranks = packing(len_ref)
    found = []
    for k in range(LOCAL):
        block = own + PEERS * k
        owner = ranks[0]
        for i in range(1, SEQ):
            owner = jnp.where(starts[i] <= block, ranks[i], owner)
        found.append(owner)
    return found


def holdings(len_ref, own):
    starts, sizes, ranks = packing(len_ref)
    first = jnp.int32(LEN_BLK * LOCAL)
    count = jnp.int32(0)
    for i in range(SEQ):
        mine = ranks[i] == own
        first = jnp.where(mine, jnp.minimum(first, starts[i]), first)
        count = jnp.where(mine, count + sizes[i], count)
    return starts, sizes, ranks, first, count


def history_starts(hist_ref, own, starts, sizes, ranks, first):
    for j in range(LEN_BLK):
        hist_ref[j] = j
    for i in range(SEQ):

        @pl.when(ranks[i] == own)
        def _(i=i):
            begin = starts[i] - first

            def put(j, carry):
                hist_ref[j] = begin
                return carry

            lax.fori_loop(begin, begin + sizes[i], put, 0)


def send_kernel(len_ref, own_ref, rows_ref, grads_ref, rows_out, grads_out, sems):
    owner = owners(len_ref, own_ref[0])
    copies = []
    for n, (src, dst) in enumerate(((rows_ref, rows_out), (grads_ref, grads_out))):
        for k in range(LOCAL):
            copies.append(pltpu.make_async_copy(src.at[k], dst.at[owner[k]], sems.at[n, k]))
    for copy in copies:
        copy.start()
    for copy in copies:
        copy.wait()


def home_kernel(len_ref, own_ref, back_ref, out_ref, sems):
    owner = owners(len_ref, own_ref[0])
    copies = [
        pltpu.make_async_copy(back_ref.at[owner[k]], out_ref.at[k], sems.at[k])
        for k in range(LOCAL)
    ]
    for copy in copies:
        copy.start()
    for copy in copies:
        copy.wait()


def fetch(src_ref, dst_ref, sems, first, count):
    for j in range(LEN_BLK):

        @pl.when(j < count)
        def _(j=j):
            slot = (first + j) & (PEERS - 1)
            pltpu.make_async_copy(src_ref.at[slot], dst_ref.at[j], sems.at[j]).start()


def arrive(src_ref, dst_ref, sems, count):
    for j in range(LEN_BLK):

        @pl.when(j < count)
        def _(j=j):
            pltpu.make_async_copy(src_ref.at[0], dst_ref.at[j], sems.at[j]).wait()


def tile_rows(ref, t, count):
    tile = ref[pl.ds(t * 4, 4)].reshape(TILE, D).astype(F32)
    place = lax.broadcasted_iota(jnp.int32, (TILE, D), 0) + t * TILE
    return jnp.where(place < count * BLOCK, tile, 0.0)


def normed_rows(values):
    centred = values - jnp.mean(values, axis=-1, keepdims=True)
    rstd = lax.rsqrt(jnp.mean(centred * centred, axis=-1, keepdims=True) + EPS)
    return centred * rstd, rstd


def head_masks():
    lane = lax.broadcasted_iota(jnp.int32, (1, LANES), 1)
    low = (lane < 64).astype(F32).astype(BF)
    high = (lane >= 64).astype(F32).astype(BF)
    return low, high


def rows_at(t):
    return pl.ds(pl.multiple_of(t * TILE, TILE), TILE)


def block_starts(hist_ref, t, shape, dim):
    place = lax.broadcasted_iota(jnp.int32, shape, dim)
    begin = jnp.full(shape, hist_ref[4 * t], jnp.int32)
    for b in range(1, 4):
        begin = jnp.where(place >= b * BLOCK, hist_ref[4 * t + b], begin)
    return begin * BLOCK


def key_tiles(hist_ref, i):
    low = hist_ref[4 * i] // 4
    clear = jnp.minimum((hist_ref[4 * i + 3] + 3) // 4, i)
    return low, jnp.maximum(clear, low)


def forward_kernel(
    len_ref,
    own_ref,
    got_ref,
    w_ref,
    gain_ref,
    upper_ref,
    values_ref,
    query_ref,
    keys_ref,
    slope_ref,
    attn_ref,
    scaled_ref,
    rows_ref,
    acc_ref,
    hist_ref,
    sems,
):
    own = own_ref[0]
    starts, sizes, ranks, first, count = holdings(len_ref, own)
    fetch(got_ref, rows_ref, sems, first, count)
    history_starts(hist_ref, own, starts, sizes, ranks, first)
    live = (count + 3) // 4
    arrive(got_ref, rows_ref, sems, count)

    def project(t, carry):
        normed, _ = normed_rows(tile_rows(rows_ref, t, count))
        scaled = (normed * gain_ref[...]).astype(BF)
        rows = rows_at(t)
        scaled_ref[rows, :] = scaled
        for quarter in range(4):
            half = 0.5 * dot(scaled, w_ref[:, quarter * D : (quarter + 1) * D])
            swing = jnp.tanh(half)
            active = half + half * swing
            slope = ((0.5 + 0.5 * swing) * (1.0 + (half - half * swing))).astype(BF)
            if quarter == 0:
                upper_ref[rows, :] = active.astype(BF)
            if quarter == 2:
                active = active * 0.0625
            active = active.astype(BF)
            for p in range(PAIRS):
                lanes = slice(p * LANES, (p + 1) * LANES)
                slope_ref[quarter * PAIRS + p, rows, :] = slope[:, lanes]
                if quarter:
                    ref = (None, values_ref, query_ref, keys_ref)[quarter]
                    ref[p, rows, :] = active[:, lanes]
        return carry

    lax.fori_loop(0, live, project, 0)

    def clear(t, carry):
        scaled_ref[rows_at(t), :] = jnp.zeros((TILE, D), BF)
        return carry

    lax.fori_loop(live, TILES, clear, 0)

    masks = head_masks()

    def pair(p, carry):
        def query_tile(i, carry):
            query = query_ref[p, rows_at(i), :]
            acc_ref[...] = jnp.zeros((TILE, LANES), F32)

            def step(j, masked):
                keys = keys_ref[p, rows_at(j), :]
                values = values_ref[p, rows_at(j), :]
                if masked:
                    shape = (TILE, TILE)
                    col = lax.broadcasted_iota(jnp.int32, shape, 1) + j * TILE
                    row = lax.broadcasted_iota(jnp.int32, shape, 0) + i * TILE
                    allowed = (col <= row) & (col >= block_starts(hist_ref, i, shape, 0))
                total = acc_ref[...]
                for mask in masks:
                    half = dot_cols(query, keys * mask)
                    weights = half + half * jnp.tanh(half)
                    if masked:
                        weights = jnp.where(allowed, weights, 0.0)
                    total += dot(weights.astype(BF), values * mask)
                acc_ref[...] = total

            low, clear_from = key_tiles(hist_ref, i)

            def masked_step(j, carry):
                step(j, True)
                return carry

            def clear_step(j, carry):
                step(j, False)
                return carry

            lax.fori_loop(low, clear_from, masked_step, 0)
            lax.fori_loop(clear_from, i, clear_step, 0)
            step(i, True)
            attn_ref[p, rows_at(i), :] = acc_ref[...].astype(BF)
            return carry

        return lax.fori_loop(0, live, query_tile, carry)

    lax.fori_loop(0, PAIRS, pair, 0)


def backward_kernel(
    len_ref,
    own_ref,
    got_ref,
    grads_ref,
    upper_ref,
    values_ref,
    query_ref,
    keys_ref,
    slope_ref,
    attn_ref,
    scaled_ref,
    w_ref,
    w_out_ref,
    gain_in_ref,
    gain_attn_ref,
    back_ref,
    terms_ref,
    rows_ref,
    cot_ref,
    d_attn_ref,
    d_hidden_ref,
    out_ref,
    gains_ref,
    d_query_ref,
    d_keys_ref,
    d_values_ref,
    hist_ref,
    row_sems,
    cot_sems,
):
    own = own_ref[0]
    core = own & 1
    starts, sizes, ranks, first, count = holdings(len_ref, own)
    fetch(grads_ref, cot_ref, cot_sems, first, count)
    fetch(got_ref, rows_ref, row_sems, first, count)
    history_starts(hist_ref, own, starts, sizes, ranks, first)
    live = (count + 3) // 4
    out_ref[...] = jnp.zeros((D, D), F32)
    gains_ref[...] = jnp.zeros((2, D), F32)
    arrive(grads_ref, cot_ref, cot_sems, count)

    def middle(t, carry):
        rows = rows_at(t)
        attn = jnp.concatenate([attn_ref[p, rows, :] for p in range(PAIRS)], axis=1)
        normed, rstd = normed_rows(attn.astype(F32))
        upper = upper_ref[rows, :].astype(F32)
        cot = tile_rows(cot_ref, t, count).astype(BF)
        d_mixed = dot_cols(cot, w_out_ref[...])
        gained = normed * gain_attn_ref[...]
        out_ref[...] += dot_rows((gained * upper).astype(BF), cot)
        d_upper = d_mixed * gained
        pull = d_mixed * upper
        gains_ref[1:2, :] += jnp.sum(pull * normed, axis=0, keepdims=True)
        pull = pull * gain_attn_ref[...]
        d_attn = rstd * (
            pull
            - jnp.mean(pull, axis=-1, keepdims=True)
            - normed * jnp.mean(pull * normed, axis=-1, keepdims=True)
        )
        for p in range(PAIRS):
            lanes = slice(p * LANES, (p + 1) * LANES)
            d_attn_ref[p, rows, :] = d_attn[:, lanes].astype(BF)
            slope = slope_ref[p, rows, :].astype(F32)
            d_hidden_ref[p, rows, :] = (d_upper[:, lanes] * slope).astype(BF)
        return carry

    lax.fori_loop(0, live, middle, 0)

    def clear(t, carry):
        d_hidden_ref[:, rows_at(t), :] = jnp.zeros((4 * PAIRS, TILE, LANES), BF)
        return carry

    lax.fori_loop(live, TILES, clear, 0)

    masks = head_masks()

    def pair(p, carry):
        d_keys_ref[...] = jnp.zeros((ROWS, LANES), F32)
        d_values_ref[...] = jnp.zeros((ROWS, LANES), F32)

        def query_tile(i, carry):
            query = query_ref[p, rows_at(i), :]
            d_attn = d_attn_ref[p, rows_at(i), :]
            d_query_ref[...] = jnp.zeros((TILE, LANES), F32)

            def step(j, masked):
                rows = rows_at(j)
                keys = keys_ref[p, rows, :]
                values = values_ref[p, rows, :]
                if masked:
                    shape = (TILE, TILE)
                    key_row = lax.broadcasted_iota(jnp.int32, shape, 0) + j * TILE
                    query_row = lax.broadcasted_iota(jnp.int32, shape, 1) + i * TILE
                    allowed = (key_row <= query_row) & (
                        key_row >= block_starts(hist_ref, i, shape, 1)
                    )
                d_query = d_query_ref[...]
                d_keys = d_keys_ref[rows, :]
                d_values = d_values_ref[rows, :]
                for mask in masks:
                    masked_keys = keys * mask
                    half = dot_cols(masked_keys, query)
                    swing = jnp.tanh(half)
                    bend = half * swing
                    weights = half + bend
                    slope = (1.0 + swing) * ((1.0 + half) - bend)
                    grad = dot_cols(values * mask, d_attn) * slope
                    if masked:
                        weights = jnp.where(allowed, weights, 0.0)
                        grad = jnp.where(allowed, grad, 0.0)
                    grad = grad.astype(BF)
                    d_values += dot(weights.astype(BF), d_attn * mask)
                    d_keys += dot(grad, query * mask)
                    d_query += dot_rows(grad, masked_keys)
                d_query_ref[...] = d_query
                d_keys_ref[rows, :] = d_keys
                d_values_ref[rows, :] = d_values

            low, clear_from = key_tiles(hist_ref, i)

            def masked_step(j, carry):
                step(j, True)
                return carry

            def clear_step(j, carry):
                step(j, False)
                return carry

            lax.fori_loop(low, clear_from, masked_step, 0)
            lax.fori_loop(clear_from, i, clear_step, 0)
            step(i, True)
            slope = slope_ref[2 * PAIRS + p, rows_at(i), :].astype(F32)
            d_hidden_ref[2 * PAIRS + p, rows_at(i), :] = (
                d_query_ref[...] * 0.0625 * slope
            ).astype(BF)
            return carry

        lax.fori_loop(0, live, query_tile, 0)

        def finish(t, carry):
            rows = rows_at(t)
            for place, ref in ((1, d_values_ref), (3, d_keys_ref)):
                slope = slope_ref[place * PAIRS + p, rows, :].astype(F32)
                d_hidden_ref[place * PAIRS + p, rows, :] = (ref[rows, :] * slope).astype(BF)
            return carry

        lax.fori_loop(0, live, finish, 0)
        return carry

    lax.fori_loop(0, PAIRS, pair, 0)

    arrive(got_ref, rows_ref, row_sems, count)

    def final(t, carry):
        rows = rows_at(t)
        normed, rstd = normed_rows(tile_rows(rows_ref, t, count))
        d_scaled = jnp.zeros((TILE, D), F32)
        for c in range(8):
            part = jnp.concatenate(
                [d_hidden_ref[2 * c, rows, :], d_hidden_ref[2 * c + 1, rows, :]], axis=1
            )
            d_scaled += dot_cols(part, w_ref[:, c * 256 : (c + 1) * 256])
        gains_ref[0:1, :] += jnp.sum(d_scaled * normed, axis=0, keepdims=True)
        pull = d_scaled * gain_in_ref[...]
        d_rows = rstd * (
            pull
            - jnp.mean(pull, axis=-1, keepdims=True)
            - normed * jnp.mean(pull * normed, axis=-1, keepdims=True)
        )
        d_rows = (d_rows + tile_rows(cot_ref, t, count)).astype(BF)
        for b in range(4):
            slot = (first + t * 4 + b) & (PEERS - 1)
            back_ref[slot] = d_rows[b * BLOCK : (b + 1) * BLOCK, :]
        return carry

    lax.fori_loop(0, live, final, 0)

    def put(piece, values):
        half, place = divmod(piece, 10)
        terms_ref[half ^ core, place * D : (place + 1) * D, :] = values.astype(BF)

    for c in range(8):
        part = jnp.concatenate([d_hidden_ref[2 * c], d_hidden_ref[2 * c + 1]], axis=1)
        term = dot_rows(scaled_ref[...], part)
        put(2 * c, term[:, :LANES])
        put(2 * c + 1, term[:, LANES:])
    for p in range(PAIRS):
        put(16 + p, out_ref[:, p * LANES : (p + 1) * LANES])
    for half in range(2):
        terms_ref[half ^ core, 10 * D :, :] = jnp.concatenate(
            [gains_ref[half : half + 1, p * LANES : (p + 1) * LANES] for p in range(PAIRS)]
            + [jnp.zeros((HALF - 10 * D - PAIRS, LANES), F32)],
            axis=0,
        ).astype(BF)


def spread_kernel(own_ref, mine_ref, other_ref, proj_ref, out_ref, gain_in_ref, gain_attn_ref):
    core = own_ref[0] & 1

    def write(low_ref, high_ref):
        for piece in range(20):
            half, place = divmod(piece, 10)
            part = (low_ref, high_ref)[half][place * D : (place + 1) * D, :].astype(F32)
            if piece < 16:
                proj_ref[:, piece * LANES : (piece + 1) * LANES] = part
            else:
                out_ref[:, (piece - 16) * LANES : (piece - 15) * LANES] = part
        gain_in_ref[...] = low_ref[10 * D : 10 * D + 16, :].astype(F32)[:PAIRS]
        gain_attn_ref[...] = high_ref[10 * D : 10 * D + 16, :].astype(F32)[:PAIRS]

    @pl.when(core == 0)
    def _():
        write(mine_ref, other_ref)

    @pl.when(core == 1)
    def _():
        write(other_ref, mine_ref)


def struct(shape, dtype):
    return jax.ShapeDtypeStruct(shape, dtype)


def params():
    return pltpu.CompilerParams(vmem_limit_bytes=VMEM_LIMIT)


def per_device(events, cotangent, lengths, gain_in, w_proj, gain_attn, w_out):
    own = lax.axis_index(("chip", "core")).astype(jnp.int32).reshape(1)
    lens = lengths[0]
    blocks = struct((PEERS, BLOCK, D), BF)
    send_rows, send_grads = pl.pallas_call(
        send_kernel,
        out_shape=(blocks, blocks),
        in_specs=[SMEM_SPEC, SMEM_SPEC, ANY_SPEC, ANY_SPEC],
        out_specs=(ANY_SPEC, ANY_SPEC),
        scratch_shapes=[pltpu.SemaphoreType.DMA((2, LOCAL))],
        name="send_blocks",
    )(lens, own, events.reshape(LOCAL, BLOCK, D), cotangent.reshape(LOCAL, BLOCK, D))
    got_rows = lax.all_to_all(send_rows, ("chip", "core"), 0, 0, tiled=True)
    got_grads = lax.all_to_all(send_grads, ("chip", "core"), 0, 0, tiled=True)
    pairs = struct((PAIRS, ROWS, LANES), BF)
    wide = struct((ROWS, D), BF)
    saved = pl.pallas_call(
        forward_kernel,
        out_shape=(
            wide,
            pairs,
            pairs,
            pairs,
            struct((4 * PAIRS, ROWS, LANES), BF),
            pairs,
            wide,
        ),
        in_specs=[SMEM_SPEC, SMEM_SPEC, ANY_SPEC, VMEM_SPEC, VMEM_SPEC],
        out_specs=(VMEM_SPEC,) * 7,
        scratch_shapes=[
            pltpu.VMEM((LEN_BLK, BLOCK, D), BF),
            pltpu.VMEM((TILE, LANES), F32),
            pltpu.SMEM((LEN_BLK,), jnp.int32),
            pltpu.SemaphoreType.DMA((LEN_BLK,)),
        ],
        compiler_params=params(),
        name="forward_layer",
    )(lens, own, got_rows, w_proj, gain_in.reshape(1, D))
    send_back, terms = pl.pallas_call(
        backward_kernel,
        out_shape=(blocks, struct((2, HALF, LANES), BF)),
        in_specs=[SMEM_SPEC, SMEM_SPEC, ANY_SPEC, ANY_SPEC] + [VMEM_SPEC] * 11,
        out_specs=(VMEM_SPEC, VMEM_SPEC),
        scratch_shapes=[
            pltpu.VMEM((LEN_BLK, BLOCK, D), BF),
            pltpu.VMEM((LEN_BLK, BLOCK, D), BF),
            pltpu.VMEM((PAIRS, ROWS, LANES), BF),
            pltpu.VMEM((4 * PAIRS, ROWS, LANES), BF),
            pltpu.VMEM((D, D), F32),
            pltpu.VMEM((2, D), F32),
            pltpu.VMEM((TILE, LANES), F32),
            pltpu.VMEM((ROWS, LANES), F32),
            pltpu.VMEM((ROWS, LANES), F32),
            pltpu.SMEM((LEN_BLK,), jnp.int32),
            pltpu.SemaphoreType.DMA((LEN_BLK,)),
            pltpu.SemaphoreType.DMA((LEN_BLK,)),
        ],
        compiler_params=params(),
        name="backward_layer",
    )(
        lens,
        own,
        got_rows,
        got_grads,
        *saved,
        w_proj,
        w_out,
        gain_in.reshape(1, D),
        gain_attn.reshape(1, D),
    )
    swap = [(0, 1), (1, 0)]
    other = lax.ppermute(terms[1], "core", swap)
    chip_sum = (terms[0].astype(F32) + other.astype(F32)).astype(BF)
    parts = lax.all_to_all(chip_sum.reshape(64, PART, LANES), ("grp", "chip"), 0, 0, tiled=True)
    total = (jnp.sum(parts.astype(F32), axis=0) * (1.0 / DEVICES)).astype(BF)
    copies = jnp.broadcast_to(total[None], (64, PART, LANES))
    mine = lax.all_to_all(copies, ("grp", "chip"), 0, 0, tiled=True).reshape(HALF, LANES)
    others = lax.ppermute(mine, "core", swap)
    came_back = lax.all_to_all(send_back, ("chip", "core"), 0, 0, tiled=True)
    d_rows = pl.pallas_call(
        home_kernel,
        out_shape=struct((LOCAL, BLOCK, D), BF),
        in_specs=[SMEM_SPEC, SMEM_SPEC, ANY_SPEC],
        out_specs=ANY_SPEC,
        scratch_shapes=[pltpu.SemaphoreType.DMA((LOCAL,))],
        name="take_home",
    )(lens, own, came_back)
    gain = struct((PAIRS, LANES), F32)
    grad_proj, grad_out, grad_in, grad_attn = pl.pallas_call(
        spread_kernel,
        out_shape=(struct((D, 4 * D), F32), struct((D, D), F32), gain, gain),
        in_specs=[SMEM_SPEC, VMEM_SPEC, VMEM_SPEC],
        out_specs=(VMEM_SPEC,) * 4,
        compiler_params=params(),
        name="spread_grads",
    )(own, mine, others)
    return (
        d_rows.reshape(1, LOCAL * BLOCK, D),
        grad_proj,
        grad_out,
        grad_in.reshape(D),
        grad_attn.reshape(D),
    )


def solution(mesh):
    fine = Mesh(mesh.devices.reshape(8, 8, 2), ("grp", "chip", "core"))
    rows = P("grp", ("chip", "core"), None)
    return jax.shard_map(
        per_device,
        mesh=fine,
        in_specs=(rows, rows, P("grp", None), P(), P(), P(), P()),
        out_specs=(rows, P(), P(), P(), P()),
        check_vma=False,
    )
```

time: 644 us -> 262 us (0.41)
  matrix products: 205 us -> 0 us
  Pallas kernels: 0 us -> 143 us
  local copies, waits for them, and re-layouts: 132 us -> 3.86 us
  waiting for transfers between devices: 90.9 us -> 3.21 us
  other arithmetic: 70.4 us -> 0.61 us
  loops' own time: 29.7 us -> 0 us
  blocking collectives: 74.6 us -> 101 us
  between operations: 16 us -> 0.76 us
  starting transfers between devices: 19.2 us -> 8.28 us
    dot_general x74 -> x0, matrix products: 205 us -> none  [the longest x24 103 us: contract_cols(): lax.dot_general(left, right, (((1,), (1,)), ((), ())), preferred_element_...]
    pallas_call x0 -> x5, Pallas kernels: none -> 143 us  [the longest x1 51.2 us: per_device(): pl.pallas_call(backward_kernel, out_shape=(blocks, struct((2, HALF, LANES...]
    all_to_all x0 -> x4, blocking collectives: none -> 101 us  [the longest x1 29.6 us: per_device(): lax.all_to_all(chip_sum.reshape(64, PART, LANES), ('grp', 'chip'), 0, 0,...]
    psum x1 -> x0, waiting for transfers between devices: 79.3 us -> none  [per_device(): sums = lax.psum((terms[0], terms[1], terms[2], terms[3]), ('grp', 'bal'))]
    psum x1 -> x0, blocking collectives: 74.6 us -> none  [per_device(): sums = lax.psum((terms[0], terms[1], terms[2], terms[3]), ('grp', 'bal'))]
    dynamic_update_slice x64 -> x0, local copies, waits for them, and re-layouts: 59.5 us -> none  [the longest x48 57.7 us: held_tiles_map(): return lax.map(each_tile, (jnp.arange(count, dtype=jnp.int32), pieces))]
    another operation x16 -> x0, loops' own time: 29.7 us -> none  [the longest x1 20.9 us: pack_histories(): final_state, ranks = lax.scan(advance, start_state, seq_lengths)]
    dynamic_slice x32 -> x0, local copies, waits for them, and re-layouts: 29.6 us -> none  [the longest x16 19.9 us: pack_histories(): final_state, ranks = lax.scan(advance, start_state, seq_lengths)]
  transfers between devices with their start and end apart: 4 -> 3, of which waited for: 2 -> 1; matrix products, arithmetic and copies ran while one was open for 23% -> 0% of each run, Pallas kernels for 0% -> 20%
where the time goes in v1:
time: 262 us; the launch traced here: 261 us
  Pallas kernels  143 us (55%)
  blocking collectives  101 us (39%)
  starting transfers between devices  8.28 us (3%)
  local copies, waits for them, and re-layouts  3.86 us (1%)
  waiting for transfers between devices  3.21 us (1%)
    pallas_call x1, Pallas kernels, per_device(): pl.pallas_call(backward_kernel, out_shape=(blocks, struct((2, HALF, LANES...  51.2 us
    pallas_call x1, Pallas kernels, per_device(): pl.pallas_call(forward_kernel, out_shape=(wide, pairs, pairs, pairs, stru...  34.9 us
    pallas_call x1, Pallas kernels, per_device(): pl.pallas_call(send_kernel, out_shape=(blocks, blocks), in_specs=[SMEM_SP...  33.7 us
    all_to_all x1, blocking collectives, per_device(): lax.all_to_all(chip_sum.reshape(64, PART, LANES), ('grp', 'chip'), 0, 0,...  29.6 us
    all_to_all x1, blocking collectives, per_device(): got_rows = lax.all_to_all(send_rows, ('chip', 'core'), 0, 0, tiled=True)  26.3 us
    all_to_all x1, blocking collectives, per_device(): lax.all_to_all(copies, ('grp', 'chip'), 0, 0, tiled=True)  25.5 us
    all_to_all x1, blocking collectives, per_device(): came_back = lax.all_to_all(send_back, ('chip', 'core'), 0, 0, tiled=True)  20.1 us
    pallas_call x1, Pallas kernels, per_device(): pl.pallas_call(home_kernel, out_shape=struct((LOCAL, BLOCK, D), BF), in_s...  17.8 us
  transfers between devices with their start and end apart: 3, of which 1 were waited for; matrix products, arithmetic and copies ran while one was open for 0% of the time, Pallas kernels for 20%

profile of v1, /device:TPU:1, one launch (start us, length us, event | category | flops | bytes accessed | tf_op | source)
XLA Modules:
  0.0 260.7 jit_solution(17754563380105544915)
XLA Ops:
  0.6 33.7 %send_blocks.1 = (bf16[16,64,512]{2,1,0:T(8,128)(2,1)}, bf16[16,64,512]{2,1,0:T(8,128)(2,1)}) custom-call(s32[16]{0:T(128)} %bitcast.22, s32[1]{0:T(128)} %bitcast.1.own_ref, bf16[8,64,512]{2,1,0:T(8,128)(2,1)} %bitcast.19, bf16[8,64,512]{2,1,0:T(8,128)(2,1)} %bitcast.20), custom_call_target="tpu_custom_call" | custom-call | tf_op jit(solution)/shard_map/send_blocks/pallas_call | solution.py:512
  34.4 26.3 %all_to_all.25.got_ref = bf16[16,64,512]{2,1,0:T(8,128)(2,1)} all-to-all(bf16[16,64,512]{2,1,0:T(8,128)(2,1)} %get-tuple-element.20), channel_id=1, replica_groups=mesh['grp'=8,'chip'=8,'core'=2] {'chip','core'}, dimensions={0} | all-to-all | bytes 2097152 | tf_op jit(solution)/shard_map/all_to_all | solution.py:520
  60.7 4.6 %all-to-all-start.1 = ((bf16[16,64,512]{2,1,0:T(8,128)(2,1)}), bf16[16,64,512]{2,1,0:T(8,128)(2,1)S(1)}, u32[]{:S(2)}, u32[]{:S(2)}) async-start(bf16[16,64,512]{2,1,0:T(8,128)(2,1)} %get-tuple-element.21), calls=%async_computation.1 | async-start | bytes 2097152 | tf_op jit(solution)/shard_map/all_to_all | solution.py:521
  65.3 34.9 %forward_layer.1 = (bf16[1024,512]{1,0:T(8,128)(2,1)}, bf16[4,1024,128]{2,1,0:T(8,128)(2,1)}, bf16[4,1024,128]{2,1,0:T(8,128)(2,1)}, bf16[4,1024,128]{2,1,0:T(8,...) custom-call(s32[16]{0:T(128)} %bitcast.23, s32[1]{0:T(128)} %bitcast.1.own_ref, ...), custom_call_target="tpu_custom_call" | custom-call | tf_op jit(solution)/shard_map/forward_layer/pallas_call | solution.py:524
  100.3 0.0 all-to-all-done.1.grads_ref
  100.3 0.0 copy-start.1
  100.3 1.0 copy-done.1
  101.2 51.2 %backward_layer.1 = (bf16[16,64,512]{2,1,0:T(8,128)(2,1)}, bf16[2,5632,128]{2,1,0:T(8,128)(2,1)}) custom-call(s32[16]{0:T(128)} %bitcast.24, s32[1]{0:T(128)} %bitcast.1.own_ref, bf16[16,64,512]{2,1,0:T(8,128)(2,1)} %all_to_all.25.got_ref, bf16[16,64,512]{2,1,0:T(8,128)(2,1)} %copy-done.1, bf16[1024,512]{1,0:T(8,128)(2,1)} %get-tuple-element.22.upper_ref, ...), custom_call_target="tpu_custom_call" | custom-call | tf_op jit(solution)/shard_map/backward_layer/pallas_call | solution.py:546
  152.5 0.0 copy-start.2
  152.5 1.6 slice_bitcast_fusion
  154.1 0.1 collective-permute-start
  154.2 3.2 %collective-permute-done = bf16[5632,128]{1,0:T(8,128)(2,1)S(1)} collective-permute-done((bf16[5632,128]{1,0:T(8,128)(2,1)S(1)}, bf16[5632,128]{1,0:T(8,128)(2,1)S(1)}, u32[]{:S(2)}, u32[]{:S(2)}) %collective-permute-start) | collective-permute-done | bytes 1441824 | tf_op jit(solution)/shard_map/ppermute | solution.py:579
  157.4 0.0 copy-done.2
  157.4 0.4 fusion
  157.8 29.6 %all_to_all.26 = bf16[64,88,128]{2,1,0:T(8,128)(2,1)S(1)} all-to-all(bf16[64,88,128]{2,1,0:T(8,128)(2,1)S(1)} %bitcast.18), channel_id=1, replica_groups=mesh['grp'=8,'chip'=8,'core'=2] {'grp','chip'}, dimensions={0} | all-to-all | bytes 2883584 | tf_op jit(solution)/shard_map/all_to_all | solution.py:581
  187.3 0.2 convert_reduce_fusion
  187.6 0.2 broadcast_in_dim.2
  187.8 0.0 copy-start.4
  187.8 25.5 %all_to_all.27 = bf16[64,88,128]{2,1,0:T(8,128)(2,1)S(1)} all-to-all(bf16[64,88,128]{2,1,0:T(8,128)(2,1)S(1)} %broadcast_in_dim.2), channel_id=1, replica_groups=mesh['grp'=8,'chip'=8,'core'=2] {'grp','chip'}, dimensions={0} | all-to-all | bytes 2883584 | tf_op jit(solution)/shard_map/all_to_all | solution.py:584
  213.2 0.0 copy-start
  213.2 3.6 %collective-permute-start.1 = (bf16[5632,128]{1,0:T(8,128)(2,1)S(1)}, bf16[5632,128]{1,0:T(8,128)(2,1)S(1)}, u32[]{:S(2)}, u32[]{:S(2)}) collective-permute-start(bf16[5632,128]{1,0:T(8,128)(2,1)S(1)} %bitcast.16), channel_id=1, source_target_pairs={{0,1},{1,0},{2,3},{3,2},{4,5},{5,4},{6,7},{7,6},{8,9},{9,8},{10,11... | collective-permute-start | bytes 4325384 | tf_op jit(solution)/shard_map/ppermute | solution.py:585
  216.8 0.0 copy-done.4
  216.8 20.1 %all_to_all.28.back_ref = bf16[16,64,512]{2,1,0:T(8,128)(2,1)} all-to-all(bf16[16,64,512]{2,1,0:T(8,128)(2,1)S(1)} %copy-done.4), channel_id=1, replica_groups=mesh['grp'=8,'chip'=8,'core'=2] {'chip','core'}, dimensions={0} | all-to-all | bytes 2097152 | tf_op jit(solution)/shard_map/all_to_all | solution.py:586
  236.9 17.8 %take_home.1 = bf16[8,64,512]{2,1,0:T(8,128)(2,1)} custom-call(s32[16]{0:T(128)} %bitcast.25, s32[1]{0:T(128)} %bitcast.1.own_ref, bf16[16,64,512]{2,1,0:T(8,128)(2,1)} %all_to_all.28.back_ref), custom_call_target="tpu_custom_call" | custom-call | tf_op jit(solution)/shard_map/take_home/pallas_call | solution.py:587
  254.7 0.0 copy-done
  254.7 0.0 collective-permute-done.1.other_ref
  254.8 0.0 copy-start.3
  254.8 1.1 copy-done.3
  255.8 4.8 %spread_grads.1 = (f32[512,2048]{1,0:T(8,128)}, f32[512,512]{1,0:T(8,128)}, f32[4,128]{1,0:T(4,128)}, f32[4,128]{1,0:T(4,128)}) custom-call(s32[1]{0:T(128)} %bitcast.1.own_ref, bf16[5632,128]{1,0:T(8,128)(2,1)} %bitcast.17, bf16[5632,128]{1,0:T(8,128)(2,1)} %copy-done.3), custom_call_target="tpu_custom_call" | custom-call | tf_op jit(solution)/shard_map/spread_grads/pallas_call | solution.py:596
  (1 shorter events, 0.0 us)
Async XLA Ops:
  60.7 39.6 %all-to-all-start.1 = ((bf16[16,64,512]{2,1,0:T(8,128)(2,1)}), bf16[16,64,512]{2,1,0:T(8,128)(2,1)S(1)}, u32[]{:S(2)}, u32[]{:S(2)}) async-start(bf16[16,64,512]{2,1,0:T(8,128)(2,1)} %get-tuple-element.21), calls=%async_computation.1 | async-start | bytes 2097152 | tf_op jit(solution)/shard_map/all_to_all | solution.py:521
  100.3 1.0 copy-start.1
  152.5 4.9 %copy-start.2 = (bf16[2,5632,128]{2,1,0:T(8,128)(2,1)S(1)}, bf16[2,5632,128]{2,1,0:T(8,128)(2,1)}, u32[]{:S(2)}) copy-start(bf16[2,5632,128]{2,1,0:T(8,128)(2,1)} %get-tuple-element.30) | copy-start | bytes 8650756
  154.1 3.3 %collective-permute-start = (bf16[5632,128]{1,0:T(8,128)(2,1)S(1)}, bf16[5632,128]{1,0:T(8,128)(2,1)S(1)}, u32[]{:S(2)}, u32[]{:S(2)}) collective-permute-start(bf16[5632,128]{1,0:T(8,128)(2,1)S(1)} %slice_bitcast_fusion), channel_id=1, source_target_pairs={{0,1},{1,0},{2,3},{3,2},{4,5},{5,4},{6,7},{7,6},{8,9},{9,8},{10,11... | collective-permute-start | bytes 4325384 | tf_op jit(solution)/shard_map/ppermute | solution.py:579
  187.8 29.1 %copy-start.4 = (bf16[16,64,512]{2,1,0:T(8,128)(2,1)S(1)}, bf16[16,64,512]{2,1,0:T(8,128)(2,1)}, u32[]{:S(2)}) copy-start(bf16[16,64,512]{2,1,0:T(8,128)(2,1)} %get-tuple-element.29) | copy-start | bytes 3145732
  213.2 41.5 %copy-start = (bf16[64,88,128]{2,1,0:T(8,128)(2,1)}, bf16[64,88,128]{2,1,0:T(8,128)(2,1)S(1)}, u32[]{:S(2)}) copy-start(bf16[64,88,128]{2,1,0:T(8,128)(2,1)S(1)} %all_to_all.27) | copy-start | bytes 4325380
  213.2 41.5 %collective-permute-start.1 = (bf16[5632,128]{1,0:T(8,128)(2,1)S(1)}, bf16[5632,128]{1,0:T(8,128)(2,1)S(1)}, u32[]{:S(2)}, u32[]{:S(2)}) collective-permute-start(bf16[5632,128]{1,0:T(8,128)(2,1)S(1)} %bitcast.16), channel_id=1, source_target_pairs={{0,1},{1,0},{2,3},{3,2},{4,5},{5,4},{6,7},{7,6},{8,9},{9,8},{10,11... | collective-permute-start | bytes 4325384 | tf_op jit(solution)/shard_map/ppermute | solution.py:585
  254.8 1.1 copy-start.3

commit v2 on v1

--- a/solution.py
+++ b/solution.py
@@ -98,28 +98,16 @@
             lax.fori_loop(begin, begin + sizes[i], put, 0)
 
 
-def send_kernel(len_ref, own_ref, rows_ref, grads_ref, rows_out, grads_out, sems):
+def send_kernel(len_ref, own_ref, rows_ref, out_ref):
     owner = owners(len_ref, own_ref[0])
-    copies = []
-    for n, (src, dst) in enumerate(((rows_ref, rows_out), (grads_ref, grads_out))):
-        for k in range(LOCAL):
-            copies.append(pltpu.make_async_copy(src.at[k], dst.at[owner[k]], sems.at[n, k]))
-    for copy in copies:
-        copy.start()
-    for copy in copies:
-        copy.wait()
-
-
-def home_kernel(len_ref, own_ref, back_ref, out_ref, sems):
+    for k in range(LOCAL):
+        out_ref[owner[k]] = rows_ref[k]
+
+
+def home_kernel(len_ref, own_ref, back_ref, out_ref):
     owner = owners(len_ref, own_ref[0])
-    copies = [
-        pltpu.make_async_copy(back_ref.at[owner[k]], out_ref.at[k], sems.at[k])
-        for k in range(LOCAL)
-    ]
-    for copy in copies:
-        copy.start()
-    for copy in copies:
-        copy.wait()
+    for k in range(LOCAL):
+        out_ref[k] = back_ref[owner[k]]
 
 
 def fetch(src_ref, dst_ref, sems, first, count):
@@ -505,23 +493,20 @@
     return pltpu.CompilerParams(vmem_limit_bytes=VMEM_LIMIT)
 
 
-def per_device(events, cotangent, lengths, gain_in, w_proj, gain_attn, w_out):
-    own = lax.axis_index(("chip", "core")).astype(jnp.int32).reshape(1)
-    lens = lengths[0]
-    blocks = struct((PEERS, BLOCK, D), BF)
-    send_rows, send_grads = pl.pallas_call(
+def send_blocks(lens, own, rows):
+    return pl.pallas_call(
         send_kernel,
-        out_shape=(blocks, blocks),
-        in_specs=[SMEM_SPEC, SMEM_SPEC, ANY_SPEC, ANY_SPEC],
-        out_specs=(ANY_SPEC, ANY_SPEC),
-        scratch_shapes=[pltpu.SemaphoreType.DMA((2, LOCAL))],
+        out_shape=struct((PEERS, BLOCK, D), BF),
+        in_specs=[SMEM_SPEC, SMEM_SPEC, VMEM_SPEC],
+        out_specs=VMEM_SPEC,
         name="send_blocks",
-    )(lens, own, events.reshape(LOCAL, BLOCK, D), cotangent.reshape(LOCAL, BLOCK, D))
-    got_rows = lax.all_to_all(send_rows, ("chip", "core"), 0, 0, tiled=True)
-    got_grads = lax.all_to_all(send_grads, ("chip", "core"), 0, 0, tiled=True)
+    )(lens, own, rows.reshape(LOCAL, BLOCK, D))
+
+
+def forward_layer(lens, own, got_rows, w_proj, gain_in):
     pairs = struct((PAIRS, ROWS, LANES), BF)
     wide = struct((ROWS, D), BF)
-    saved = pl.pallas_call(
+    return pl.pallas_call(
         forward_kernel,
         out_shape=(
             wide,
@@ -542,10 +527,13 @@
         ],
         compiler_params=params(),
         name="forward_layer",
-    )(lens, own, got_rows, w_proj, gain_in.reshape(1, D))
-    send_back, terms = pl.pallas_call(
+    )(lens, own, got_rows, w_proj, gain_in)
+
+
+def backward_layer(lens, own, got_rows, got_grads, saved, w_proj, w_out, gain_in, gain_attn):
+    return pl.pallas_call(
         backward_kernel,
-        out_shape=(blocks, struct((2, HALF, LANES), BF)),
+        out_shape=(struct((PEERS, BLOCK, D), BF), struct((2, HALF, LANES), BF)),
         in_specs=[SMEM_SPEC, SMEM_SPEC, ANY_SPEC, ANY_SPEC] + [VMEM_SPEC] * 11,
         out_specs=(VMEM_SPEC, VMEM_SPEC),
         scratch_shapes=[
@@ -565,15 +553,19 @@
         compiler_params=params(),
         name="backward_layer",
     )(
-        lens,
-        own,
-        got_rows,
-        got_grads,
-        *saved,
-        w_proj,
-        w_out,
-        gain_in.reshape(1, D),
-        gain_attn.reshape(1, D),
+        lens, own, got_rows, got_grads, *saved, w_proj, w_out, gain_in, gain_attn
+    )
+
+
+def per_device(events, cotangent, lengths, gain_in, w_proj, gain_attn, w_out):
+    own = lax.axis_index(("chip", "core")).astype(jnp.int32).reshape(1)
+    lens = lengths[0]
+    got_rows = lax.all_to_all(send_blocks(lens, own, events), ("chip", "core"), 0, 0, tiled=True)
+    got_grads = lax.all_to_all(send_blocks(lens, own, cotangent), ("chip", "core"), 0, 0, tiled=True)
+    gain_in = gain_in.reshape(1, D)
+    saved = forward_layer(lens, own, got_rows, w_proj, gain_in)
+    send_back, terms = backward_layer(
+        lens, own, got_rows, got_grads, saved, w_proj, w_out, gain_in, gain_attn.reshape(1, D)
     )
     swap = [(0, 1), (1, 0)]
     other = lax.ppermute(terms[1], "core", swap)
@@ -587,9 +579,8 @@
     d_rows = pl.pallas_call(
         home_kernel,
         out_shape=struct((LOCAL, BLOCK, D), BF),
-        in_specs=[SMEM_SPEC, SMEM_SPEC, ANY_SPEC],
-        out_specs=ANY_SPEC,
-        scratch_shapes=[pltpu.SemaphoreType.DMA((LOCAL,))],
+        in_specs=[SMEM_SPEC, SMEM_SPEC, VMEM_SPEC],
+        out_specs=VMEM_SPEC,
         name="take_home",
     )(lens, own, came_back)
     gain = struct((PAIRS, LANES), F32)

time: 262 us -> 215 us (0.82)
  Pallas kernels: 143 us -> 72.9 us
  starting transfers between devices: 8.28 us -> 42.2 us
  blocking collectives: 101 us -> 75.7 us
  waiting for transfers between devices: 3.21 us -> 17.8 us
    pallas_call x3 -> x4, Pallas kernels: 120 us -> 65.9 us  [the longest x1 36.7 us: backward_layer(): pl.pallas_call(backward_kernel, out_shape=(struct((PEERS, BLOCK, D), BF),...]
    all_to_all x1 -> x0, blocking collectives: 26.3 us -> none  [per_device(): got_rows = lax.all_to_all(send_rows, ('chip', 'core'), 0, 0, tiled=True)]
    ppermute x1, starting transfers between devices: 0.09 us -> 25.2 us  [per_device(): other = lax.ppermute(terms[1], 'core', swap)]
    pallas_call x1, Pallas kernels: 17.8 us -> 2.21 us  [per_device(): pl.pallas_call(home_kernel, out_shape=struct((LOCAL, BLOCK, D), BF), in_s...]
    all_to_all x1 -> x2, waiting for transfers between devices: 0.01 us -> 15 us  [the longest x1 15 us: per_device(): lax.all_to_all(send_blocks(lens, own, events), ('chip', 'core'), 0, 0, ti...]
    all_to_all x1 -> x2, starting transfers between devices: 4.61 us -> 13.6 us  [the longest x1 9.29 us: per_device(): lax.all_to_all(send_blocks(lens, own, events), ('chip', 'core'), 0, 0, ti...]
  transfers between devices with their start and end apart: 3 -> 4, of which waited for: 1 -> 2; matrix products, arithmetic and copies ran while one was open for 0% -> 0% of each run, Pallas kernels for 20% -> 14%
where the time goes in v2:
time: 215 us; the launch traced here: 214 us
  blocking collectives  75.7 us (35%)
  Pallas kernels  72.9 us (34%)
  starting transfers between devices  42.2 us (20%)
  waiting for transfers between devices  17.8 us (8%)
  local copies, waits for them, and re-layouts  3.87 us (2%)
    pallas_call x1, Pallas kernels, backward_layer(): pl.pallas_call(backward_kernel, out_shape=(struct((PEERS, BLOCK, D), BF),...  36.7 us
    all_to_all x1, blocking collectives, per_device(): lax.all_to_all(chip_sum.reshape(64, PART, LANES), ('grp', 'chip'), 0, 0,...  30.3 us
    all_to_all x1, blocking collectives, per_device(): lax.all_to_all(copies, ('grp', 'chip'), 0, 0, tiled=True)  25.3 us
    ppermute x1, starting transfers between devices, per_device(): other = lax.ppermute(terms[1], 'core', swap)  25.2 us
    pallas_call x1, Pallas kernels, forward_layer(): pl.pallas_call(forward_kernel, out_shape=(wide, pairs, pairs, pairs, stru...  24.7 us
    all_to_all x1, blocking collectives, per_device(): came_back = lax.all_to_all(send_back, ('chip', 'core'), 0, 0, tiled=True)  20.1 us
    all_to_all x1, waiting for transfers between devices, per_device(): lax.all_to_all(send_blocks(lens, own, events), ('chip', 'core'), 0, 0, ti...  15 us
    all_to_all x1, starting transfers between devices, per_device(): lax.all_to_all(send_blocks(lens, own, events), ('chip', 'core'), 0, 0, ti...  9.29 us
  transfers between devices with their start and end apart: 4, of which 2 were waited for; matrix products, arithmetic and copies ran while one was open for 0% of the time, Pallas kernels for 14%

profile of v2, /device:TPU:1, one launch (start us, length us, event | category | flops | bytes accessed | tf_op | source)
XLA Modules:
  0.0 213.8 jit_solution(13320150727854509730)
XLA Ops:
  0.6 2.2 %send_blocks.2 = bf16[16,64,512]{2,1,0:T(8,128)(2,1)} custom-call(s32[16]{0:T(128)} %bitcast.22, s32[1]{0:T(128)} %bitcast.1.own_ref, bf16[8,64,512]{2,1,0:T(8,128)(2,1)} %bitcast.19), custom_call_target="tpu_custom_call" | custom-call | tf_op jit(solution)/shard_map/send_blocks/pallas_call | solution.py:497
  2.9 9.3 %all-to-all-start = ((bf16[16,64,512]{2,1,0:T(8,128)(2,1)}), bf16[16,64,512]{2,1,0:T(8,128)(2,1)S(1)}, u32[]{:S(2)}, u32[]{:S(2)}) async-start(bf16[16,64,512]{2,1,0:T(8,128)(2,1)} %send_blocks.2), calls=%async_computation | async-start | bytes 2097152 | tf_op jit(solution)/shard_map/all_to_all | solution.py:563
  12.2 2.2 %send_blocks.3 = bf16[16,64,512]{2,1,0:T(8,128)(2,1)} custom-call(s32[16]{0:T(128)} %bitcast.23, s32[1]{0:T(128)} %bitcast.1.own_ref, bf16[8,64,512]{2,1,0:T(8,128)(2,1)} %bitcast.20), custom_call_target="tpu_custom_call" | custom-call | tf_op jit(solution)/shard_map/send_blocks/pallas_call | solution.py:497
  14.4 15.0 %all-to-all-done.got_ref = bf16[16,64,512]{2,1,0:T(8,128)(2,1)S(1)} async-done(((bf16[16,64,512]{2,1,0:T(8,128)(2,1)}), bf16[16,64,512]{2,1,0:T(8,128)(2,1)S(1)}, u32[]{:S(2)}, u32[]{:S(2)}) %all-to-all-start) | async-done | bytes 1048608 | tf_op jit(solution)/shard_map/all_to_all | solution.py:563
  29.4 0.0 copy-start
  29.4 4.4 %all-to-all-start.1 = ((bf16[16,64,512]{2,1,0:T(8,128)(2,1)}), bf16[16,64,512]{2,1,0:T(8,128)(2,1)S(1)}, u32[]{:S(2)}, u32[]{:S(2)}) async-start(bf16[16,64,512]{2,1,0:T(8,128)(2,1)} %send_blocks.3), calls=%async_computation.1 | async-start | bytes 2097152 | tf_op jit(solution)/shard_map/all_to_all | solution.py:564
  33.7 0.0 copy-done
  33.7 24.7 %forward_layer.1 = (bf16[1024,512]{1,0:T(8,128)(2,1)}, bf16[4,1024,128]{2,1,0:T(8,128)(2,1)}, bf16[4,1024,128]{2,1,0:T(8,128)(2,1)}, bf16[4,1024,128]{2,1,0:T(8,...) custom-call(s32[16]{0:T(128)} %bitcast.24, s32[1]{0:T(128)} %bitcast.1.own_ref, ...), custom_call_target="tpu_custom_call" | custom-call | tf_op jit(solution)/shard_map/forward_layer/pallas_call | solution.py:509
  58.4 0.0 all-to-all-done.1.grads_ref
  58.4 0.0 copy-start.2
  58.5 1.0 copy-done.2
  59.4 36.7 %backward_layer.1 = (bf16[16,64,512]{2,1,0:T(8,128)(2,1)}, bf16[2,5632,128]{2,1,0:T(8,128)(2,1)}) custom-call(s32[16]{0:T(128)} %bitcast.25, s32[1]{0:T(128)} %bitcast.1.own_ref, bf16[16,64,512]{2,1,0:T(8,128)(2,1)} %copy-done, bf16[16,64,512]{2,1,0:T(8,128)(2,1)} %copy-done.2, bf16[1024,512]{1,0:T(8,128)(2,1)} %get-tuple-element.18.upper_ref, ...), custom_call_target="tpu_custom_call" | custom-call | tf_op jit(solution)/shard_map/backward_layer/pallas_call | solution.py:534
  96.1 0.0 copy-start.3
  96.2 1.6 slice_bitcast_fusion
  97.8 25.2 %collective-permute-start = (bf16[5632,128]{1,0:T(8,128)(2,1)S(1)}, bf16[5632,128]{1,0:T(8,128)(2,1)S(1)}, u32[]{:S(2)}, u32[]{:S(2)}) collective-permute-start(bf16[5632,128]{1,0:T(8,128)(2,1)S(1)} %slice_bitcast_fusion), channel_id=1, source_target_pairs={{0,1},{1,0},{2,3},{3,2},{4,5},{5,4},{6,7},{7,6},{8,9},{9,8},{10,11... | collective-permute-start | bytes 4325384 | tf_op jit(solution)/shard_map/ppermute | solution.py:571
  122.9 2.8 %collective-permute-done = bf16[5632,128]{1,0:T(8,128)(2,1)S(1)} collective-permute-done((bf16[5632,128]{1,0:T(8,128)(2,1)S(1)}, bf16[5632,128]{1,0:T(8,128)(2,1)S(1)}, u32[]{:S(2)}, u32[]{:S(2)}) %collective-permute-start) | collective-permute-done | bytes 1441824 | tf_op jit(solution)/shard_map/ppermute | solution.py:571
  125.8 0.0 copy-done.3
  125.8 0.4 fusion
  126.1 30.3 %all_to_all.25 = bf16[64,88,128]{2,1,0:T(8,128)(2,1)S(1)} all-to-all(bf16[64,88,128]{2,1,0:T(8,128)(2,1)S(1)} %bitcast.18), channel_id=1, replica_groups=mesh['grp'=8,'chip'=8,'core'=2] {'grp','chip'}, dimensions={0} | all-to-all | bytes 2883584 | tf_op jit(solution)/shard_map/all_to_all | solution.py:573
  156.4 0.2 convert_reduce_fusion
  156.7 0.2 broadcast_in_dim.2
  156.9 0.0 copy-start.5
  156.9 25.3 %all_to_all.26 = bf16[64,88,128]{2,1,0:T(8,128)(2,1)S(1)} all-to-all(bf16[64,88,128]{2,1,0:T(8,128)(2,1)S(1)} %broadcast_in_dim.2), channel_id=1, replica_groups=mesh['grp'=8,'chip'=8,'core'=2] {'grp','chip'}, dimensions={0} | all-to-all | bytes 2883584 | tf_op jit(solution)/shard_map/all_to_all | solution.py:576
  182.2 0.0 copy-start.1
  182.2 3.4 %collective-permute-start.1 = (bf16[5632,128]{1,0:T(8,128)(2,1)S(1)}, bf16[5632,128]{1,0:T(8,128)(2,1)S(1)}, u32[]{:S(2)}, u32[]{:S(2)}) collective-permute-start(bf16[5632,128]{1,0:T(8,128)(2,1)S(1)} %bitcast.16), channel_id=1, source_target_pairs={{0,1},{1,0},{2,3},{3,2},{4,5},{5,4},{6,7},{7,6},{8,9},{9,8},{10,11... | collective-permute-start | bytes 4325384 | tf_op jit(solution)/shard_map/ppermute | solution.py:577
  185.6 0.0 copy-done.5
  185.6 20.1 %all_to_all.27.back_ref = bf16[16,64,512]{2,1,0:T(8,128)(2,1)} all-to-all(bf16[16,64,512]{2,1,0:T(8,128)(2,1)S(1)} %copy-done.5), channel_id=1, replica_groups=mesh['grp'=8,'chip'=8,'core'=2] {'chip','core'}, dimensions={0} | all-to-all | bytes 2097152 | tf_op jit(solution)/shard_map/all_to_all | solution.py:578
  205.7 2.2 %take_home.1 = bf16[8,64,512]{2,1,0:T(8,128)(2,1)} custom-call(s32[16]{0:T(128)} %bitcast.26, s32[1]{0:T(128)} %bitcast.1.own_ref, bf16[16,64,512]{2,1,0:T(8,128)(2,1)} %all_to_all.27.back_ref), custom_call_target="tpu_custom_call" | custom-call | tf_op jit(solution)/shard_map/take_home/pallas_call | solution.py:579
  207.9 0.0 copy-done.1
  207.9 0.0 collective-permute-done.1.other_ref
  207.9 0.0 copy-start.4
  207.9 1.1 copy-done.4
  209.0 4.8 %spread_grads.1 = (f32[512,2048]{1,0:T(8,128)}, f32[512,512]{1,0:T(8,128)}, f32[4,128]{1,0:T(4,128)}, f32[4,128]{1,0:T(4,128)}) custom-call(s32[1]{0:T(128)} %bitcast.1.own_ref, bf16[5632,128]{1,0:T(8,128)(2,1)} %bitcast.17, bf16[5632,128]{1,0:T(8,128)(2,1)} %copy-done.4), custom_call_target="tpu_custom_call" | custom-call | tf_op jit(solution)/shard_map/spread_grads/pallas_call | solution.py:587
  (1 shorter events, 0.0 us)
Async XLA Ops:
  2.9 26.5 %all-to-all-start = ((bf16[16,64,512]{2,1,0:T(8,128)(2,1)}), bf16[16,64,512]{2,1,0:T(8,128)(2,1)S(1)}, u32[]{:S(2)}, u32[]{:S(2)}) async-start(bf16[16,64,512]{2,1,0:T(8,128)(2,1)} %send_blocks.2), calls=%async_computation | async-start | bytes 2097152 | tf_op jit(solution)/shard_map/all_to_all | solution.py:563
  29.4 4.4 %copy-start = (bf16[16,64,512]{2,1,0:T(8,128)(2,1)}, bf16[16,64,512]{2,1,0:T(8,128)(2,1)S(1)}, u32[]{:S(2)}) copy-start(bf16[16,64,512]{2,1,0:T(8,128)(2,1)S(1)} %all-to-all-done.got_ref) | copy-start | bytes 3145732
  29.4 29.1 %all-to-all-start.1 = ((bf16[16,64,512]{2,1,0:T(8,128)(2,1)}), bf16[16,64,512]{2,1,0:T(8,128)(2,1)S(1)}, u32[]{:S(2)}, u32[]{:S(2)}) async-start(bf16[16,64,512]{2,1,0:T(8,128)(2,1)} %send_blocks.3), calls=%async_computation.1 | async-start | bytes 2097152 | tf_op jit(solution)/shard_map/all_to_all | solution.py:564
  58.4 1.0 copy-start.2
  96.1 29.6 %copy-start.3 = (bf16[2,5632,128]{2,1,0:T(8,128)(2,1)S(1)}, bf16[2,5632,128]{2,1,0:T(8,128)(2,1)}, u32[]{:S(2)}) copy-start(bf16[2,5632,128]{2,1,0:T(8,128)(2,1)} %get-tuple-element.26) | copy-start | bytes 8650756
  97.8 28.0 %collective-permute-start = (bf16[5632,128]{1,0:T(8,128)(2,1)S(1)}, bf16[5632,128]{1,0:T(8,128)(2,1)S(1)}, u32[]{:S(2)}, u32[]{:S(2)}) collective-permute-start(bf16[5632,128]{1,0:T(8,128)(2,1)S(1)} %slice_bitcast_fusion), channel_id=1, source_target_pairs={{0,1},{1,0},{2,3},{3,2},{4,5},{5,4},{6,7},{7,6},{8,9},{9,8},{10,11... | collective-permute-start | bytes 4325384 | tf_op jit(solution)/shard_map/ppermute | solution.py:571
  156.9 28.7 %copy-start.5 = (bf16[16,64,512]{2,1,0:T(8,128)(2,1)S(1)}, bf16[16,64,512]{2,1,0:T(8,128)(2,1)}, u32[]{:S(2)}) copy-start(bf16[16,64,512]{2,1,0:T(8,128)(2,1)} %get-tuple-element.25) | copy-start | bytes 3145732
  182.2 25.7 %copy-start.1 = (bf16[64,88,128]{2,1,0:T(8,128)(2,1)}, bf16[64,88,128]{2,1,0:T(8,128)(2,1)S(1)}, u32[]{:S(2)}) copy-start(bf16[64,88,128]{2,1,0:T(8,128)(2,1)S(1)} %all_to_all.26) | copy-start | bytes 4325380
  182.2 25.7 %collective-permute-start.1 = (bf16[5632,128]{1,0:T(8,128)(2,1)S(1)}, bf16[5632,128]{1,0:T(8,128)(2,1)S(1)}, u32[]{:S(2)}, u32[]{:S(2)}) collective-permute-start(bf16[5632,128]{1,0:T(8,128)(2,1)S(1)} %bitcast.16), channel_id=1, source_target_pairs={{0,1},{1,0},{2,3},{3,2},{4,5},{5,4},{6,7},{7,6},{8,9},{9,8},{10,11... | collective-permute-start | bytes 4325384 | tf_op jit(solution)/shard_map/ppermute | solution.py:577
  207.9 1.1 copy-start.4

commit v3 on v2

--- a/solution.py
+++ b/solution.py
@@ -23,7 +23,7 @@
 DEVICES = 128
 BF = jnp.bfloat16
 F32 = jnp.float32
-VMEM_LIMIT = 56 * 1024 * 1024
+VMEM_LIMIT = 52 * 1024 * 1024
 
 SMEM_SPEC = pl.BlockSpec(memory_space=pltpu.SMEM)
 ANY_SPEC = pl.BlockSpec(memory_space=pl.ANY)
@@ -146,6 +146,9 @@
     return low, high
 
 
+GROUP = 4
+
+
 def rows_at(t):
     return pl.ds(pl.multiple_of(t * TILE, TILE), TILE)
 
@@ -170,17 +173,24 @@
     got_ref,
     w_ref,
     gain_ref,
+    attn_ref,
+    upper_out,
+    values_out,
+    query_out,
+    keys_out,
+    slope_out,
+    scaled_out,
     upper_ref,
     values_ref,
     query_ref,
     keys_ref,
     slope_ref,
-    attn_ref,
     scaled_ref,
     rows_ref,
     acc_ref,
     hist_ref,
     sems,
+    save_sems,
 ):
     own = own_ref[0]
     starts, sizes, ranks, first, count = holdings(len_ref, own)
@@ -220,29 +230,47 @@
 
     lax.fori_loop(live, TILES, clear, 0)
 
+    saves = [
+        pltpu.make_async_copy(src, dst, save_sems.at[n])
+        for n, (src, dst) in enumerate(
+            (
+                (upper_ref, upper_out),
+                (values_ref, values_out),
+                (query_ref, query_out),
+                (keys_ref, keys_out),
+                (slope_ref, slope_out),
+                (scaled_ref, scaled_out),
+            )
+        )
+    ]
+    for save in saves:
+        save.start()
+
     masks = head_masks()
 
-    def pair(p, carry):
+    def group(g, carry):
         def query_tile(i, carry):
-            query = query_ref[p, rows_at(i), :]
-            acc_ref[...] = jnp.zeros((TILE, LANES), F32)
+            acc_ref[...] = jnp.zeros((GROUP, TILE, LANES), F32)
 
             def step(j, masked):
-                keys = keys_ref[p, rows_at(j), :]
-                values = values_ref[p, rows_at(j), :]
                 if masked:
                     shape = (TILE, TILE)
                     col = lax.broadcasted_iota(jnp.int32, shape, 1) + j * TILE
                     row = lax.broadcasted_iota(jnp.int32, shape, 0) + i * TILE
                     allowed = (col <= row) & (col >= block_starts(hist_ref, i, shape, 0))
-                total = acc_ref[...]
-                for mask in masks:
-                    half = dot_cols(query, keys * mask)
-                    weights = half + half * jnp.tanh(half)
-                    if masked:
-                        weights = jnp.where(allowed, weights, 0.0)
-                    total += dot(weights.astype(BF), values * mask)
-                acc_ref[...] = total
+                for n in range(GROUP):
+                    p = g * GROUP + n
+                    query = query_ref[p, rows_at(i), :]
+                    keys = keys_ref[p, rows_at(j), :]
+                    values = values_ref[p, rows_at(j), :]
+                    total = acc_ref[n]
+                    for mask in masks:
+                        half = dot_cols(query, keys * mask)
+                        weights = half + half * jnp.tanh(half)
+                        if masked:
+                            weights = jnp.where(allowed, weights, 0.0)
+                        total += dot(weights.astype(BF), values * mask)
+                    acc_ref[n] = total
 
             low, clear_from = key_tiles(hist_ref, i)
 
@@ -257,12 +285,15 @@
             lax.fori_loop(low, clear_from, masked_step, 0)
             lax.fori_loop(clear_from, i, clear_step, 0)
             step(i, True)
-            attn_ref[p, rows_at(i), :] = acc_ref[...].astype(BF)
+            for n in range(GROUP):
+                attn_ref[g * GROUP + n, rows_at(i), :] = acc_ref[n].astype(BF)
             return carry
 
         return lax.fori_loop(0, live, query_tile, carry)
 
-    lax.fori_loop(0, PAIRS, pair, 0)
+    lax.fori_loop(0, PAIRS // GROUP, group, 0)
+    for save in saves:
+        save.wait()
 
 
 def backward_kernel(
@@ -270,14 +301,14 @@
     own_ref,
     got_ref,
     grads_ref,
-    upper_ref,
-    values_ref,
-    query_ref,
-    keys_ref,
-    slope_ref,
-    attn_ref,
-    scaled_ref,
-    w_ref,
+    attn_in,
+    upper_in,
+    values_in,
+    query_in,
+    keys_in,
+    slope_in,
+    scaled_in,
+    w_in,
     w_out_ref,
     gain_in_ref,
     gain_attn_ref,
@@ -290,22 +321,54 @@
     out_ref,
     gains_ref,
     d_query_ref,
+    keys_t_ref,
     d_keys_ref,
     d_values_ref,
     hist_ref,
     row_sems,
     cot_sems,
+    load_sems,
+    attn_ref,
+    upper_ref,
+    values_ref,
+    query_ref,
+    keys_ref,
+    slope_ref,
+    scaled_ref,
+    w_ref,
 ):
     own = own_ref[0]
     core = own & 1
     starts, sizes, ranks, first, count = holdings(len_ref, own)
     fetch(grads_ref, cot_ref, cot_sems, first, count)
+    early = pl.ds(0, PAIRS)
+    late = pl.ds(PAIRS, 3 * PAIRS)
+    loads = [
+        pltpu.make_async_copy(src, dst, load_sems.at[n])
+        for n, (src, dst) in enumerate(
+            (
+                (attn_in, attn_ref),
+                (upper_in, upper_ref),
+                (slope_in.at[early], slope_ref.at[early]),
+                (keys_in, keys_ref),
+                (query_in, query_ref),
+                (values_in, values_ref),
+                (slope_in.at[late], slope_ref.at[late]),
+                (w_in, w_ref),
+                (scaled_in, scaled_ref),
+            )
+        )
+    ]
+    for load in loads:
+        load.start()
     fetch(got_ref, rows_ref, row_sems, first, count)
     history_starts(hist_ref, own, starts, sizes, ranks, first)
     live = (count + 3) // 4
     out_ref[...] = jnp.zeros((D, D), F32)
     gains_ref[...] = jnp.zeros((2, D), F32)
     arrive(grads_ref, cot_ref, cot_sems, count)
+    for load in loads[:3]:
+        load.wait()
 
     def middle(t, carry):
         rows = rows_at(t)
@@ -341,20 +404,25 @@
     lax.fori_loop(live, TILES, clear, 0)
 
     masks = head_masks()
-
-    def pair(p, carry):
-        d_keys_ref[...] = jnp.zeros((ROWS, LANES), F32)
-        d_values_ref[...] = jnp.zeros((ROWS, LANES), F32)
+    for load in loads[3:7]:
+        load.wait()
+
+    def turn(t, carry):
+        for p in range(PAIRS):
+            keys_t_ref[p, :, rows_at(t)] = keys_ref[p, rows_at(t), :].T
+        return carry
+
+    lax.fori_loop(0, live, turn, 0)
+
+    def group(g, carry):
+        d_keys_ref[...] = jnp.zeros((GROUP, ROWS, LANES), F32)
+        d_values_ref[...] = jnp.zeros((GROUP, ROWS, LANES), F32)
 
         def query_tile(i, carry):
-            query = query_ref[p, rows_at(i), :]
-            d_attn = d_attn_ref[p, rows_at(i), :]
-            d_query_ref[...] = jnp.zeros((TILE, LANES), F32)
+            d_query_ref[...] = jnp.zeros((GROUP, LANES, TILE), F32)
 
             def step(j, masked):
                 rows = rows_at(j)
-                keys = keys_ref[p, rows, :]
-                values = values_ref[p, rows, :]
                 if masked:
                     shape = (TILE, TILE)
                     key_row = lax.broadcasted_iota(jnp.int32, shape, 0) + j * TILE
@@ -362,27 +430,32 @@
                     allowed = (key_row <= query_row) & (
                         key_row >= block_starts(hist_ref, i, shape, 1)
                     )
-                d_query = d_query_ref[...]
-                d_keys = d_keys_ref[rows, :]
-                d_values = d_values_ref[rows, :]
-                for mask in masks:
-                    masked_keys = keys * mask
-                    half = dot_cols(masked_keys, query)
-                    swing = jnp.tanh(half)
-                    bend = half * swing
-                    weights = half + bend
-                    slope = (1.0 + swing) * ((1.0 + half) - bend)
-                    grad = dot_cols(values * mask, d_attn) * slope
-                    if masked:
-                        weights = jnp.where(allowed, weights, 0.0)
-                        grad = jnp.where(allowed, grad, 0.0)
-                    grad = grad.astype(BF)
-                    d_values += dot(weights.astype(BF), d_attn * mask)
-                    d_keys += dot(grad, query * mask)
-                    d_query += dot_rows(grad, masked_keys)
-                d_query_ref[...] = d_query
-                d_keys_ref[rows, :] = d_keys
-                d_values_ref[rows, :] = d_values
+                for n in range(GROUP):
+                    p = g * GROUP + n
+                    query = query_ref[p, rows_at(i), :]
+                    d_attn = d_attn_ref[p, rows_at(i), :]
+                    keys = keys_ref[p, rows, :]
+                    values = values_ref[p, rows, :]
+                    d_keys = d_keys_ref[n, rows, :]
+                    d_values = d_values_ref[n, rows, :]
+                    for h, mask in enumerate(masks):
+                        masked_keys = keys * mask
+                        half = dot_cols(masked_keys, query)
+                        swing = jnp.tanh(half)
+                        bend = half * swing
+                        weights = half + bend
+                        slope = (1.0 + swing) * ((1.0 + half) - bend)
+                        grad = dot_cols(values * mask, d_attn) * slope
+                        if masked:
+                            weights = jnp.where(allowed, weights, 0.0)
+                            grad = jnp.where(allowed, grad, 0.0)
+                        grad = grad.astype(BF)
+                        d_values += dot(weights.astype(BF), d_attn * mask)
+                        d_keys += dot(grad, query * mask)
+                        head_rows = slice(h * 64, h * 64 + 64)
+                        d_query_ref[n, head_rows, :] += dot(keys_t_ref[p, head_rows, rows], grad)
+                    d_keys_ref[n, rows, :] = d_keys
+                    d_values_ref[n, rows, :] = d_values
 
             low, clear_from = key_tiles(hist_ref, i)
 
@@ -397,27 +470,31 @@
             lax.fori_loop(low, clear_from, masked_step, 0)
             lax.fori_loop(clear_from, i, clear_step, 0)
             step(i, True)
-            slope = slope_ref[2 * PAIRS + p, rows_at(i), :].astype(F32)
-            d_hidden_ref[2 * PAIRS + p, rows_at(i), :] = (
-                d_query_ref[...] * 0.0625 * slope
-            ).astype(BF)
+            for n in range(GROUP):
+                place = 2 * PAIRS + g * GROUP + n
+                slope = slope_ref[place, rows_at(i), :].astype(F32)
+                d_hidden_ref[place, rows_at(i), :] = (d_query_ref[n].T * 0.0625 * slope).astype(BF)
             return carry
 
         lax.fori_loop(0, live, query_tile, 0)
 
         def finish(t, carry):
             rows = rows_at(t)
-            for place, ref in ((1, d_values_ref), (3, d_keys_ref)):
-                slope = slope_ref[place * PAIRS + p, rows, :].astype(F32)
-                d_hidden_ref[place * PAIRS + p, rows, :] = (ref[rows, :] * slope).astype(BF)
+            for n in range(GROUP):
+                for quarter, ref in ((1, d_values_ref), (3, d_keys_ref)):
+                    place = quarter * PAIRS + g * GROUP + n
+                    slope = slope_ref[place, rows, :].astype(F32)
+                    d_hidden_ref[place, rows, :] = (ref[n, rows, :] * slope).astype(BF)
             return carry
 
         lax.fori_loop(0, live, finish, 0)
         return carry
 
-    lax.fori_loop(0, PAIRS, pair, 0)
+    lax.fori_loop(0, PAIRS // GROUP, group, 0)
 
     arrive(got_ref, rows_ref, row_sems, count)
+    for load in loads[7:]:
+        load.wait()
 
     def final(t, carry):
         rows = rows_at(t)
@@ -503,27 +580,25 @@
     )(lens, own, rows.reshape(LOCAL, BLOCK, D))
 
 
+def saved_shapes(make):
+    pairs = make((PAIRS, ROWS, LANES), BF)
+    wide = make((ROWS, D), BF)
+    return [wide, pairs, pairs, pairs, make((4 * PAIRS, ROWS, LANES), BF), wide]
+
+
 def forward_layer(lens, own, got_rows, w_proj, gain_in):
-    pairs = struct((PAIRS, ROWS, LANES), BF)
-    wide = struct((ROWS, D), BF)
     return pl.pallas_call(
         forward_kernel,
-        out_shape=(
-            wide,
-            pairs,
-            pairs,
-            pairs,
-            struct((4 * PAIRS, ROWS, LANES), BF),
-            pairs,
-            wide,
-        ),
+        out_shape=[struct((PAIRS, ROWS, LANES), BF)] + saved_shapes(struct),
         in_specs=[SMEM_SPEC, SMEM_SPEC, ANY_SPEC, VMEM_SPEC, VMEM_SPEC],
-        out_specs=(VMEM_SPEC,) * 7,
-        scratch_shapes=[
+        out_specs=[VMEM_SPEC] + [ANY_SPEC] * 6,
+        scratch_shapes=saved_shapes(pltpu.VMEM)
+        + [
             pltpu.VMEM((LEN_BLK, BLOCK, D), BF),
-            pltpu.VMEM((TILE, LANES), F32),
+            pltpu.VMEM((GROUP, TILE, LANES), F32),
             pltpu.SMEM((LEN_BLK,), jnp.int32),
             pltpu.SemaphoreType.DMA((LEN_BLK,)),
+            pltpu.SemaphoreType.DMA((6,)),
         ],
         compiler_params=params(),
         name="forward_layer",
@@ -534,7 +609,7 @@
     return pl.pallas_call(
         backward_kernel,
         out_shape=(struct((PEERS, BLOCK, D), BF), struct((2, HALF, LANES), BF)),
-        in_specs=[SMEM_SPEC, SMEM_SPEC, ANY_SPEC, ANY_SPEC] + [VMEM_SPEC] * 11,
+        in_specs=[SMEM_SPEC, SMEM_SPEC] + [ANY_SPEC] * 10 + [VMEM_SPEC] * 3,
         out_specs=(VMEM_SPEC, VMEM_SPEC),
         scratch_shapes=[
             pltpu.VMEM((LEN_BLK, BLOCK, D), BF),
@@ -543,18 +618,21 @@
             pltpu.VMEM((4 * PAIRS, ROWS, LANES), BF),
             pltpu.VMEM((D, D), F32),
             pltpu.VMEM((2, D), F32),
-            pltpu.VMEM((TILE, LANES), F32),
-            pltpu.VMEM((ROWS, LANES), F32),
-            pltpu.VMEM((ROWS, LANES), F32),
+            pltpu.VMEM((GROUP, LANES, TILE), F32),
+            pltpu.VMEM((PAIRS, LANES, ROWS), BF),
+            pltpu.VMEM((GROUP, ROWS, LANES), F32),
+            pltpu.VMEM((GROUP, ROWS, LANES), F32),
             pltpu.SMEM((LEN_BLK,), jnp.int32),
             pltpu.SemaphoreType.DMA((LEN_BLK,)),
             pltpu.SemaphoreType.DMA((LEN_BLK,)),
-        ],
+            pltpu.SemaphoreType.DMA((9,)),
+            pltpu.VMEM((PAIRS, ROWS, LANES), BF),
+        ]
+        + saved_shapes(pltpu.VMEM)
+        + [pltpu.VMEM((D, 4 * D), BF)],
         compiler_params=params(),
         name="backward_layer",
-    )(
-        lens, own, got_rows, got_grads, *saved, w_proj, w_out, gain_in, gain_attn
-    )
+    )(lens, own, got_rows, got_grads, *saved, w_proj, w_out, gain_in, gain_attn)
 
 
 def per_device(events, cotangent, lengths, gain_in, w_proj, gain_attn, w_out):

time: 215 us -> 187 us (0.87)
  starting transfers between devices: 42.2 us -> 17.3 us
  Pallas kernels: 72.9 us -> 69.5 us
    ppermute x1, starting transfers between devices: 25.2 us -> 0.09 us  [per_device(): other = lax.ppermute(terms[1], 'core', swap)]
    pallas_call x1, Pallas kernels: 24.7 us -> 18.6 us  [forward_layer(): pl.pallas_call(forward_kernel, out_shape=[struct((PAIRS, ROWS, LANES), BF...]
    pallas_call x1, Pallas kernels: 36.7 us -> 39.8 us  [backward_layer(): pl.pallas_call(backward_kernel, out_shape=(struct((PEERS, BLOCK, D), BF),...]
  transfers between devices with their start and end apart: 4 -> 4, of which waited for: 2 -> 2; matrix products, arithmetic and copies ran while one was open for 0% -> 0% of each run, Pallas kernels for 14% -> 12%
where the time goes in v3:
time: 187 us; the launch traced here: 186 us
  blocking collectives  74.9 us (40%)
  Pallas kernels  69.5 us (37%)
  waiting for transfers between devices  18.2 us (10%)
  starting transfers between devices  17.3 us (9%)
  local copies, waits for them, and re-layouts  4.97 us (3%)
    pallas_call x1, Pallas kernels, backward_layer(): pl.pallas_call(backward_kernel, out_shape=(struct((PEERS, BLOCK, D), BF),...  39.8 us
    all_to_all x1, blocking collectives, per_device(): lax.all_to_all(chip_sum.reshape(64, PART, LANES), ('grp', 'chip'), 0, 0,...  29.5 us
    all_to_all x1, blocking collectives, per_device(): lax.all_to_all(copies, ('grp', 'chip'), 0, 0, tiled=True)  25.3 us
    all_to_all x1, blocking collectives, per_device(): came_back = lax.all_to_all(send_back, ('chip', 'core'), 0, 0, tiled=True)  20.1 us
    pallas_call x1, Pallas kernels, forward_layer(): pl.pallas_call(forward_kernel, out_shape=[struct((PAIRS, ROWS, LANES), BF...  18.6 us
    all_to_all x1, waiting for transfers between devices, per_device(): lax.all_to_all(send_blocks(lens, own, events), ('chip', 'core'), 0, 0, ti...  15 us
    all_to_all x1, starting transfers between devices, per_device(): lax.all_to_all(send_blocks(lens, own, events), ('chip', 'core'), 0, 0, ti...  9.29 us
    pallas_call x2, Pallas kernels, send_blocks(): pl.pallas_call(send_kernel, out_shape=struct((PEERS, BLOCK, D), BF), in_s...  4.49 us
  transfers between devices with their start and end apart: 4, of which 2 were waited for; matrix products, arithmetic and copies ran while one was open for 0% of the time, Pallas kernels for 12%

profile of v3, /device:TPU:1, one launch (start us, length us, event | category | flops | bytes accessed | tf_op | source)
XLA Modules:
  0.0 186.2 jit_solution(4592145028209699972)
XLA Ops:
  0.6 2.2 %send_blocks.2 = bf16[16,64,512]{2,1,0:T(8,128)(2,1)} custom-call(s32[16]{0:T(128)} %bitcast.18, s32[1]{0:T(128)} %bitcast.1.own_ref, bf16[8,64,512]{2,1,0:T(8,128)(2,1)} %bitcast.27), custom_call_target="tpu_custom_call" | custom-call | tf_op jit(solution)/shard_map/send_blocks/pallas_call | solution.py:574
  2.9 9.3 %all-to-all-start = ((bf16[16,64,512]{2,1,0:T(8,128)(2,1)}), bf16[16,64,512]{2,1,0:T(8,128)(2,1)S(1)}, u32[]{:S(2)}, u32[]{:S(2)}) async-start(bf16[16,64,512]{2,1,0:T(8,128)(2,1)} %send_blocks.2), calls=%async_computation | async-start | bytes 2097152 | tf_op jit(solution)/shard_map/all_to_all | solution.py:641
  12.2 2.3 %send_blocks.3 = bf16[16,64,512]{2,1,0:T(8,128)(2,1)} custom-call(s32[16]{0:T(128)} %bitcast.19, s32[1]{0:T(128)} %bitcast.1.own_ref, bf16[8,64,512]{2,1,0:T(8,128)(2,1)} %bitcast.28), custom_call_target="tpu_custom_call" | custom-call | tf_op jit(solution)/shard_map/send_blocks/pallas_call | solution.py:574
  14.4 0.0 copy-start.2
  14.4 0.0 copy-start.3
  14.4 15.0 %all-to-all-done.got_ref = bf16[16,64,512]{2,1,0:T(8,128)(2,1)S(1)} async-done(((bf16[16,64,512]{2,1,0:T(8,128)(2,1)}), bf16[16,64,512]{2,1,0:T(8,128)(2,1)S(1)}, u32[]{:S(2)}, u32[]{:S(2)}) %all-to-all-start) | async-done | bytes 1048608 | tf_op jit(solution)/shard_map/all_to_all | solution.py:641
  29.4 0.0 copy-start.5
  29.4 4.4 %all-to-all-start.1 = ((bf16[16,64,512]{2,1,0:T(8,128)(2,1)}), bf16[16,64,512]{2,1,0:T(8,128)(2,1)S(1)}, u32[]{:S(2)}, u32[]{:S(2)}) async-start(bf16[16,64,512]{2,1,0:T(8,128)(2,1)} %send_blocks.3), calls=%async_computation.1 | async-start | bytes 2097152 | tf_op jit(solution)/shard_map/all_to_all | solution.py:642
  33.7 0.0 copy-done.5
  33.7 0.0 copy-done.2
  33.8 0.0 copy-done.3
  33.8 0.0 copy-start.1
  33.8 0.0 copy-start.4
  33.8 18.6 %forward_layer.1 = (bf16[4,1024,128]{2,1,0:T(8,128)(2,1)S(1)}, bf16[1024,512]{1,0:T(8,128)(2,1)}, bf16[4,1024,128]{2,1,0:T(8,128)(2,1)}, bf16[4,1024,128]{2,1,0:...) custom-call(s32[16]{0:T(128)S(1)} %bitcast.21, ...), custom_call_target="tpu_custom_call" | custom-call | tf_op jit(solution)/shard_map/forward_layer/pallas_call | solution.py:590
  52.4 0.0 copy-start
  52.4 1.1 copy-done
  53.4 0.0 all-to-all-done.1.grads_ref
  53.4 0.0 copy-start.6
  53.4 1.0 copy-done.6
  54.4 0.0 copy-done.1
  54.4 0.0 copy-done.4
  54.4 39.8 %backward_layer.1 = (bf16[16,64,512]{2,1,0:T(8,128)(2,1)S(1)}, bf16[2,5632,128]{2,1,0:T(8,128)(2,1)}) custom-call(s32[16]{0:T(128)S(1)} %bitcast.22, s32[1]{0:T(128)} %bitcast.1.own_ref, bf16[16,64,512]{2,1,0:T(8,128)(2,1)} %copy-done.5, bf16[16,64,512]{2,1,0:T(8,128)(2,1)} %copy-done.6, bf16[4,1024,128]{2,1,0:T(8,128)(2,1)} %copy-done, ...), custom_call_target="tpu_custom_call" | custom-call | tf_op jit(solution)/shard_map/backward_layer/pallas_call | solution.py:609
  94.2 0.0 copy-start.7
  94.2 1.6 slice_bitcast_fusion
  95.9 0.1 collective-permute-start
  96.0 3.2 %collective-permute-done = bf16[5632,128]{1,0:T(8,128)(2,1)S(1)} collective-permute-done((bf16[5632,128]{1,0:T(8,128)(2,1)S(1)}, bf16[5632,128]{1,0:T(8,128)(2,1)S(1)}, u32[]{:S(2)}, u32[]{:S(2)}) %collective-permute-start) | collective-permute-done | bytes 1441824 | tf_op jit(solution)/shard_map/ppermute | solution.py:649
  99.2 0.0 copy-done.7
  99.2 0.4 fusion
  99.5 29.5 %all_to_all.25 = bf16[64,88,128]{2,1,0:T(8,128)(2,1)S(1)} all-to-all(bf16[64,88,128]{2,1,0:T(8,128)(2,1)S(1)} %bitcast.26), channel_id=1, replica_groups=mesh['grp'=8,'chip'=8,'core'=2] {'grp','chip'}, dimensions={0} | all-to-all | bytes 2883584 | tf_op jit(solution)/shard_map/all_to_all | solution.py:651
  129.1 0.2 convert_reduce_fusion
  129.3 0.2 broadcast_in_dim.2
  129.5 25.3 %all_to_all.26 = bf16[64,88,128]{2,1,0:T(8,128)(2,1)S(1)} all-to-all(bf16[64,88,128]{2,1,0:T(8,128)(2,1)S(1)} %broadcast_in_dim.2), channel_id=1, replica_groups=mesh['grp'=8,'chip'=8,'core'=2] {'grp','chip'}, dimensions={0} | all-to-all | bytes 2883584 | tf_op jit(solution)/shard_map/all_to_all | solution.py:654
  154.8 3.6 %collective-permute-start.1 = (bf16[5632,128]{1,0:T(8,128)(2,1)S(1)}, bf16[5632,128]{1,0:T(8,128)(2,1)S(1)}, u32[]{:S(2)}, u32[]{:S(2)}) collective-permute-start(bf16[5632,128]{1,0:T(8,128)(2,1)S(1)} %bitcast.16), channel_id=1, source_target_pairs={{0,1},{1,0},{2,3},{3,2},{4,5},{5,4},{6,7},{7,6},{8,9},{9,8},{10,11... | collective-permute-start | bytes 4325384 | tf_op jit(solution)/shard_map/ppermute | solution.py:655
  158.4 20.1 %all_to_all.27.back_ref = bf16[16,64,512]{2,1,0:T(8,128)(2,1)} all-to-all(bf16[16,64,512]{2,1,0:T(8,128)(2,1)S(1)} %get-tuple-element.25), channel_id=1, replica_groups=mesh['grp'=8,'chip'=8,'core'=2] {'chip','core'}, dimensions={0} | all-to-all | bytes 2097152 | tf_op jit(solution)/shard_map/all_to_all | solution.py:656
  178.5 2.2 %take_home.1 = bf16[8,64,512]{2,1,0:T(8,128)(2,1)} custom-call(s32[16]{0:T(128)} %bitcast.20, s32[1]{0:T(128)} %bitcast.1.own_ref, bf16[16,64,512]{2,1,0:T(8,128)(2,1)} %all_to_all.27.back_ref), custom_call_target="tpu_custom_call" | custom-call | tf_op jit(solution)/shard_map/take_home/pallas_call | solution.py:657
  180.7 0.0 collective-permute-done.1.other_ref
  180.7 0.0 copy-start.8
  180.7 1.1 copy-done.8
  181.8 4.4 %spread_grads.1 = (f32[512,2048]{1,0:T(8,128)}, f32[512,512]{1,0:T(8,128)}, f32[4,128]{1,0:T(4,128)}, f32[4,128]{1,0:T(4,128)}) custom-call(s32[1]{0:T(128)} %bitcast.1.own_ref, bf16[5632,128]{1,0:T(8,128)(2,1)S(1)} %bitcast.17, bf16[5632,128]{1,0:T(8,128)(2,1)} %copy-done.8), custom_call_target="tpu_custom_call" | custom-call | tf_op jit(solution)/shard_map/spread_grads/pallas_call | solution.py:665
  (1 shorter events, 0.0 us)
Async XLA Ops:
  2.9 26.5 %all-to-all-start = ((bf16[16,64,512]{2,1,0:T(8,128)(2,1)}), bf16[16,64,512]{2,1,0:T(8,128)(2,1)S(1)}, u32[]{:S(2)}, u32[]{:S(2)}) async-start(bf16[16,64,512]{2,1,0:T(8,128)(2,1)} %send_blocks.2), calls=%async_computation | async-start | bytes 2097152 | tf_op jit(solution)/shard_map/all_to_all | solution.py:641
  14.4 19.3 %copy-start.2 = (s32[1,16]{1,0:T(1,128)S(1)}, s32[1,16]{1,0:T(1,128)}, u32[]{:S(2)}) copy-start(s32[1,16]{1,0:T(1,128)} %param.9) | copy-start | bytes 196
  14.4 19.3 %copy-start.3 = (f32[512]{0:T(512)S(1)}, f32[512]{0:T(512)}, u32[]{:S(2)}) copy-start(f32[512]{0:T(512)} %param.10) | copy-start | bytes 6148
  29.4 4.4 %copy-start.5 = (bf16[16,64,512]{2,1,0:T(8,128)(2,1)}, bf16[16,64,512]{2,1,0:T(8,128)(2,1)S(1)}, u32[]{:S(2)}) copy-start(bf16[16,64,512]{2,1,0:T(8,128)(2,1)S(1)} %all-to-all-done.got_ref) | copy-start | bytes 3145732
  29.4 24.0 %all-to-all-start.1 = ((bf16[16,64,512]{2,1,0:T(8,128)(2,1)}), bf16[16,64,512]{2,1,0:T(8,128)(2,1)S(1)}, u32[]{:S(2)}, u32[]{:S(2)}) async-start(bf16[16,64,512]{2,1,0:T(8,128)(2,1)} %send_blocks.3), calls=%async_computation.1 | async-start | bytes 2097152 | tf_op jit(solution)/shard_map/all_to_all | solution.py:642
  33.8 20.6 %copy-start.1 = (bf16[512,512]{1,0:T(8,128)(2,1)S(1)}, bf16[512,512]{1,0:T(8,128)(2,1)}, u32[]{:S(2)}) copy-start(bf16[512,512]{1,0:T(8,128)(2,1)} %w_out_ref.1) | copy-start | bytes 1572868
  33.8 20.6 %copy-start.4 = (f32[512]{0:T(512)S(1)}, f32[512]{0:T(512)}, u32[]{:S(2)}) copy-start(f32[512]{0:T(512)} %param.12) | copy-start | bytes 6148
  52.4 1.1 copy-start
  53.4 1.0 copy-start.6
  94.2 4.9 %copy-start.7 = (bf16[2,5632,128]{2,1,0:T(8,128)(2,1)S(1)}, bf16[2,5632,128]{2,1,0:T(8,128)(2,1)}, u32[]{:S(2)}) copy-start(bf16[2,5632,128]{2,1,0:T(8,128)(2,1)} %get-tuple-element.26) | copy-start | bytes 8650756
  95.9 3.3 %collective-permute-start = (bf16[5632,128]{1,0:T(8,128)(2,1)S(1)}, bf16[5632,128]{1,0:T(8,128)(2,1)S(1)}, u32[]{:S(2)}, u32[]{:S(2)}) collective-permute-start(bf16[5632,128]{1,0:T(8,128)(2,1)S(1)} %slice_bitcast_fusion), channel_id=1, source_target_pairs={{0,1},{1,0},{2,3},{3,2},{4,5},{5,4},{6,7},{7,6},{8,9},{9,8},{10,11... | collective-permute-start | bytes 4325384 | tf_op jit(solution)/shard_map/ppermute | solution.py:649
  154.8 25.9 %collective-permute-start.1 = (bf16[5632,128]{1,0:T(8,128)(2,1)S(1)}, bf16[5632,128]{1,0:T(8,128)(2,1)S(1)}, u32[]{:S(2)}, u32[]{:S(2)}) collective-permute-start(bf16[5632,128]{1,0:T(8,128)(2,1)S(1)} %bitcast.16), channel_id=1, source_target_pairs={{0,1},{1,0},{2,3},{3,2},{4,5},{5,4},{6,7},{7,6},{8,9},{9,8},{10,11... | collective-permute-start | bytes 4325384 | tf_op jit(solution)/shard_map/ppermute | solution.py:655
  180.7 1.1 copy-start.8

commit v4 on v3

--- a/solution.py
+++ b/solution.py
@@ -23,11 +23,12 @@
 DEVICES = 128
 BF = jnp.bfloat16
 F32 = jnp.float32
-VMEM_LIMIT = 52 * 1024 * 1024
+MIB = 1024 * 1024
 
 SMEM_SPEC = pl.BlockSpec(memory_space=pltpu.SMEM)
 ANY_SPEC = pl.BlockSpec(memory_space=pl.ANY)
 VMEM_SPEC = pl.BlockSpec(memory_space=pltpu.VMEM)
+HBM_SPEC = pl.BlockSpec(memory_space=pltpu.HBM)
 
 
 def dot(left, right):
@@ -203,7 +204,7 @@
         normed, _ = normed_rows(tile_rows(rows_ref, t, count))
         scaled = (normed * gain_ref[...]).astype(BF)
         rows = rows_at(t)
-        scaled_ref[rows, :] = scaled
+        scaled_ref[:, rows] = scaled.T
         for quarter in range(4):
             half = 0.5 * dot(scaled, w_ref[:, quarter * D : (quarter + 1) * D])
             swing = jnp.tanh(half)
@@ -225,7 +226,7 @@
     lax.fori_loop(0, live, project, 0)
 
     def clear(t, carry):
-        scaled_ref[rows_at(t), :] = jnp.zeros((TILE, D), BF)
+        scaled_ref[:, rows_at(t)] = jnp.zeros((D, TILE), BF)
         return carry
 
     lax.fori_loop(live, TILES, clear, 0)
@@ -307,19 +308,19 @@
     query_in,
     keys_in,
     slope_in,
-    scaled_in,
     w_in,
     w_out_ref,
     gain_in_ref,
     gain_attn_ref,
     back_ref,
-    terms_ref,
+    d_hidden_out,
+    out_terms_ref,
+    gains_ref,
     rows_ref,
     cot_ref,
     d_attn_ref,
     d_hidden_ref,
     out_ref,
-    gains_ref,
     d_query_ref,
     keys_t_ref,
     d_keys_ref,
@@ -334,11 +335,9 @@
     query_ref,
     keys_ref,
     slope_ref,
-    scaled_ref,
     w_ref,
 ):
     own = own_ref[0]
-    core = own & 1
     starts, sizes, ranks, first, count = holdings(len_ref, own)
     fetch(grads_ref, cot_ref, cot_sems, first, count)
     early = pl.ds(0, PAIRS)
@@ -355,7 +354,6 @@
                 (values_in, values_ref),
                 (slope_in.at[late], slope_ref.at[late]),
                 (w_in, w_ref),
-                (scaled_in, scaled_ref),
             )
         )
     ]
@@ -492,6 +490,8 @@
 
     lax.fori_loop(0, PAIRS // GROUP, group, 0)
 
+    save = pltpu.make_async_copy(d_hidden_ref, d_hidden_out, load_sems.at[8])
+    save.start()
     arrive(got_ref, rows_ref, row_sems, count)
     for load in loads[7:]:
         load.wait()
@@ -520,23 +520,64 @@
 
     lax.fori_loop(0, live, final, 0)
 
-    def put(piece, values):
+    for p in range(PAIRS):
+        out_terms_ref[p] = out_ref[:, p * LANES : (p + 1) * LANES].astype(BF)
+    save.wait()
+
+
+def terms_kernel(
+    own_ref,
+    d_hidden_in,
+    scaled_in,
+    out_terms_ref,
+    gains_ref,
+    keep_ref,
+    send_ref,
+    d_hidden_ref,
+    scaled_ref,
+    sems,
+):
+    core = own_ref[0] & 1
+    loads = [pltpu.make_async_copy(scaled_in, scaled_ref, sems.at[8])]
+    for c in range(8):
+        part = pl.ds(2 * c, 2)
+        loads.append(
+            pltpu.make_async_copy(d_hidden_in.at[part], d_hidden_ref.at[part], sems.at[c])
+        )
+    for load in loads:
+        load.start()
+
+    def put(half, rows, values):
+        values = values.astype(BF)
+
+        @pl.when(core == half)
+        def _():
+            keep_ref[rows, :] = values
+
+        @pl.when(core != half)
+        def _():
+            send_ref[rows, :] = values
+
+    def put_piece(piece, values):
         half, place = divmod(piece, 10)
-        terms_ref[half ^ core, place * D : (place + 1) * D, :] = values.astype(BF)
-
-    for c in range(8):
-        part = jnp.concatenate([d_hidden_ref[2 * c], d_hidden_ref[2 * c + 1]], axis=1)
-        term = dot_rows(scaled_ref[...], part)
-        put(2 * c, term[:, :LANES])
-        put(2 * c + 1, term[:, LANES:])
+        put(half, pl.ds(place * D, D), values)
+
     for p in range(PAIRS):
-        put(16 + p, out_ref[:, p * LANES : (p + 1) * LANES])
+        put_piece(16 + p, out_terms_ref[p])
     for half in range(2):
-        terms_ref[half ^ core, 10 * D :, :] = jnp.concatenate(
+        tail = jnp.concatenate(
             [gains_ref[half : half + 1, p * LANES : (p + 1) * LANES] for p in range(PAIRS)]
             + [jnp.zeros((HALF - 10 * D - PAIRS, LANES), F32)],
             axis=0,
-        ).astype(BF)
+        )
+        put(half, pl.ds(10 * D, HALF - 10 * D), tail)
+    loads[0].wait()
+    for c in range(8):
+        loads[1 + c].wait()
+        part = jnp.concatenate([d_hidden_ref[2 * c], d_hidden_ref[2 * c + 1]], axis=1)
+        term = dot(scaled_ref[...], part)
+        put_piece(2 * c, term[:, :LANES])
+        put_piece(2 * c + 1, term[:, LANES:])
 
 
 def spread_kernel(own_ref, mine_ref, other_ref, proj_ref, out_ref, gain_in_ref, gain_attn_ref):
@@ -566,8 +607,8 @@
     return jax.ShapeDtypeStruct(shape, dtype)
 
 
-def params():
-    return pltpu.CompilerParams(vmem_limit_bytes=VMEM_LIMIT)
+def params(mebibytes):
+    return pltpu.CompilerParams(vmem_limit_bytes=mebibytes * MIB)
 
 
 def send_blocks(lens, own, rows):
@@ -583,7 +624,8 @@
 def saved_shapes(make):
     pairs = make((PAIRS, ROWS, LANES), BF)
     wide = make((ROWS, D), BF)
-    return [wide, pairs, pairs, pairs, make((4 * PAIRS, ROWS, LANES), BF), wide]
+    tall = make((D, ROWS), BF)
+    return [wide, pairs, pairs, pairs, make((4 * PAIRS, ROWS, LANES), BF), tall]
 
 
 def forward_layer(lens, own, got_rows, w_proj, gain_in):
@@ -591,7 +633,7 @@
         forward_kernel,
         out_shape=[struct((PAIRS, ROWS, LANES), BF)] + saved_shapes(struct),
         in_specs=[SMEM_SPEC, SMEM_SPEC, ANY_SPEC, VMEM_SPEC, VMEM_SPEC],
-        out_specs=[VMEM_SPEC] + [ANY_SPEC] * 6,
+        out_specs=[VMEM_SPEC] + [HBM_SPEC] * 6,
         scratch_shapes=saved_shapes(pltpu.VMEM)
         + [
             pltpu.VMEM((LEN_BLK, BLOCK, D), BF),
@@ -600,7 +642,7 @@
             pltpu.SemaphoreType.DMA((LEN_BLK,)),
             pltpu.SemaphoreType.DMA((6,)),
         ],
-        compiler_params=params(),
+        compiler_params=params(52),
         name="forward_layer",
     )(lens, own, got_rows, w_proj, gain_in)
 
@@ -608,16 +650,20 @@
 def backward_layer(lens, own, got_rows, got_grads, saved, w_proj, w_out, gain_in, gain_attn):
     return pl.pallas_call(
         backward_kernel,
-        out_shape=(struct((PEERS, BLOCK, D), BF), struct((2, HALF, LANES), BF)),
-        in_specs=[SMEM_SPEC, SMEM_SPEC] + [ANY_SPEC] * 10 + [VMEM_SPEC] * 3,
-        out_specs=(VMEM_SPEC, VMEM_SPEC),
+        out_shape=(
+            struct((PEERS, BLOCK, D), BF),
+            struct((4 * PAIRS, ROWS, LANES), BF),
+            struct((PAIRS, D, LANES), BF),
+            struct((2, D), F32),
+        ),
+        in_specs=[SMEM_SPEC, SMEM_SPEC] + [ANY_SPEC] * 3 + [HBM_SPEC] * 6 + [VMEM_SPEC] * 3,
+        out_specs=(VMEM_SPEC, HBM_SPEC, VMEM_SPEC, VMEM_SPEC),
         scratch_shapes=[
             pltpu.VMEM((LEN_BLK, BLOCK, D), BF),
             pltpu.VMEM((LEN_BLK, BLOCK, D), BF),
             pltpu.VMEM((PAIRS, ROWS, LANES), BF),
             pltpu.VMEM((4 * PAIRS, ROWS, LANES), BF),
             pltpu.VMEM((D, D), F32),
-            pltpu.VMEM((2, D), F32),
             pltpu.VMEM((GROUP, LANES, TILE), F32),
             pltpu.VMEM((PAIRS, LANES, ROWS), BF),
             pltpu.VMEM((GROUP, ROWS, LANES), F32),
@@ -628,11 +674,31 @@
             pltpu.SemaphoreType.DMA((9,)),
             pltpu.VMEM((PAIRS, ROWS, LANES), BF),
         ]
-        + saved_shapes(pltpu.VMEM)
+        + saved_shapes(pltpu.VMEM)[:5]
         + [pltpu.VMEM((D, 4 * D), BF)],
-        compiler_params=params(),
+        compiler_params=params(52),
         name="backward_layer",
-    )(lens, own, got_rows, got_grads, *saved, w_proj, w_out, gain_in, gain_attn)
+    )(lens, own, got_rows, got_grads, *saved[:6], w_proj, w_out, gain_in, gain_attn)
+
+
+def gradient_terms(own, d_hidden, scaled, out_terms, gains):
+    half = struct((HALF, LANES), BF)
+    return pl.pallas_call(
+        terms_kernel,
+        out_shape=(half, half),
+        in_specs=[SMEM_SPEC, HBM_SPEC, HBM_SPEC, VMEM_SPEC, VMEM_SPEC],
+        out_specs=(VMEM_SPEC, VMEM_SPEC),
+        scratch_shapes=[
+            pltpu.VMEM((4 * PAIRS, ROWS, LANES), BF),
+            pltpu.VMEM((D, ROWS), BF),
+            pltpu.SemaphoreType.DMA((9,)),
+        ],
+        compiler_params=params(52),
+        cost_estimate=pl.CostEstimate(
+            flops=8 * ROWS * D * D, transcendentals=0, bytes_accessed=8 * MIB
+        ),
+        name="gradient_terms",
+    )(own, d_hidden, scaled, out_terms, gains)
 
 
 def per_device(events, cotangent, lengths, gain_in, w_proj, gain_attn, w_out):
@@ -642,18 +708,20 @@
     got_grads = lax.all_to_all(send_blocks(lens, own, cotangent), ("chip", "core"), 0, 0, tiled=True)
     gain_in = gain_in.reshape(1, D)
     saved = forward_layer(lens, own, got_rows, w_proj, gain_in)
-    send_back, terms = backward_layer(
+    send_back, d_hidden, out_terms, gains = backward_layer(
         lens, own, got_rows, got_grads, saved, w_proj, w_out, gain_in, gain_attn.reshape(1, D)
     )
+    came_back = lax.all_to_all(send_back, ("chip", "core"), 0, 0, tiled=True)
+    keep, send = gradient_terms(own, d_hidden, saved[6], out_terms, gains)
+    send, came_back = lax.optimization_barrier((send, came_back))
     swap = [(0, 1), (1, 0)]
-    other = lax.ppermute(terms[1], "core", swap)
-    chip_sum = (terms[0].astype(F32) + other.astype(F32)).astype(BF)
+    other = lax.ppermute(send, "core", swap)
+    chip_sum = (keep.astype(F32) + other.astype(F32)).astype(BF)
     parts = lax.all_to_all(chip_sum.reshape(64, PART, LANES), ("grp", "chip"), 0, 0, tiled=True)
     total = (jnp.sum(parts.astype(F32), axis=0) * (1.0 / DEVICES)).astype(BF)
     copies = jnp.broadcast_to(total[None], (64, PART, LANES))
     mine = lax.all_to_all(copies, ("grp", "chip"), 0, 0, tiled=True).reshape(HALF, LANES)
     others = lax.ppermute(mine, "core", swap)
-    came_back = lax.all_to_all(send_back, ("chip", "core"), 0, 0, tiled=True)
     d_rows = pl.pallas_call(
         home_kernel,
         out_shape=struct((LOCAL, BLOCK, D), BF),
@@ -667,7 +735,7 @@
         out_shape=(struct((D, 4 * D), F32), struct((D, D), F32), gain, gain),
         in_specs=[SMEM_SPEC, VMEM_SPEC, VMEM_SPEC],
         out_specs=(VMEM_SPEC,) * 4,
-        compiler_params=params(),
+        compiler_params=params(16),
         name="spread_grads",
     )(own, mine, others)
     return (

time: 187 us -> 182 us (0.973)
  blocking collectives: 74.9 us -> 54.3 us
  starting transfers between devices: 17.3 us -> 32.7 us
  waiting for transfers between devices: 18.2 us -> 27.8 us
  Pallas kernels: 69.5 us -> 61.9 us
  local copies, waits for them, and re-layouts: 4.97 us -> 2.19 us
    all_to_all x1 -> x0, blocking collectives: 20.1 us -> none  [per_device(): came_back = lax.all_to_all(send_back, ('chip', 'core'), 0, 0, tiled=True)]
    all_to_all x0 -> x1, starting transfers between devices: none -> 14.8 us  [per_device(): came_back = lax.all_to_all(send_back, ('chip', 'core'), 0, 0, tiled=True)]
    pallas_call x1, Pallas kernels: 39.8 us -> 27.8 us  [backward_layer(): pl.pallas_call(backward_kernel, out_shape=(struct((PEERS, BLOCK, D), BF),...]
    all_to_all x0 -> x1, waiting for transfers between devices: none -> 8.68 us  [per_device(): came_back = lax.all_to_all(send_back, ('chip', 'core'), 0, 0, tiled=True)]
    pallas_call x0 -> x1, Pallas kernels: none -> 8.52 us  [gradient_terms(): pl.pallas_call(terms_kernel, out_shape=(half, half), in_specs=[SMEM_SPEC,...]
    pallas_call x1, Pallas kernels: 18.6 us -> 15.8 us  [forward_layer(): pl.pallas_call(forward_kernel, out_shape=[struct((PAIRS, ROWS, LANES), BF...]
  transfers between devices with their start and end apart: 4 -> 5, of which waited for: 2 -> 5; matrix products, arithmetic and copies ran while one was open for 0% -> 0% of each run, Pallas kernels for 12% -> 16%
where the time goes in v4:
time: 182 us
  Pallas kernels  61.9 us (34%)
  blocking collectives  54.3 us (30%)
  starting transfers between devices  32.7 us (18%)
  waiting for transfers between devices  27.8 us (15%)
  local copies, waits for them, and re-layouts  2.19 us (1%)
  other arithmetic  1.97 us (1%)
    all_to_all x1, blocking collectives, per_device(): lax.all_to_all(chip_sum.reshape(64, PART, LANES), ('grp', 'chip'), 0, 0,...  29.1 us
    pallas_call x1, Pallas kernels, backward_layer(): pl.pallas_call(backward_kernel, out_shape=(struct((PEERS, BLOCK, D), BF),...  27.8 us
    all_to_all x1, blocking collectives, per_device(): lax.all_to_all(copies, ('grp', 'chip'), 0, 0, tiled=True)  25.2 us
    pallas_call x1, Pallas kernels, forward_layer(): pl.pallas_call(forward_kernel, out_shape=[struct((PAIRS, ROWS, LANES), BF...  15.8 us
    all_to_all x1, waiting for transfers between devices, per_device(): lax.all_to_all(send_blocks(lens, own, events), ('chip', 'core'), 0, 0, ti...  14.9 us
    all_to_all x1, starting transfers between devices, per_device(): came_back = lax.all_to_all(send_back, ('chip', 'core'), 0, 0, tiled=True)  14.8 us
    all_to_all x1, starting transfers between devices, per_device(): lax.all_to_all(send_blocks(lens, own, events), ('chip', 'core'), 0, 0, ti...  9.29 us
    all_to_all x1, waiting for transfers between devices, per_device(): came_back = lax.all_to_all(send_back, ('chip', 'core'), 0, 0, tiled=True)  8.68 us
  transfers between devices with their start and end apart: 5, of which 5 were waited for; matrix products, arithmetic and copies ran while one was open for 0% of the time, Pallas kernels for 16%

profile of v4, /device:TPU:1, one launch (start us, length us, event | category | flops | bytes accessed | tf_op | source)
XLA Modules:
  0.0 181.6 jit_solution(7682211245107314386)
XLA Ops:
  0.6 2.2 %send_blocks.2 = bf16[16,64,512]{2,1,0:T(8,128)(2,1)} custom-call(s32[16]{0:T(128)} %bitcast.13, s32[1]{0:T(128)} %bitcast.1.own_ref, bf16[8,64,512]{2,1,0:T(8,128)(2,1)} %bitcast.22), custom_call_target="tpu_custom_call" | custom-call | tf_op jit(solution)/shard_map/send_blocks/pallas_call | solution.py:615
  2.9 9.3 %all-to-all-start = ((bf16[16,64,512]{2,1,0:T(8,128)(2,1)}), bf16[16,64,512]{2,1,0:T(8,128)(2,1)S(1)}, u32[]{:S(2)}, u32[]{:S(2)}) async-start(bf16[16,64,512]{2,1,0:T(8,128)(2,1)} %send_blocks.2), calls=%async_computation | async-start | bytes 2097152 | tf_op jit(solution)/shard_map/all_to_all | solution.py:707
  12.2 2.3 %send_blocks.3 = bf16[16,64,512]{2,1,0:T(8,128)(2,1)} custom-call(s32[16]{0:T(128)} %bitcast.14, s32[1]{0:T(128)} %bitcast.1.own_ref, bf16[8,64,512]{2,1,0:T(8,128)(2,1)} %bitcast.23), custom_call_target="tpu_custom_call" | custom-call | tf_op jit(solution)/shard_map/send_blocks/pallas_call | solution.py:615
  14.4 0.0 copy-start.2
  14.4 0.0 copy-start.3
  14.4 14.9 %all-to-all-done.got_ref = bf16[16,64,512]{2,1,0:T(8,128)(2,1)S(1)} async-done(((bf16[16,64,512]{2,1,0:T(8,128)(2,1)}), bf16[16,64,512]{2,1,0:T(8,128)(2,1)S(1)}, u32[]{:S(2)}, u32[]{:S(2)}) %all-to-all-start) | async-done | bytes 1048608 | tf_op jit(solution)/shard_map/all_to_all | solution.py:707
  29.4 0.0 copy-start.6
  29.4 4.4 %all-to-all-start.1 = ((bf16[16,64,512]{2,1,0:T(8,128)(2,1)}), bf16[16,64,512]{2,1,0:T(8,128)(2,1)S(1)}, u32[]{:S(2)}, u32[]{:S(2)}) async-start(bf16[16,64,512]{2,1,0:T(8,128)(2,1)} %send_blocks.3), calls=%async_computation.1 | async-start | bytes 2097152 | tf_op jit(solution)/shard_map/all_to_all | solution.py:708
  33.7 0.0 copy-done.6
  33.7 0.0 copy-done.2
  33.8 0.0 copy-done.3
  33.8 0.0 copy-start.1
  33.8 0.0 copy-start.4
  33.8 15.8 %forward_layer.1 = (bf16[4,1024,128]{2,1,0:T(8,128)(2,1)S(1)}, bf16[1024,512]{1,0:T(8,128)(2,1)}, bf16[4,1024,128]{2,1,0:T(8,128)(2,1)}, bf16[4,1024,128]{2,1,0:...) custom-call(s32[16]{0:T(128)S(1)} %bitcast.16, ...), custom_call_target="tpu_custom_call" | custom-call | tf_op jit(solution)/shard_map/forward_layer/pallas_call | solution.py:632
  49.6 0.0 copy-start
  49.6 1.0 copy-done
  50.6 0.5 all-to-all-done.1.grads_ref
  51.0 0.0 copy-start.8
  51.0 1.0 copy-done.8
  52.0 0.0 copy-done.1
  52.0 0.0 copy-done.4
  52.0 27.8 %backward_layer.1 = (bf16[16,64,512]{2,1,0:T(8,128)(2,1)}, bf16[16,1024,128]{2,1,0:T(8,128)(2,1)}, bf16[4,512,128]{2,1,0:T(8,128)(2,1)S(1)}, f32[2,512]{1,0:T(2,128)S(1)}) custom-call(s32[16]{0:T(128)S(1)} %bitcast.17, s32[1]{0:T(128)} %bitcast.1.own_ref, bf16[16,64,512]{2,1,0:T(8,128)(2,1)} %copy-done.6, bf16[16,64,512]{2,1,0:T(8,128)(2,1)} %copy-done.8, ...), custom_call_target="tpu_custom_call" | custom-call | tf_op jit(solution)/shard_map/backward_layer/pallas_call | solution.py:651
  79.9 0.0 copy-start.5
  79.9 14.8 %all-to-all-start.2 = ((bf16[16,64,512]{2,1,0:T(8,128)(2,1)}), bf16[16,64,512]{2,1,0:T(8,128)(2,1)S(1)}, u32[]{:S(2)}, u32[]{:S(2)}) async-start(bf16[16,64,512]{2,1,0:T(8,128)(2,1)} %get-tuple-element.35), calls=%async_computation.2 | async-start | bytes 2097152 | tf_op jit(solution)/shard_map/all_to_all | solution.py:714
  94.7 0.0 copy-done.5
  94.7 8.5 %gradient_terms.1 = (bf16[5632,128]{1,0:T(8,128)(2,1)}, bf16[5632,128]{1,0:T(8,128)(2,1)}) custom-call(s32[1]{0:T(128)} %bitcast.1.own_ref, bf16[16,1024,128]{2,1,0:T(8,128)(2,1)} %get-tuple-element.30.d_hidden_in, bf16[512,1024]{1,0:T(8,128)(2,1)S(1)} %copy-done.5, bf16[4,512,128]{2,1,0:T(8,128)(2,1)S(1)} %get-tuple-element.32.out_terms_ref, ...), custom_call_target="tpu_custom_call" | custom-call | flops 2147483648 | bytes 8388608 | tf_op jit(solution)/shard_map/gradient_terms/pallas_call | solution.py:686
  103.2 8.7 %all-to-all-done.2.back_ref = bf16[16,64,512]{2,1,0:T(8,128)(2,1)S(1)} async-done(((bf16[16,64,512]{2,1,0:T(8,128)(2,1)}), bf16[16,64,512]{2,1,0:T(8,128)(2,1)S(1)}, u32[]{:S(2)}, u32[]{:S(2)}) %all-to-all-start.2) | async-done | bytes 1048608 | tf_op jit(solution)/shard_map/all_to_all | solution.py:714
  111.9 0.0 copy-start.7
  111.9 0.9 collective-permute-start
  112.8 3.1 %collective-permute-done = bf16[5632,128]{1,0:T(8,128)(2,1)S(1)} collective-permute-done((bf16[5632,128]{1,0:T(8,128)(2,1)}, bf16[5632,128]{1,0:T(8,128)(2,1)S(1)}, u32[]{:S(2)}, u32[]{:S(2)}) %collective-permute-start) | collective-permute-done | bytes 1441824 | tf_op jit(solution)/shard_map/ppermute | solution.py:718
  115.8 1.7 add_convert_fusion
  117.6 0.0 copy-done.7
  117.6 29.1 %all_to_all.25 = bf16[64,88,128]{2,1,0:T(8,128)(2,1)S(1)} all-to-all(bf16[64,88,128]{2,1,0:T(8,128)(2,1)S(1)} %bitcast.21), channel_id=1, replica_groups=mesh['grp'=8,'chip'=8,'core'=2] {'grp','chip'}, dimensions={0} | all-to-all | bytes 2883584 | tf_op jit(solution)/shard_map/all_to_all | solution.py:720
  146.7 0.2 convert_reduce_fusion
  147.0 0.2 broadcast_in_dim.2
  147.2 25.2 %all_to_all.26 = bf16[64,88,128]{2,1,0:T(8,128)(2,1)S(1)} all-to-all(bf16[64,88,128]{2,1,0:T(8,128)(2,1)S(1)} %broadcast_in_dim.2), channel_id=1, replica_groups=mesh['grp'=8,'chip'=8,'core'=2] {'grp','chip'}, dimensions={0} | all-to-all | bytes 2883584 | tf_op jit(solution)/shard_map/all_to_all | solution.py:723
  172.3 3.4 %collective-permute-start.1 = (bf16[5632,128]{1,0:T(8,128)(2,1)S(1)}, bf16[5632,128]{1,0:T(8,128)(2,1)S(1)}, u32[]{:S(2)}, u32[]{:S(2)}) collective-permute-start(bf16[5632,128]{1,0:T(8,128)(2,1)S(1)} %bitcast.11), channel_id=1, source_target_pairs={{0,1},{1,0},{2,3},{3,2},{4,5},{5,4},{6,7},{7,6},{8,9},{9,8},{10,11... | collective-permute-start | bytes 4325384 | tf_op jit(solution)/shard_map/ppermute | solution.py:724
  175.7 2.2 %take_home.1 = bf16[8,64,512]{2,1,0:T(8,128)(2,1)} custom-call(s32[16]{0:T(128)} %bitcast.15, s32[1]{0:T(128)} %bitcast.1.own_ref, bf16[16,64,512]{2,1,0:T(8,128)(2,1)} %copy-done.7), custom_call_target="tpu_custom_call" | custom-call | tf_op jit(solution)/shard_map/take_home/pallas_call | solution.py:725
  177.9 0.6 collective-permute-done.1.other_ref
  178.6 3.0 %spread_grads.1 = (f32[512,2048]{1,0:T(8,128)}, f32[512,512]{1,0:T(8,128)}, f32[4,128]{1,0:T(4,128)}, f32[4,128]{1,0:T(4,128)}) custom-call(s32[1]{0:T(128)} %bitcast.1.own_ref, bf16[5632,128]{1,0:T(8,128)(2,1)S(1)} %bitcast.12, bf16[5632,128]{1,0:T(8,128)(2,1)S(1)} %collective-permute-done.1.other_ref), custom_call_target="tpu_custom_call" | custom-call | tf_op jit(solution)/shard_map/spread_grads/pallas_call | solution.py:733
  (1 shorter events, 0.0 us)
Async XLA Ops:
  2.9 26.5 %all-to-all-start = ((bf16[16,64,512]{2,1,0:T(8,128)(2,1)}), bf16[16,64,512]{2,1,0:T(8,128)(2,1)S(1)}, u32[]{:S(2)}, u32[]{:S(2)}) async-start(bf16[16,64,512]{2,1,0:T(8,128)(2,1)} %send_blocks.2), calls=%async_computation | async-start | bytes 2097152 | tf_op jit(solution)/shard_map/all_to_all | solution.py:707
  14.4 19.3 %copy-start.2 = (s32[1,16]{1,0:T(1,128)S(1)}, s32[1,16]{1,0:T(1,128)}, u32[]{:S(2)}) copy-start(s32[1,16]{1,0:T(1,128)} %param.9) | copy-start | bytes 196
  14.4 19.3 %copy-start.3 = (f32[512]{0:T(512)S(1)}, f32[512]{0:T(512)}, u32[]{:S(2)}) copy-start(f32[512]{0:T(512)} %param.10) | copy-start | bytes 6148
  29.4 4.4 %copy-start.6 = (bf16[16,64,512]{2,1,0:T(8,128)(2,1)}, bf16[16,64,512]{2,1,0:T(8,128)(2,1)S(1)}, u32[]{:S(2)}) copy-start(bf16[16,64,512]{2,1,0:T(8,128)(2,1)S(1)} %all-to-all-done.got_ref) | copy-start | bytes 3145732
  29.4 21.6 %all-to-all-start.1 = ((bf16[16,64,512]{2,1,0:T(8,128)(2,1)}), bf16[16,64,512]{2,1,0:T(8,128)(2,1)S(1)}, u32[]{:S(2)}, u32[]{:S(2)}) async-start(bf16[16,64,512]{2,1,0:T(8,128)(2,1)} %send_blocks.3), calls=%async_computation.1 | async-start | bytes 2097152 | tf_op jit(solution)/shard_map/all_to_all | solution.py:708
  33.8 18.3 %copy-start.1 = (bf16[512,512]{1,0:T(8,128)(2,1)S(1)}, bf16[512,512]{1,0:T(8,128)(2,1)}, u32[]{:S(2)}) copy-start(bf16[512,512]{1,0:T(8,128)(2,1)} %w_out_ref.1) | copy-start | bytes 1572868
  33.8 18.3 %copy-start.4 = (f32[512]{0:T(512)S(1)}, f32[512]{0:T(512)}, u32[]{:S(2)}) copy-start(f32[512]{0:T(512)} %param.12) | copy-start | bytes 6148
  49.6 1.0 copy-start
  51.0 1.0 copy-start.8
  79.9 14.8 %copy-start.5 = (bf16[512,1024]{1,0:T(8,128)(2,1)S(1)}, bf16[512,1024]{1,0:T(8,128)(2,1)}, u32[]{:S(2)}) copy-start(bf16[512,1024]{1,0:T(8,128)(2,1)} %get-tuple-element.31.scaled_in) | copy-start | bytes 3145732
  79.9 32.0 %all-to-all-start.2 = ((bf16[16,64,512]{2,1,0:T(8,128)(2,1)}), bf16[16,64,512]{2,1,0:T(8,128)(2,1)S(1)}, u32[]{:S(2)}, u32[]{:S(2)}) async-start(bf16[16,64,512]{2,1,0:T(8,128)(2,1)} %get-tuple-element.35), calls=%async_computation.2 | async-start | bytes 2097152 | tf_op jit(solution)/shard_map/all_to_all | solution.py:714
  111.9 5.7 %copy-start.7 = (bf16[16,64,512]{2,1,0:T(8,128)(2,1)}, bf16[16,64,512]{2,1,0:T(8,128)(2,1)S(1)}, u32[]{:S(2)}) copy-start(bf16[16,64,512]{2,1,0:T(8,128)(2,1)S(1)} %all-to-all-done.2.back_ref) | copy-start | bytes 3145732
  111.9 4.0 %collective-permute-start = (bf16[5632,128]{1,0:T(8,128)(2,1)}, bf16[5632,128]{1,0:T(8,128)(2,1)S(1)}, u32[]{:S(2)}, u32[]{:S(2)}) collective-permute-start(bf16[5632,128]{1,0:T(8,128)(2,1)} %get-tuple-element.38), channel_id=1, source_target_pairs={{0,1},{1,0},{2,3},{3,2},{4,5},{5,4},{6,7},{7,6},{8,9},{9,8},{10,11... | collective-permute-start | bytes 4325384 | tf_op jit(solution)/shard_map/ppermute | solution.py:718
  172.3 6.2 %collective-permute-start.1 = (bf16[5632,128]{1,0:T(8,128)(2,1)S(1)}, bf16[5632,128]{1,0:T(8,128)(2,1)S(1)}, u32[]{:S(2)}, u32[]{:S(2)}) collective-permute-start(bf16[5632,128]{1,0:T(8,128)(2,1)S(1)} %bitcast.11), channel_id=1, source_target_pairs={{0,1},{1,0},{2,3},{3,2},{4,5},{5,4},{6,7},{7,6},{8,9},{9,8},{10,11... | collective-permute-start | bytes 4325384 | tf_op jit(solution)/shard_map/ppermute | solution.py:724

commit v5 on v4

--- a/solution.py
+++ b/solution.py
@@ -99,10 +99,19 @@
             lax.fori_loop(begin, begin + sizes[i], put, 0)
 
 
-def send_kernel(len_ref, own_ref, rows_ref, out_ref):
+def send_kernel(len_ref, own_ref, rows_ref, out_ref, held_ref, sems):
+    load = pltpu.make_async_copy(rows_ref, held_ref, sems.at[LOCAL])
+    load.start()
     owner = owners(len_ref, own_ref[0])
-    for k in range(LOCAL):
-        out_ref[owner[k]] = rows_ref[k]
+    copies = [
+        pltpu.make_async_copy(held_ref.at[k], out_ref.at[owner[k]], sems.at[k])
+        for k in range(LOCAL)
+    ]
+    load.wait()
+    for copy in copies:
+        copy.start()
+    for copy in copies:
+        copy.wait()
 
 
 def home_kernel(len_ref, own_ref, back_ref, out_ref):
@@ -314,13 +323,15 @@
     gain_attn_ref,
     back_ref,
     d_hidden_out,
-    out_terms_ref,
+    mixed_out,
+    cot_out,
     gains_ref,
     rows_ref,
     cot_ref,
     d_attn_ref,
     d_hidden_ref,
-    out_ref,
+    mixed_ref,
+    cot_rows_ref,
     d_query_ref,
     keys_t_ref,
     d_keys_ref,
@@ -362,7 +373,6 @@
     fetch(got_ref, rows_ref, row_sems, first, count)
     history_starts(hist_ref, own, starts, sizes, ranks, first)
     live = (count + 3) // 4
-    out_ref[...] = jnp.zeros((D, D), F32)
     gains_ref[...] = jnp.zeros((2, D), F32)
     arrive(grads_ref, cot_ref, cot_sems, count)
     for load in loads[:3]:
@@ -376,7 +386,8 @@
         cot = tile_rows(cot_ref, t, count).astype(BF)
         d_mixed = dot_cols(cot, w_out_ref[...])
         gained = normed * gain_attn_ref[...]
-        out_ref[...] += dot_rows((gained * upper).astype(BF), cot)
+        mixed_ref[:, rows] = (gained * upper).astype(BF).T
+        cot_rows_ref[rows, :] = cot
         d_upper = d_mixed * gained
         pull = d_mixed * upper
         gains_ref[1:2, :] += jnp.sum(pull * normed, axis=0, keepdims=True)
@@ -397,9 +408,17 @@
 
     def clear(t, carry):
         d_hidden_ref[:, rows_at(t), :] = jnp.zeros((4 * PAIRS, TILE, LANES), BF)
+        mixed_ref[:, rows_at(t)] = jnp.zeros((D, TILE), BF)
+        cot_rows_ref[rows_at(t), :] = jnp.zeros((TILE, D), BF)
         return carry
 
     lax.fori_loop(live, TILES, clear, 0)
+    saves = [
+        pltpu.make_async_copy(mixed_ref, mixed_out, load_sems.at[9]),
+        pltpu.make_async_copy(cot_rows_ref, cot_out, load_sems.at[10]),
+    ]
+    for save in saves:
+        save.start()
 
     masks = head_masks()
     for load in loads[3:7]:
@@ -490,8 +509,8 @@
 
     lax.fori_loop(0, PAIRS // GROUP, group, 0)
 
-    save = pltpu.make_async_copy(d_hidden_ref, d_hidden_out, load_sems.at[8])
-    save.start()
+    saves.append(pltpu.make_async_copy(d_hidden_ref, d_hidden_out, load_sems.at[8]))
+    saves[-1].start()
     arrive(got_ref, rows_ref, row_sems, count)
     for load in loads[7:]:
         load.wait()
@@ -512,7 +531,7 @@
             - jnp.mean(pull, axis=-1, keepdims=True)
             - normed * jnp.mean(pull * normed, axis=-1, keepdims=True)
         )
-        d_rows = (d_rows + tile_rows(cot_ref, t, count)).astype(BF)
+        d_rows = (d_rows + cot_rows_ref[rows, :].astype(F32)).astype(BF)
         for b in range(4):
             slot = (first + t * 4 + b) & (PEERS - 1)
             back_ref[slot] = d_rows[b * BLOCK : (b + 1) * BLOCK, :]
@@ -520,25 +539,31 @@
 
     lax.fori_loop(0, live, final, 0)
 
-    for p in range(PAIRS):
-        out_terms_ref[p] = out_ref[:, p * LANES : (p + 1) * LANES].astype(BF)
-    save.wait()
+    for save in saves:
+        save.wait()
 
 
 def terms_kernel(
     own_ref,
     d_hidden_in,
     scaled_in,
-    out_terms_ref,
+    mixed_in,
+    cot_in,
     gains_ref,
     keep_ref,
     send_ref,
     d_hidden_ref,
     scaled_ref,
+    mixed_ref,
+    cot_ref,
     sems,
 ):
     core = own_ref[0] & 1
-    loads = [pltpu.make_async_copy(scaled_in, scaled_ref, sems.at[8])]
+    loads = [
+        pltpu.make_async_copy(mixed_in, mixed_ref, sems.at[9]),
+        pltpu.make_async_copy(cot_in, cot_ref, sems.at[10]),
+        pltpu.make_async_copy(scaled_in, scaled_ref, sems.at[8]),
+    ]
     for c in range(8):
         part = pl.ds(2 * c, 2)
         loads.append(
@@ -562,8 +587,6 @@
         half, place = divmod(piece, 10)
         put(half, pl.ds(place * D, D), values)
 
-    for p in range(PAIRS):
-        put_piece(16 + p, out_terms_ref[p])
     for half in range(2):
         tail = jnp.concatenate(
             [gains_ref[half : half + 1, p * LANES : (p + 1) * LANES] for p in range(PAIRS)]
@@ -572,25 +595,45 @@
         )
         put(half, pl.ds(10 * D, HALF - 10 * D), tail)
     loads[0].wait()
+    loads[1].wait()
+    for c in range(2):
+        term = dot(mixed_ref[...], cot_ref[:, c * 256 : (c + 1) * 256])
+        put_piece(16 + 2 * c, term[:, :LANES])
+        put_piece(17 + 2 * c, term[:, LANES:])
+    loads[2].wait()
     for c in range(8):
-        loads[1 + c].wait()
+        loads[3 + c].wait()
         part = jnp.concatenate([d_hidden_ref[2 * c], d_hidden_ref[2 * c + 1]], axis=1)
         term = dot(scaled_ref[...], part)
         put_piece(2 * c, term[:, :LANES])
         put_piece(2 * c + 1, term[:, LANES:])
 
 
-def spread_kernel(own_ref, mine_ref, other_ref, proj_ref, out_ref, gain_in_ref, gain_attn_ref):
+def spread_kernel(
+    own_ref,
+    mine_ref,
+    other_ref,
+    proj_ref,
+    out_ref,
+    gain_in_ref,
+    gain_attn_ref,
+    wide_ref,
+    sems,
+):
     core = own_ref[0] & 1
+
+    def copy(piece):
+        if piece < 16:
+            target = proj_ref.at[:, pl.ds(piece * LANES, LANES)]
+        else:
+            target = out_ref.at[:, pl.ds((piece - 16) * LANES, LANES)]
+        return pltpu.make_async_copy(wide_ref.at[piece], target, sems.at[piece])
 
     def write(low_ref, high_ref):
         for piece in range(20):
             half, place = divmod(piece, 10)
-            part = (low_ref, high_ref)[half][place * D : (place + 1) * D, :].astype(F32)
-            if piece < 16:
-                proj_ref[:, piece * LANES : (piece + 1) * LANES] = part
-            else:
-                out_ref[:, (piece - 16) * LANES : (piece - 15) * LANES] = part
+            wide_ref[piece] = (low_ref, high_ref)[half][place * D : (place + 1) * D, :].astype(F32)
+            copy(piece).start()
         gain_in_ref[...] = low_ref[10 * D : 10 * D + 16, :].astype(F32)[:PAIRS]
         gain_attn_ref[...] = high_ref[10 * D : 10 * D + 16, :].astype(F32)[:PAIRS]
 
@@ -601,6 +644,9 @@
     @pl.when(core == 1)
     def _():
         write(other_ref, mine_ref)
+
+    for piece in range(20):
+        copy(piece).wait()
 
 
 def struct(shape, dtype):
@@ -615,8 +661,12 @@
     return pl.pallas_call(
         send_kernel,
         out_shape=struct((PEERS, BLOCK, D), BF),
-        in_specs=[SMEM_SPEC, SMEM_SPEC, VMEM_SPEC],
-        out_specs=VMEM_SPEC,
+        in_specs=[SMEM_SPEC, SMEM_SPEC, ANY_SPEC],
+        out_specs=ANY_SPEC,
+        scratch_shapes=[
+            pltpu.VMEM((LOCAL, BLOCK, D), BF),
+            pltpu.SemaphoreType.DMA((LOCAL + 1,)),
+        ],
         name="send_blocks",
     )(lens, own, rows.reshape(LOCAL, BLOCK, D))
 
@@ -631,7 +681,7 @@
 def forward_layer(lens, own, got_rows, w_proj, gain_in):
     return pl.pallas_call(
         forward_kernel,
-        out_shape=[struct((PAIRS, ROWS, LANES), BF)] + saved_shapes(struct),
+        out_shape=[pltpu.HBM((PAIRS, ROWS, LANES), BF)] + saved_shapes(pltpu.HBM),
         in_specs=[SMEM_SPEC, SMEM_SPEC, ANY_SPEC, VMEM_SPEC, VMEM_SPEC],
         out_specs=[VMEM_SPEC] + [HBM_SPEC] * 6,
         scratch_shapes=saved_shapes(pltpu.VMEM)
@@ -642,7 +692,7 @@
             pltpu.SemaphoreType.DMA((LEN_BLK,)),
             pltpu.SemaphoreType.DMA((6,)),
         ],
-        compiler_params=params(52),
+        compiler_params=params(32),
         name="forward_layer",
     )(lens, own, got_rows, w_proj, gain_in)
 
@@ -651,19 +701,21 @@
     return pl.pallas_call(
         backward_kernel,
         out_shape=(
-            struct((PEERS, BLOCK, D), BF),
-            struct((4 * PAIRS, ROWS, LANES), BF),
-            struct((PAIRS, D, LANES), BF),
+            pltpu.HBM((PEERS, BLOCK, D), BF),
+            pltpu.HBM((4 * PAIRS, ROWS, LANES), BF),
+            pltpu.HBM((D, ROWS), BF),
+            pltpu.HBM((ROWS, D), BF),
             struct((2, D), F32),
         ),
         in_specs=[SMEM_SPEC, SMEM_SPEC] + [ANY_SPEC] * 3 + [HBM_SPEC] * 6 + [VMEM_SPEC] * 3,
-        out_specs=(VMEM_SPEC, HBM_SPEC, VMEM_SPEC, VMEM_SPEC),
+        out_specs=(VMEM_SPEC, HBM_SPEC, HBM_SPEC, HBM_SPEC, VMEM_SPEC),
         scratch_shapes=[
             pltpu.VMEM((LEN_BLK, BLOCK, D), BF),
             pltpu.VMEM((LEN_BLK, BLOCK, D), BF),
             pltpu.VMEM((PAIRS, ROWS, LANES), BF),
             pltpu.VMEM((4 * PAIRS, ROWS, LANES), BF),
-            pltpu.VMEM((D, D), F32),
+            pltpu.VMEM((D, ROWS), BF),
+            pltpu.VMEM((ROWS, D), BF),
             pltpu.VMEM((GROUP, LANES, TILE), F32),
             pltpu.VMEM((PAIRS, LANES, ROWS), BF),
             pltpu.VMEM((GROUP, ROWS, LANES), F32),
@@ -671,34 +723,40 @@
             pltpu.SMEM((LEN_BLK,), jnp.int32),
             pltpu.SemaphoreType.DMA((LEN_BLK,)),
             pltpu.SemaphoreType.DMA((LEN_BLK,)),
-            pltpu.SemaphoreType.DMA((9,)),
+            pltpu.SemaphoreType.DMA((11,)),
             pltpu.VMEM((PAIRS, ROWS, LANES), BF),
         ]
         + saved_shapes(pltpu.VMEM)[:5]
         + [pltpu.VMEM((D, 4 * D), BF)],
-        compiler_params=params(52),
+        compiler_params=params(44),
         name="backward_layer",
     )(lens, own, got_rows, got_grads, *saved[:6], w_proj, w_out, gain_in, gain_attn)
 
 
-def gradient_terms(own, d_hidden, scaled, out_terms, gains):
+def gradient_terms(own, d_hidden, scaled, mixed, cot, gains):
     half = struct((HALF, LANES), BF)
     return pl.pallas_call(
         terms_kernel,
         out_shape=(half, half),
-        in_specs=[SMEM_SPEC, HBM_SPEC, HBM_SPEC, VMEM_SPEC, VMEM_SPEC],
+        in_specs=[SMEM_SPEC] + [HBM_SPEC] * 4 + [VMEM_SPEC],
         out_specs=(VMEM_SPEC, VMEM_SPEC),
         scratch_shapes=[
             pltpu.VMEM((4 * PAIRS, ROWS, LANES), BF),
             pltpu.VMEM((D, ROWS), BF),
-            pltpu.SemaphoreType.DMA((9,)),
+            pltpu.VMEM((D, ROWS), BF),
+            pltpu.VMEM((ROWS, D), BF),
+            pltpu.SemaphoreType.DMA((11,)),
         ],
-        compiler_params=params(52),
+        compiler_params=params(40),
         cost_estimate=pl.CostEstimate(
-            flops=8 * ROWS * D * D, transcendentals=0, bytes_accessed=8 * MIB
+            flops=10 * ROWS * D * D, transcendentals=0, bytes_accessed=10 * MIB
         ),
         name="gradient_terms",
-    )(own, d_hidden, scaled, out_terms, gains)
+    )(own, d_hidden, scaled, mixed, cot, gains)
+
+
+def in_hbm(array):
+    return pltpu.with_memory_space_constraint(array, pltpu.HBM)
 
 
 def per_device(events, cotangent, lengths, gain_in, w_proj, gain_attn, w_out):
@@ -707,12 +765,13 @@
     got_rows = lax.all_to_all(send_blocks(lens, own, events), ("chip", "core"), 0, 0, tiled=True)
     got_grads = lax.all_to_all(send_blocks(lens, own, cotangent), ("chip", "core"), 0, 0, tiled=True)
     gain_in = gain_in.reshape(1, D)
-    saved = forward_layer(lens, own, got_rows, w_proj, gain_in)
-    send_back, d_hidden, out_terms, gains = backward_layer(
+    saved = [in_hbm(x) for x in forward_layer(lens, own, got_rows, w_proj, gain_in)]
+    send_back, *kept, gains = backward_layer(
         lens, own, got_rows, got_grads, saved, w_proj, w_out, gain_in, gain_attn.reshape(1, D)
     )
     came_back = lax.all_to_all(send_back, ("chip", "core"), 0, 0, tiled=True)
-    keep, send = gradient_terms(own, d_hidden, saved[6], out_terms, gains)
+    d_hidden, mixed, cot = (in_hbm(x) for x in kept)
+    keep, send = gradient_terms(own, d_hidden, saved[6], mixed, cot, gains)
     send, came_back = lax.optimization_barrier((send, came_back))
     swap = [(0, 1), (1, 0)]
     other = lax.ppermute(send, "core", swap)
@@ -734,7 +793,8 @@
         spread_kernel,
         out_shape=(struct((D, 4 * D), F32), struct((D, D), F32), gain, gain),
         in_specs=[SMEM_SPEC, VMEM_SPEC, VMEM_SPEC],
-        out_specs=(VMEM_SPEC,) * 4,
+        out_specs=(ANY_SPEC, ANY_SPEC, VMEM_SPEC, VMEM_SPEC),
+        scratch_shapes=[pltpu.VMEM((20, D, LANES), F32), pltpu.SemaphoreType.DMA((20,))],
         compiler_params=params(16),
         name="spread_grads",
     )(own, mine, others)

time: 182 us -> 178 us (0.978)
  Pallas kernels: 61.9 us -> 37.4 us
  starting transfers between devices: 32.7 us -> 47.7 us
  waiting for transfers between devices: 27.8 us -> 36.4 us
    pallas_call x3, Pallas kernels: 52.1 us -> 26.8 us  [the longest x1 10.7 us: backward_layer(): pl.pallas_call(backward_kernel, out_shape=(pltpu.HBM((PEERS, BLOCK, D), B...]
    all_to_all x1, starting transfers between devices: 14.8 us -> 29.1 us  [per_device(): came_back = lax.all_to_all(send_back, ('chip', 'core'), 0, 0, tiled=True)]
    all_to_all x1, waiting for transfers between devices: 0.46 us -> 9.97 us  [per_device(): lax.all_to_all(send_blocks(lens, own, cotangent), ('chip', 'core'), 0, 0,...]
  transfers between devices with their start and end apart: 5 -> 5, of which waited for: 5 -> 5; matrix products, arithmetic and copies ran while one was open for 0% -> 0% of each run, Pallas kernels for 16% -> 12%
where the time goes in v5:
time: 178 us
  blocking collectives  53.2 us (30%)
  starting transfers between devices  47.7 us (27%)
  Pallas kernels  37.4 us (21%)
  waiting for transfers between devices  36.4 us (20%)
    all_to_all x1, starting transfers between devices, per_device(): came_back = lax.all_to_all(send_back, ('chip', 'core'), 0, 0, tiled=True)  29.1 us
    all_to_all x1, blocking collectives, per_device(): lax.all_to_all(chip_sum.reshape(64, PART, LANES), ('grp', 'chip'), 0, 0,...  28 us
    all_to_all x1, blocking collectives, per_device(): lax.all_to_all(copies, ('grp', 'chip'), 0, 0, tiled=True)  25.2 us
    all_to_all x1, waiting for transfers between devices, per_device(): lax.all_to_all(send_blocks(lens, own, events), ('chip', 'core'), 0, 0, ti...  14.5 us
    pallas_call x1, Pallas kernels, backward_layer(): pl.pallas_call(backward_kernel, out_shape=(pltpu.HBM((PEERS, BLOCK, D), B...  10.7 us
    all_to_all x1, waiting for transfers between devices, per_device(): lax.all_to_all(send_blocks(lens, own, cotangent), ('chip', 'core'), 0, 0,...  9.97 us
    all_to_all x1, starting transfers between devices, per_device(): lax.all_to_all(send_blocks(lens, own, events), ('chip', 'core'), 0, 0, ti...  9.3 us
    pallas_call x1, Pallas kernels, gradient_terms(): pl.pallas_call(terms_kernel, out_shape=(half, half), in_specs=[SMEM_SPEC]...  8.78 us
  transfers between devices with their start and end apart: 5, of which 5 were waited for; matrix products, arithmetic and copies ran while one was open for 0% of the time, Pallas kernels for 12%

profile of v5, /device:TPU:1, one launch (start us, length us, event | category | flops | bytes accessed | tf_op | source)
XLA Modules:
  0.0 177.6 jit_solution(17149278615566022216)
XLA Ops:
  0.6 2.6 %send_blocks.2 = bf16[16,64,512]{2,1,0:T(8,128)(2,1)} custom-call(s32[16]{0:T(128)} %bitcast.13, s32[1]{0:T(128)} %bitcast.1.own_ref, bf16[8,64,512]{2,1,0:T(8,128)(2,1)} %bitcast.22), custom_call_target="tpu_custom_call" | custom-call | tf_op jit(solution)/shard_map/send_blocks/pallas_call | solution.py:661
  3.2 9.3 %all-to-all-start = ((bf16[16,64,512]{2,1,0:T(8,128)(2,1)}), bf16[16,64,512]{2,1,0:T(8,128)(2,1)S(1)}, u32[]{:S(2)}, u32[]{:S(2)}) async-start(bf16[16,64,512]{2,1,0:T(8,128)(2,1)} %send_blocks.2), calls=%async_computation | async-start | bytes 2097152 | tf_op jit(solution)/shard_map/all_to_all | solution.py:765
  12.5 0.0 copy-start.3
  12.5 2.7 %send_blocks.3 = bf16[16,64,512]{2,1,0:T(8,128)(2,1)} custom-call(s32[16]{0:T(128)} %bitcast.14, s32[1]{0:T(128)} %bitcast.1.own_ref, bf16[8,64,512]{2,1,0:T(8,128)(2,1)} %bitcast.23), custom_call_target="tpu_custom_call" | custom-call | tf_op jit(solution)/shard_map/send_blocks/pallas_call | solution.py:661
  15.2 0.0 copy-start
  15.2 0.0 copy-start.2
  15.3 14.5 %all-to-all-done.got_ref = bf16[16,64,512]{2,1,0:T(8,128)(2,1)S(1)} async-done(((bf16[16,64,512]{2,1,0:T(8,128)(2,1)}), bf16[16,64,512]{2,1,0:T(8,128)(2,1)S(1)}, u32[]{:S(2)}, u32[]{:S(2)}) %all-to-all-start) | async-done | bytes 1048608 | tf_op jit(solution)/shard_map/all_to_all | solution.py:765
  29.7 5.0 %all-to-all-start.1 = ((bf16[16,64,512]{2,1,0:T(8,128)(2,1)}), bf16[16,64,512]{2,1,0:T(8,128)(2,1)}, u32[]{:S(2)}, u32[]{:S(2)}) async-start(bf16[16,64,512]{2,1,0:T(8,128)(2,1)} %send_blocks.3), calls=%async_computation.1 | async-start | bytes 2097152 | tf_op jit(solution)/shard_map/all_to_all | solution.py:766
  34.7 0.0 copy-done.3
  34.7 0.0 copy-done
  34.7 0.0 copy-done.2
  34.7 0.0 copy-start.4
  34.7 7.4 %forward_layer.1 = (bf16[4,1024,128]{2,1,0:T(8,128)(2,1)}, bf16[1024,512]{1,0:T(8,128)(2,1)}, bf16[4,1024,128]{2,1,0:T(8,128)(2,1)}, bf16[4,1024,128]{2,1,0:T(8,...) custom-call(s32[16]{0:T(128)S(1)} %bitcast.16, ...), custom_call_target="tpu_custom_call" | custom-call | tf_op jit(solution)/shard_map/forward_layer/pallas_call | solution.py:682
  42.1 10.0 %all-to-all-done.1.grads_ref = bf16[16,64,512]{2,1,0:T(8,128)(2,1)} async-done(((bf16[16,64,512]{2,1,0:T(8,128)(2,1)}), bf16[16,64,512]{2,1,0:T(8,128)(2,1)}, u32[]{:S(2)}, u32[]{:S(2)}) %all-to-all-start.1) | async-done | bytes 1048608 | tf_op jit(solution)/shard_map/all_to_all | solution.py:766
  52.1 0.0 copy-done.4
  52.1 0.0 copy-start.1
  52.1 1.0 copy-done.1
  53.1 10.7 %backward_layer.1 = (bf16[16,64,512]{2,1,0:T(8,128)(2,1)}, bf16[16,1024,128]{2,1,0:T(8,128)(2,1)}, bf16[512,1024]{1,0:T(8,128)(2,1)}, bf16[1024,512]{1,0:T(8,128)(2,1)}, f32[2,512]{1,0:T(2,128)S(1)}) custom-call(s32[16]{0:T(128)S(1)} %bitcast.17, s32[1]{0:T(128)} %bitcast.1.own_ref, bf16[16,64,512]{2,1,0:T(8,128)(2,1)S(1)} %all-to-all-done.got_ref, ...), custom_call_target="tpu_custom_call" | custom-call | tf_op jit(solution)/shard_map/backward_layer/pallas_call | solution.py:701
  63.8 29.1 %all-to-all-start.2 = ((bf16[16,64,512]{2,1,0:T(8,128)(2,1)}), bf16[16,64,512]{2,1,0:T(8,128)(2,1)}, u32[]{:S(2)}, u32[]{:S(2)}) async-start(bf16[16,64,512]{2,1,0:T(8,128)(2,1)} %get-tuple-element.37), calls=%async_computation.2 | async-start | bytes 2097152 | tf_op jit(solution)/shard_map/all_to_all | solution.py:772
  92.9 8.8 %gradient_terms.1 = (bf16[5632,128]{1,0:T(8,128)(2,1)S(1)}, bf16[5632,128]{1,0:T(8,128)(2,1)S(1)}) custom-call(s32[1]{0:T(128)} %bitcast.1.own_ref, bf16[16,1024,128]{2,1,0:T(8,128)(2,1)} %get-tuple-element.31.d_hidden_in, bf16[512,1024]{1,0:T(8,128)(2,1)} %get-tuple-element.32.scaled_in, bf16[512,1024]{1,0:T(8,128)(2,1)} %get-tuple-element.33.mixed_in, ...), custom_call_target="tpu_custom_call" | custom-call | flops 2684354560 | bytes 10485760 | tf_op jit(solution)/shard_map/gradient_terms/pallas_call | solution.py:738
  101.7 8.5 %all-to-all-done.2.back_ref = bf16[16,64,512]{2,1,0:T(8,128)(2,1)} async-done(((bf16[16,64,512]{2,1,0:T(8,128)(2,1)}), bf16[16,64,512]{2,1,0:T(8,128)(2,1)}, u32[]{:S(2)}, u32[]{:S(2)}) %all-to-all-start.2) | async-done | bytes 1048608 | tf_op jit(solution)/shard_map/all_to_all | solution.py:772
  110.3 0.9 collective-permute-start
  111.2 2.8 %collective-permute-done = bf16[5632,128]{1,0:T(8,128)(2,1)S(1)} collective-permute-done((bf16[5632,128]{1,0:T(8,128)(2,1)S(1)}, bf16[5632,128]{1,0:T(8,128)(2,1)S(1)}, u32[]{:S(2)}, u32[]{:S(2)}) %collective-permute-start) | collective-permute-done | bytes 1441824 | tf_op jit(solution)/shard_map/ppermute | solution.py:777
  114.0 0.4 add_convert_fusion
  114.4 28.0 %all_to_all.25 = bf16[64,88,128]{2,1,0:T(8,128)(2,1)S(1)} all-to-all(bf16[64,88,128]{2,1,0:T(8,128)(2,1)S(1)} %bitcast.21), channel_id=1, replica_groups=mesh['grp'=8,'chip'=8,'core'=2] {'grp','chip'}, dimensions={0} | all-to-all | bytes 2883584 | tf_op jit(solution)/shard_map/all_to_all | solution.py:779
  142.4 0.2 convert_reduce_fusion
  142.7 0.2 broadcast_in_dim.2
  142.9 25.2 %all_to_all.26 = bf16[64,88,128]{2,1,0:T(8,128)(2,1)S(1)} all-to-all(bf16[64,88,128]{2,1,0:T(8,128)(2,1)S(1)} %broadcast_in_dim.2), channel_id=1, replica_groups=mesh['grp'=8,'chip'=8,'core'=2] {'grp','chip'}, dimensions={0} | all-to-all | bytes 2883584 | tf_op jit(solution)/shard_map/all_to_all | solution.py:782
  168.0 3.4 %collective-permute-start.1 = (bf16[5632,128]{1,0:T(8,128)(2,1)S(1)}, bf16[5632,128]{1,0:T(8,128)(2,1)S(1)}, u32[]{:S(2)}, u32[]{:S(2)}) collective-permute-start(bf16[5632,128]{1,0:T(8,128)(2,1)S(1)} %bitcast.11), channel_id=1, source_target_pairs={{0,1},{1,0},{2,3},{3,2},{4,5},{5,4},{6,7},{7,6},{8,9},{9,8},{10,11... | collective-permute-start | bytes 4325384 | tf_op jit(solution)/shard_map/ppermute | solution.py:783
  171.4 2.2 %take_home.1 = bf16[8,64,512]{2,1,0:T(8,128)(2,1)} custom-call(s32[16]{0:T(128)} %bitcast.15, s32[1]{0:T(128)} %bitcast.1.own_ref, bf16[16,64,512]{2,1,0:T(8,128)(2,1)} %all-to-all-done.2.back_ref), custom_call_target="tpu_custom_call" | custom-call | tf_op jit(solution)/shard_map/take_home/pallas_call | solution.py:784
  173.6 0.6 collective-permute-done.1.other_ref
  174.3 3.1 %spread_grads.1 = (f32[512,2048]{1,0:T(8,128)}, f32[512,512]{1,0:T(8,128)}, f32[4,128]{1,0:T(4,128)}, f32[4,128]{1,0:T(4,128)}) custom-call(s32[1]{0:T(128)} %bitcast.1.own_ref, bf16[5632,128]{1,0:T(8,128)(2,1)S(1)} %bitcast.12, bf16[5632,128]{1,0:T(8,128)(2,1)S(1)} %collective-permute-done.1.other_ref), custom_call_target="tpu_custom_call" | custom-call | tf_op jit(solution)/shard_map/spread_grads/pallas_call | solution.py:792
  (1 shorter events, 0.0 us)
Async XLA Ops:
  3.2 26.5 %all-to-all-start = ((bf16[16,64,512]{2,1,0:T(8,128)(2,1)}), bf16[16,64,512]{2,1,0:T(8,128)(2,1)S(1)}, u32[]{:S(2)}, u32[]{:S(2)}) async-start(bf16[16,64,512]{2,1,0:T(8,128)(2,1)} %send_blocks.2), calls=%async_computation | async-start | bytes 2097152 | tf_op jit(solution)/shard_map/all_to_all | solution.py:765
  12.5 22.2 %copy-start.3 = (f32[512]{0:T(512)S(1)}, f32[512]{0:T(512)}, u32[]{:S(2)}) copy-start(f32[512]{0:T(512)} %param.10) | copy-start | bytes 6148
  15.2 19.5 %copy-start = (bf16[512,2048]{1,0:T(8,128)(2,1)S(1)}, bf16[512,2048]{1,0:T(8,128)(2,1)}, u32[]{:S(2)}) copy-start(bf16[512,2048]{1,0:T(8,128)(2,1)} %w_in.1) | copy-start | bytes 6291460
  15.2 19.5 %copy-start.2 = (s32[1,16]{1,0:T(1,128)S(1)}, s32[1,16]{1,0:T(1,128)}, u32[]{:S(2)}) copy-start(s32[1,16]{1,0:T(1,128)} %param.9) | copy-start | bytes 196
  29.7 22.4 %all-to-all-start.1 = ((bf16[16,64,512]{2,1,0:T(8,128)(2,1)}), bf16[16,64,512]{2,1,0:T(8,128)(2,1)}, u32[]{:S(2)}, u32[]{:S(2)}) async-start(bf16[16,64,512]{2,1,0:T(8,128)(2,1)} %send_blocks.3), calls=%async_computation.1 | async-start | bytes 2097152 | tf_op jit(solution)/shard_map/all_to_all | solution.py:766
  34.7 17.4 %copy-start.4 = (f32[512]{0:T(512)S(1)}, f32[512]{0:T(512)}, u32[]{:S(2)}) copy-start(f32[512]{0:T(512)} %param.12) | copy-start | bytes 6148
  52.1 1.0 copy-start.1
  63.8 46.4 %all-to-all-start.2 = ((bf16[16,64,512]{2,1,0:T(8,128)(2,1)}), bf16[16,64,512]{2,1,0:T(8,128)(2,1)}, u32[]{:S(2)}, u32[]{:S(2)}) async-start(bf16[16,64,512]{2,1,0:T(8,128)(2,1)} %get-tuple-element.37), calls=%async_computation.2 | async-start | bytes 2097152 | tf_op jit(solution)/shard_map/all_to_all | solution.py:772
  110.3 3.8 %collective-permute-start = (bf16[5632,128]{1,0:T(8,128)(2,1)S(1)}, bf16[5632,128]{1,0:T(8,128)(2,1)S(1)}, u32[]{:S(2)}, u32[]{:S(2)}) collective-permute-start(bf16[5632,128]{1,0:T(8,128)(2,1)S(1)} %get-tuple-element.40), channel_id=1, source_target_pairs={{0,1},{1,0},{2,3},{3,2},{4,5},{5,4},{6,7},{7,6},{8,9},{9,8},{10,11... | collective-permute-start | bytes 4325384 | tf_op jit(solution)/shard_map/ppermute | solution.py:777
  168.0 6.2 %collective-permute-start.1 = (bf16[5632,128]{1,0:T(8,128)(2,1)S(1)}, bf16[5632,128]{1,0:T(8,128)(2,1)S(1)}, u32[]{:S(2)}, u32[]{:S(2)}) collective-permute-start(bf16[5632,128]{1,0:T(8,128)(2,1)S(1)} %bitcast.11), channel_id=1, source_target_pairs={{0,1},{1,0},{2,3},{3,2},{4,5},{5,4},{6,7},{7,6},{8,9},{9,8},{10,11... | collective-permute-start | bytes 4325384 | tf_op jit(solution)/shard_map/ppermute | solution.py:783

commit v6 on v5

--- a/solution.py
+++ b/solution.py
@@ -99,19 +99,10 @@
             lax.fori_loop(begin, begin + sizes[i], put, 0)
 
 
-def send_kernel(len_ref, own_ref, rows_ref, out_ref, held_ref, sems):
-    load = pltpu.make_async_copy(rows_ref, held_ref, sems.at[LOCAL])
-    load.start()
+def send_kernel(len_ref, own_ref, rows_ref, out_ref):
     owner = owners(len_ref, own_ref[0])
-    copies = [
-        pltpu.make_async_copy(held_ref.at[k], out_ref.at[owner[k]], sems.at[k])
-        for k in range(LOCAL)
-    ]
-    load.wait()
-    for copy in copies:
-        copy.start()
-    for copy in copies:
-        copy.wait()
+    for k in range(LOCAL):
+        out_ref[owner[k]] = rows_ref[k]
 
 
 def home_kernel(len_ref, own_ref, back_ref, out_ref):
@@ -120,25 +111,9 @@
         out_ref[k] = back_ref[owner[k]]
 
 
-def fetch(src_ref, dst_ref, sems, first, count):
-    for j in range(LEN_BLK):
-
-        @pl.when(j < count)
-        def _(j=j):
-            slot = (first + j) & (PEERS - 1)
-            pltpu.make_async_copy(src_ref.at[slot], dst_ref.at[j], sems.at[j]).start()
-
-
-def arrive(src_ref, dst_ref, sems, count):
-    for j in range(LEN_BLK):
-
-        @pl.when(j < count)
-        def _(j=j):
-            pltpu.make_async_copy(src_ref.at[0], dst_ref.at[j], sems.at[j]).wait()
-
-
-def tile_rows(ref, t, count):
-    tile = ref[pl.ds(t * 4, 4)].reshape(TILE, D).astype(F32)
+def tile_rows(ref, t, first, count):
+    slots = [(first + t * 4 + b) & (PEERS - 1) for b in range(4)]
+    tile = jnp.concatenate([ref[slot] for slot in slots], axis=0).astype(F32)
     place = lax.broadcasted_iota(jnp.int32, (TILE, D), 0) + t * TILE
     return jnp.where(place < count * BLOCK, tile, 0.0)
 
@@ -196,21 +171,17 @@
     keys_ref,
     slope_ref,
     scaled_ref,
-    rows_ref,
     acc_ref,
     hist_ref,
-    sems,
     save_sems,
 ):
     own = own_ref[0]
     starts, sizes, ranks, first, count = holdings(len_ref, own)
-    fetch(got_ref, rows_ref, sems, first, count)
     history_starts(hist_ref, own, starts, sizes, ranks, first)
     live = (count + 3) // 4
-    arrive(got_ref, rows_ref, sems, count)
 
     def project(t, carry):
-        normed, _ = normed_rows(tile_rows(rows_ref, t, count))
+        normed, _ = normed_rows(tile_rows(got_ref, t, first, count))
         scaled = (normed * gain_ref[...]).astype(BF)
         rows = rows_at(t)
         scaled_ref[:, rows] = scaled.T
@@ -318,7 +289,7 @@
     keys_in,
     slope_in,
     w_in,
-    w_out_ref,
+    w_out_in,
     gain_in_ref,
     gain_attn_ref,
     back_ref,
@@ -326,8 +297,6 @@
     mixed_out,
     cot_out,
     gains_ref,
-    rows_ref,
-    cot_ref,
     d_attn_ref,
     d_hidden_ref,
     mixed_ref,
@@ -337,8 +306,7 @@
     d_keys_ref,
     d_values_ref,
     hist_ref,
-    row_sems,
-    cot_sems,
+    tile_sems,
     load_sems,
     attn_ref,
     upper_ref,
@@ -347,19 +315,31 @@
     keys_ref,
     slope_ref,
     w_ref,
+    w_out_ref,
 ):
     own = own_ref[0]
     starts, sizes, ranks, first, count = holdings(len_ref, own)
-    fetch(grads_ref, cot_ref, cot_sems, first, count)
+    live = (count + 3) // 4
     early = pl.ds(0, PAIRS)
     late = pl.ds(PAIRS, 3 * PAIRS)
+
+    def tile_loads(t):
+        rows = rows_at(t)
+        return [
+            pltpu.make_async_copy(
+                attn_in.at[:, rows], attn_ref.at[:, rows], tile_sems.at[0, t]
+            ),
+            pltpu.make_async_copy(upper_in.at[rows], upper_ref.at[rows], tile_sems.at[1, t]),
+            pltpu.make_async_copy(
+                slope_in.at[early, rows], slope_ref.at[early, rows], tile_sems.at[2, t]
+            ),
+        ]
+
     loads = [
         pltpu.make_async_copy(src, dst, load_sems.at[n])
         for n, (src, dst) in enumerate(
             (
-                (attn_in, attn_ref),
-                (upper_in, upper_ref),
-                (slope_in.at[early], slope_ref.at[early]),
+                (w_out_in, w_out_ref),
                 (keys_in, keys_ref),
                 (query_in, query_ref),
                 (values_in, values_ref),
@@ -368,22 +348,28 @@
             )
         )
     ]
-    for load in loads:
+    loads[0].start()
+
+    def request(t, carry):
+        for load in tile_loads(t):
+            load.start()
+        return carry
+
+    lax.fori_loop(0, live, request, 0)
+    for load in loads[1:]:
         load.start()
-    fetch(got_ref, rows_ref, row_sems, first, count)
     history_starts(hist_ref, own, starts, sizes, ranks, first)
-    live = (count + 3) // 4
     gains_ref[...] = jnp.zeros((2, D), F32)
-    arrive(grads_ref, cot_ref, cot_sems, count)
-    for load in loads[:3]:
-        load.wait()
+    loads[0].wait()
 
     def middle(t, carry):
         rows = rows_at(t)
+        for load in tile_loads(t):
+            load.wait()
         attn = jnp.concatenate([attn_ref[p, rows, :] for p in range(PAIRS)], axis=1)
         normed, rstd = normed_rows(attn.astype(F32))
         upper = upper_ref[rows, :].astype(F32)
-        cot = tile_rows(cot_ref, t, count).astype(BF)
+        cot = tile_rows(grads_ref, t, first, count).astype(BF)
         d_mixed = dot_cols(cot, w_out_ref[...])
         gained = normed * gain_attn_ref[...]
         mixed_ref[:, rows] = (gained * upper).astype(BF).T
@@ -414,14 +400,14 @@
 
     lax.fori_loop(live, TILES, clear, 0)
     saves = [
-        pltpu.make_async_copy(mixed_ref, mixed_out, load_sems.at[9]),
-        pltpu.make_async_copy(cot_rows_ref, cot_out, load_sems.at[10]),
+        pltpu.make_async_copy(mixed_ref, mixed_out, load_sems.at[7]),
+        pltpu.make_async_copy(cot_rows_ref, cot_out, load_sems.at[8]),
     ]
     for save in saves:
         save.start()
 
     masks = head_masks()
-    for load in loads[3:7]:
+    for load in loads[1:5]:
         load.wait()
 
     def turn(t, carry):
@@ -509,15 +495,13 @@
 
     lax.fori_loop(0, PAIRS // GROUP, group, 0)
 
-    saves.append(pltpu.make_async_copy(d_hidden_ref, d_hidden_out, load_sems.at[8]))
+    saves.append(pltpu.make_async_copy(d_hidden_ref, d_hidden_out, load_sems.at[6]))
     saves[-1].start()
-    arrive(got_ref, rows_ref, row_sems, count)
-    for load in loads[7:]:
-        load.wait()
+    loads[5].wait()
 
     def final(t, carry):
         rows = rows_at(t)
-        normed, rstd = normed_rows(tile_rows(rows_ref, t, count))
+        normed, rstd = normed_rows(tile_rows(got_ref, t, first, count))
         d_scaled = jnp.zeros((TILE, D), F32)
         for c in range(8):
             part = jnp.concatenate(
@@ -661,12 +645,8 @@
     return pl.pallas_call(
         send_kernel,
         out_shape=struct((PEERS, BLOCK, D), BF),
-        in_specs=[SMEM_SPEC, SMEM_SPEC, ANY_SPEC],
-        out_specs=ANY_SPEC,
-        scratch_shapes=[
-            pltpu.VMEM((LOCAL, BLOCK, D), BF),
-            pltpu.SemaphoreType.DMA((LOCAL + 1,)),
-        ],
+        in_specs=[SMEM_SPEC, SMEM_SPEC, VMEM_SPEC],
+        out_specs=VMEM_SPEC,
         name="send_blocks",
     )(lens, own, rows.reshape(LOCAL, BLOCK, D))
 
@@ -682,14 +662,12 @@
     return pl.pallas_call(
         forward_kernel,
         out_shape=[pltpu.HBM((PAIRS, ROWS, LANES), BF)] + saved_shapes(pltpu.HBM),
-        in_specs=[SMEM_SPEC, SMEM_SPEC, ANY_SPEC, VMEM_SPEC, VMEM_SPEC],
+        in_specs=[SMEM_SPEC, SMEM_SPEC, VMEM_SPEC, VMEM_SPEC, VMEM_SPEC],
         out_specs=[VMEM_SPEC] + [HBM_SPEC] * 6,
         scratch_shapes=saved_shapes(pltpu.VMEM)
         + [
-            pltpu.VMEM((LEN_BLK, BLOCK, D), BF),
             pltpu.VMEM((GROUP, TILE, LANES), F32),
             pltpu.SMEM((LEN_BLK,), jnp.int32),
-            pltpu.SemaphoreType.DMA((LEN_BLK,)),
             pltpu.SemaphoreType.DMA((6,)),
         ],
         compiler_params=params(32),
@@ -707,11 +685,9 @@
             pltpu.HBM((ROWS, D), BF),
             struct((2, D), F32),
         ),
-        in_specs=[SMEM_SPEC, SMEM_SPEC] + [ANY_SPEC] * 3 + [HBM_SPEC] * 6 + [VMEM_SPEC] * 3,
+        in_specs=[SMEM_SPEC] * 2 + [VMEM_SPEC] * 2 + [ANY_SPEC] * 8 + [VMEM_SPEC] * 2,
         out_specs=(VMEM_SPEC, HBM_SPEC, HBM_SPEC, HBM_SPEC, VMEM_SPEC),
         scratch_shapes=[
-            pltpu.VMEM((LEN_BLK, BLOCK, D), BF),
-            pltpu.VMEM((LEN_BLK, BLOCK, D), BF),
             pltpu.VMEM((PAIRS, ROWS, LANES), BF),
             pltpu.VMEM((4 * PAIRS, ROWS, LANES), BF),
             pltpu.VMEM((D, ROWS), BF),
@@ -721,13 +697,12 @@
             pltpu.VMEM((GROUP, ROWS, LANES), F32),
             pltpu.VMEM((GROUP, ROWS, LANES), F32),
             pltpu.SMEM((LEN_BLK,), jnp.int32),
-            pltpu.SemaphoreType.DMA((LEN_BLK,)),
-            pltpu.SemaphoreType.DMA((LEN_BLK,)),
-            pltpu.SemaphoreType.DMA((11,)),
+            pltpu.SemaphoreType.DMA((3, TILES)),
+            pltpu.SemaphoreType.DMA((9,)),
             pltpu.VMEM((PAIRS, ROWS, LANES), BF),
         ]
         + saved_shapes(pltpu.VMEM)[:5]
-        + [pltpu.VMEM((D, 4 * D), BF)],
+        + [pltpu.VMEM((D, 4 * D), BF), pltpu.VMEM((D, D), BF)],
         compiler_params=params(44),
         name="backward_layer",
     )(lens, own, got_rows, got_grads, *saved[:6], w_proj, w_out, gain_in, gain_attn)
@@ -767,7 +742,7 @@
     gain_in = gain_in.reshape(1, D)
     saved = [in_hbm(x) for x in forward_layer(lens, own, got_rows, w_proj, gain_in)]
     send_back, *kept, gains = backward_layer(
-        lens, own, got_rows, got_grads, saved, w_proj, w_out, gain_in, gain_attn.reshape(1, D)
+        lens, own, got_rows, got_grads, saved, w_proj, in_hbm(w_out), gain_in, gain_attn.reshape(1, D)
     )
     came_back = lax.all_to_all(send_back, ("chip", "core"), 0, 0, tiled=True)
     d_hidden, mixed, cot = (in_hbm(x) for x in kept)

time: 178 us -> 175 us (0.983)
  starting transfers between devices: 47.7 us -> 41 us
  Pallas kernels: 37.4 us -> 42.3 us
    all_to_all x1, starting transfers between devices: 29.1 us -> 22.5 us  [per_device(): came_back = lax.all_to_all(send_back, ('chip', 'core'), 0, 0, tiled=True)]
    pallas_call x1, Pallas kernels: 10.7 us -> 15.3 us  [backward_layer(): pl.pallas_call(backward_kernel, out_shape=(pltpu.HBM((PEERS, BLOCK, D), B...]
where the time goes in v6:
time: 175 us; the launch traced here: 174 us
  blocking collectives  53.2 us (30%)
  Pallas kernels  42.3 us (24%)
  starting transfers between devices  41 us (23%)
  waiting for transfers between devices  35.9 us (21%)
    all_to_all x1, blocking collectives, per_device(): lax.all_to_all(chip_sum.reshape(64, PART, LANES), ('grp', 'chip'), 0, 0,...  28 us
    all_to_all x1, blocking collectives, per_device(): lax.all_to_all(copies, ('grp', 'chip'), 0, 0, tiled=True)  25.2 us
    all_to_all x1, starting transfers between devices, per_device(): came_back = lax.all_to_all(send_back, ('chip', 'core'), 0, 0, tiled=True)  22.5 us
    pallas_call x1, Pallas kernels, backward_layer(): pl.pallas_call(backward_kernel, out_shape=(pltpu.HBM((PEERS, BLOCK, D), B...  15.3 us
    all_to_all x1, waiting for transfers between devices, per_device(): lax.all_to_all(send_blocks(lens, own, events), ('chip', 'core'), 0, 0, ti...  14.9 us
    all_to_all x1, starting transfers between devices, per_device(): lax.all_to_all(send_blocks(lens, own, events), ('chip', 'core'), 0, 0, ti...  9.29 us
    all_to_all x1, waiting for transfers between devices, per_device(): lax.all_to_all(send_blocks(lens, own, cotangent), ('chip', 'core'), 0, 0,...  8.93 us
    pallas_call x1, Pallas kernels, gradient_terms(): pl.pallas_call(terms_kernel, out_shape=(half, half), in_specs=[SMEM_SPEC]...  8.78 us
  transfers between devices with their start and end apart: 5, of which 5 were waited for; matrix products, arithmetic and copies ran while one was open for 0% of the time, Pallas kernels for 12%

profile of v6, /device:TPU:1, one launch (start us, length us, event | category | flops | bytes accessed | tf_op | source)
XLA Modules:
  0.0 174.2 jit_solution(475868424961235068)
XLA Ops:
  0.6 2.2 %send_blocks.2 = bf16[16,64,512]{2,1,0:T(8,128)(2,1)} custom-call(s32[16]{0:T(128)} %bitcast.13, s32[1]{0:T(128)} %bitcast.1.own_ref, bf16[8,64,512]{2,1,0:T(8,128)(2,1)} %bitcast.22), custom_call_target="tpu_custom_call" | custom-call | tf_op jit(solution)/shard_map/send_blocks/pallas_call | solution.py:645
  2.9 9.3 %all-to-all-start = ((bf16[16,64,512]{2,1,0:T(8,128)(2,1)}), bf16[16,64,512]{2,1,0:T(8,128)(2,1)S(1)}, u32[]{:S(2)}, u32[]{:S(2)}) async-start(bf16[16,64,512]{2,1,0:T(8,128)(2,1)} %send_blocks.2), calls=%async_computation | async-start | bytes 2097152 | tf_op jit(solution)/shard_map/all_to_all | solution.py:740
  12.2 0.0 copy-start.2
  12.2 2.2 %send_blocks.3 = bf16[16,64,512]{2,1,0:T(8,128)(2,1)} custom-call(s32[16]{0:T(128)} %bitcast.14, s32[1]{0:T(128)} %bitcast.1.own_ref, bf16[8,64,512]{2,1,0:T(8,128)(2,1)} %bitcast.23), custom_call_target="tpu_custom_call" | custom-call | tf_op jit(solution)/shard_map/send_blocks/pallas_call | solution.py:645
  14.4 0.0 copy-start
  14.4 0.0 copy-start.1
  14.4 14.9 %all-to-all-done.got_ref = bf16[16,64,512]{2,1,0:T(8,128)(2,1)S(1)} async-done(((bf16[16,64,512]{2,1,0:T(8,128)(2,1)}), bf16[16,64,512]{2,1,0:T(8,128)(2,1)S(1)}, u32[]{:S(2)}, u32[]{:S(2)}) %all-to-all-start) | async-done | bytes 1048608 | tf_op jit(solution)/shard_map/all_to_all | solution.py:740
  29.4 5.0 %all-to-all-start.1 = ((bf16[16,64,512]{2,1,0:T(8,128)(2,1)}), bf16[16,64,512]{2,1,0:T(8,128)(2,1)}, u32[]{:S(2)}, u32[]{:S(2)}) async-start(bf16[16,64,512]{2,1,0:T(8,128)(2,1)} %send_blocks.3), calls=%async_computation.1 | async-start | bytes 2097152 | tf_op jit(solution)/shard_map/all_to_all | solution.py:741
  34.4 0.0 copy-done.2
  34.4 0.0 copy-done
  34.4 0.0 copy-done.1
  34.4 0.0 copy-start.3
  34.4 8.4 %forward_layer.1 = (bf16[4,1024,128]{2,1,0:T(8,128)(2,1)}, bf16[1024,512]{1,0:T(8,128)(2,1)}, bf16[4,1024,128]{2,1,0:T(8,128)(2,1)}, bf16[4,1024,128]{2,1,0:T(8,...) custom-call(s32[16]{0:T(128)S(1)} %bitcast.16, ...), custom_call_target="tpu_custom_call" | custom-call | tf_op jit(solution)/shard_map/forward_layer/pallas_call | solution.py:662
  42.8 8.9 %all-to-all-done.1.grads_ref = bf16[16,64,512]{2,1,0:T(8,128)(2,1)} async-done(((bf16[16,64,512]{2,1,0:T(8,128)(2,1)}), bf16[16,64,512]{2,1,0:T(8,128)(2,1)}, u32[]{:S(2)}, u32[]{:S(2)}) %all-to-all-start.1) | async-done | bytes 1048608 | tf_op jit(solution)/shard_map/all_to_all | solution.py:741
  51.8 0.0 copy-done.3
  51.8 15.3 %backward_layer.1 = (bf16[16,64,512]{2,1,0:T(8,128)(2,1)}, bf16[16,1024,128]{2,1,0:T(8,128)(2,1)}, bf16[512,1024]{1,0:T(8,128)(2,1)}, bf16[1024,512]{1,0:T(8,128)(2,1)}, f32[2,512]{1,0:T(2,128)S(1)}) custom-call(s32[16]{0:T(128)S(1)} %bitcast.17, s32[1]{0:T(128)} %bitcast.1.own_ref, bf16[16,64,512]{2,1,0:T(8,128)(2,1)S(1)} %all-to-all-done.got_ref, ...), custom_call_target="tpu_custom_call" | custom-call | tf_op jit(solution)/shard_map/backward_layer/pallas_call | solution.py:679
  67.1 22.5 %all-to-all-start.2 = ((bf16[16,64,512]{2,1,0:T(8,128)(2,1)}), bf16[16,64,512]{2,1,0:T(8,128)(2,1)}, u32[]{:S(2)}, u32[]{:S(2)}) async-start(bf16[16,64,512]{2,1,0:T(8,128)(2,1)} %get-tuple-element.37), calls=%async_computation.2 | async-start | bytes 2097152 | tf_op jit(solution)/shard_map/all_to_all | solution.py:747
  89.5 8.8 %gradient_terms.1 = (bf16[5632,128]{1,0:T(8,128)(2,1)S(1)}, bf16[5632,128]{1,0:T(8,128)(2,1)S(1)}) custom-call(s32[1]{0:T(128)} %bitcast.1.own_ref, bf16[16,1024,128]{2,1,0:T(8,128)(2,1)} %get-tuple-element.31.d_hidden_in, bf16[512,1024]{1,0:T(8,128)(2,1)} %get-tuple-element.32.scaled_in, bf16[512,1024]{1,0:T(8,128)(2,1)} %get-tuple-element.33.mixed_in, ...), custom_call_target="tpu_custom_call" | custom-call | flops 2684354560 | bytes 10485760 | tf_op jit(solution)/shard_map/gradient_terms/pallas_call | solution.py:713
  98.3 8.6 %all-to-all-done.2.back_ref = bf16[16,64,512]{2,1,0:T(8,128)(2,1)} async-done(((bf16[16,64,512]{2,1,0:T(8,128)(2,1)}), bf16[16,64,512]{2,1,0:T(8,128)(2,1)}, u32[]{:S(2)}, u32[]{:S(2)}) %all-to-all-start.2) | async-done | bytes 1048608 | tf_op jit(solution)/shard_map/all_to_all | solution.py:747
  106.9 0.9 collective-permute-start
  107.8 2.8 %collective-permute-done = bf16[5632,128]{1,0:T(8,128)(2,1)S(1)} collective-permute-done((bf16[5632,128]{1,0:T(8,128)(2,1)S(1)}, bf16[5632,128]{1,0:T(8,128)(2,1)S(1)}, u32[]{:S(2)}, u32[]{:S(2)}) %collective-permute-start) | collective-permute-done | bytes 1441824 | tf_op jit(solution)/shard_map/ppermute | solution.py:752
  110.7 0.4 add_convert_fusion
  111.0 28.0 %all_to_all.25 = bf16[64,88,128]{2,1,0:T(8,128)(2,1)S(1)} all-to-all(bf16[64,88,128]{2,1,0:T(8,128)(2,1)S(1)} %bitcast.21), channel_id=1, replica_groups=mesh['grp'=8,'chip'=8,'core'=2] {'grp','chip'}, dimensions={0} | all-to-all | bytes 2883584 | tf_op jit(solution)/shard_map/all_to_all | solution.py:754
  139.1 0.2 convert_reduce_fusion
  139.3 0.2 broadcast_in_dim.2
  139.5 25.2 %all_to_all.26 = bf16[64,88,128]{2,1,0:T(8,128)(2,1)S(1)} all-to-all(bf16[64,88,128]{2,1,0:T(8,128)(2,1)S(1)} %broadcast_in_dim.2), channel_id=1, replica_groups=mesh['grp'=8,'chip'=8,'core'=2] {'grp','chip'}, dimensions={0} | all-to-all | bytes 2883584 | tf_op jit(solution)/shard_map/all_to_all | solution.py:757
  164.7 3.4 %collective-permute-start.1 = (bf16[5632,128]{1,0:T(8,128)(2,1)S(1)}, bf16[5632,128]{1,0:T(8,128)(2,1)S(1)}, u32[]{:S(2)}, u32[]{:S(2)}) collective-permute-start(bf16[5632,128]{1,0:T(8,128)(2,1)S(1)} %bitcast.11), channel_id=1, source_target_pairs={{0,1},{1,0},{2,3},{3,2},{4,5},{5,4},{6,7},{7,6},{8,9},{9,8},{10,11... | collective-permute-start | bytes 4325384 | tf_op jit(solution)/shard_map/ppermute | solution.py:758
  168.1 2.2 %take_home.1 = bf16[8,64,512]{2,1,0:T(8,128)(2,1)} custom-call(s32[16]{0:T(128)} %bitcast.15, s32[1]{0:T(128)} %bitcast.1.own_ref, bf16[16,64,512]{2,1,0:T(8,128)(2,1)} %all-to-all-done.2.back_ref), custom_call_target="tpu_custom_call" | custom-call | tf_op jit(solution)/shard_map/take_home/pallas_call | solution.py:759
  170.3 0.6 collective-permute-done.1.other_ref
  170.9 3.1 %spread_grads.1 = (f32[512,2048]{1,0:T(8,128)}, f32[512,512]{1,0:T(8,128)}, f32[4,128]{1,0:T(4,128)}, f32[4,128]{1,0:T(4,128)}) custom-call(s32[1]{0:T(128)} %bitcast.1.own_ref, bf16[5632,128]{1,0:T(8,128)(2,1)S(1)} %bitcast.12, bf16[5632,128]{1,0:T(8,128)(2,1)S(1)} %collective-permute-done.1.other_ref), custom_call_target="tpu_custom_call" | custom-call | tf_op jit(solution)/shard_map/spread_grads/pallas_call | solution.py:767
  (1 shorter events, 0.0 us)
Async XLA Ops:
  2.9 26.5 %all-to-all-start = ((bf16[16,64,512]{2,1,0:T(8,128)(2,1)}), bf16[16,64,512]{2,1,0:T(8,128)(2,1)S(1)}, u32[]{:S(2)}, u32[]{:S(2)}) async-start(bf16[16,64,512]{2,1,0:T(8,128)(2,1)} %send_blocks.2), calls=%async_computation | async-start | bytes 2097152 | tf_op jit(solution)/shard_map/all_to_all | solution.py:740
  12.2 22.2 %copy-start.2 = (f32[512]{0:T(512)S(1)}, f32[512]{0:T(512)}, u32[]{:S(2)}) copy-start(f32[512]{0:T(512)} %param.10) | copy-start | bytes 6148
  14.4 19.9 %copy-start = (bf16[512,2048]{1,0:T(8,128)(2,1)S(1)}, bf16[512,2048]{1,0:T(8,128)(2,1)}, u32[]{:S(2)}) copy-start(bf16[512,2048]{1,0:T(8,128)(2,1)} %w_in.1) | copy-start | bytes 6291460
  14.4 19.9 %copy-start.1 = (s32[1,16]{1,0:T(1,128)S(1)}, s32[1,16]{1,0:T(1,128)}, u32[]{:S(2)}) copy-start(s32[1,16]{1,0:T(1,128)} %param.9) | copy-start | bytes 196
  29.4 22.4 %all-to-all-start.1 = ((bf16[16,64,512]{2,1,0:T(8,128)(2,1)}), bf16[16,64,512]{2,1,0:T(8,128)(2,1)}, u32[]{:S(2)}, u32[]{:S(2)}) async-start(bf16[16,64,512]{2,1,0:T(8,128)(2,1)} %send_blocks.3), calls=%async_computation.1 | async-start | bytes 2097152 | tf_op jit(solution)/shard_map/all_to_all | solution.py:741
  34.4 17.4 %copy-start.3 = (f32[512]{0:T(512)S(1)}, f32[512]{0:T(512)}, u32[]{:S(2)}) copy-start(f32[512]{0:T(512)} %param.12) | copy-start | bytes 6148
  67.1 39.8 %all-to-all-start.2 = ((bf16[16,64,512]{2,1,0:T(8,128)(2,1)}), bf16[16,64,512]{2,1,0:T(8,128)(2,1)}, u32[]{:S(2)}, u32[]{:S(2)}) async-start(bf16[16,64,512]{2,1,0:T(8,128)(2,1)} %get-tuple-element.37), calls=%async_computation.2 | async-start | bytes 2097152 | tf_op jit(solution)/shard_map/all_to_all | solution.py:747
  106.9 3.8 %collective-permute-start = (bf16[5632,128]{1,0:T(8,128)(2,1)S(1)}, bf16[5632,128]{1,0:T(8,128)(2,1)S(1)}, u32[]{:S(2)}, u32[]{:S(2)}) collective-permute-start(bf16[5632,128]{1,0:T(8,128)(2,1)S(1)} %get-tuple-element.40), channel_id=1, source_target_pairs={{0,1},{1,0},{2,3},{3,2},{4,5},{5,4},{6,7},{7,6},{8,9},{9,8},{10,11... | collective-permute-start | bytes 4325384 | tf_op jit(solution)/shard_map/ppermute | solution.py:752
  164.7 6.2 %collective-permute-start.1 = (bf16[5632,128]{1,0:T(8,128)(2,1)S(1)}, bf16[5632,128]{1,0:T(8,128)(2,1)S(1)}, u32[]{:S(2)}, u32[]{:S(2)}) collective-permute-start(bf16[5632,128]{1,0:T(8,128)(2,1)S(1)} %bitcast.11), channel_id=1, source_target_pairs={{0,1},{1,0},{2,3},{3,2},{4,5},{5,4},{6,7},{7,6},{8,9},{9,8},{10,11... | collective-permute-start | bytes 4325384 | tf_op jit(solution)/shard_map/ppermute | solution.py:758

commit v7 on v6

--- a/solution.py
+++ b/solution.py
@@ -17,7 +17,7 @@
 ROWS = 1024
 LANES = 128
 PAIRS = 4
-PART = 88
+PART = 80
 HALF = 64 * PART
 EPS = 1e-06
 DEVICES = 128
@@ -296,7 +296,6 @@
     d_hidden_out,
     mixed_out,
     cot_out,
-    gains_ref,
     d_attn_ref,
     d_hidden_ref,
     mixed_ref,
@@ -359,7 +358,6 @@
     for load in loads[1:]:
         load.start()
     history_starts(hist_ref, own, starts, sizes, ranks, first)
-    gains_ref[...] = jnp.zeros((2, D), F32)
     loads[0].wait()
 
     def middle(t, carry):
@@ -376,7 +374,6 @@
         cot_rows_ref[rows, :] = cot
         d_upper = d_mixed * gained
         pull = d_mixed * upper
-        gains_ref[1:2, :] += jnp.sum(pull * normed, axis=0, keepdims=True)
         pull = pull * gain_attn_ref[...]
         d_attn = rstd * (
             pull
@@ -508,7 +505,6 @@
                 [d_hidden_ref[2 * c, rows, :], d_hidden_ref[2 * c + 1, rows, :]], axis=1
             )
             d_scaled += dot_cols(part, w_ref[:, c * 256 : (c + 1) * 256])
-        gains_ref[0:1, :] += jnp.sum(d_scaled * normed, axis=0, keepdims=True)
         pull = d_scaled * gain_in_ref[...]
         d_rows = rstd * (
             pull
@@ -533,7 +529,6 @@
     scaled_in,
     mixed_in,
     cot_in,
-    gains_ref,
     keep_ref,
     send_ref,
     d_hidden_ref,
@@ -571,13 +566,6 @@
         half, place = divmod(piece, 10)
         put(half, pl.ds(place * D, D), values)
 
-    for half in range(2):
-        tail = jnp.concatenate(
-            [gains_ref[half : half + 1, p * LANES : (p + 1) * LANES] for p in range(PAIRS)]
-            + [jnp.zeros((HALF - 10 * D - PAIRS, LANES), F32)],
-            axis=0,
-        )
-        put(half, pl.ds(10 * D, HALF - 10 * D), tail)
     loads[0].wait()
     loads[1].wait()
     for c in range(2):
@@ -593,44 +581,78 @@
         put_piece(2 * c + 1, term[:, LANES:])
 
 
-def spread_kernel(
+def spread_half(half, half_ref, w_ref, w_out_ref, proj_ref, out_ref, wide_ref, sums_ref, sems):
+    in_sum = jnp.zeros((D, LANES), F32)
+    attn_sum = jnp.zeros((D, LANES), F32)
+    for place in range(10):
+        piece = half * 10 + place
+        part = half_ref[place * D : (place + 1) * D, :].astype(F32)
+        wide_ref[place] = part
+        if piece < 16:
+            lanes = pl.ds(piece * LANES, LANES)
+            target = proj_ref.at[:, lanes]
+            in_sum += part * w_ref[:, lanes].astype(F32)
+        else:
+            lanes = pl.ds((piece - 16) * LANES, LANES)
+            target = out_ref.at[:, lanes]
+            attn_sum += part * w_out_ref[:, lanes].astype(F32)
+        pltpu.make_async_copy(wide_ref.at[place], target, sems.at[place]).start()
+    sums_ref[0] = in_sum
+    sums_ref[1] = attn_sum
+
+
+def spread_wait(proj_ref, wide_ref, sems):
+    for place in range(10):
+        target = proj_ref.at[:, pl.ds(place * LANES, LANES)]
+        pltpu.make_async_copy(wide_ref.at[place], target, sems.at[place]).wait()
+
+
+def spread_mine(own_ref, mine_ref, w_ref, w_out_ref, proj_ref, out_ref, sums_ref, wide_ref, sems):
+    core = own_ref[0] & 1
+    for half in range(2):
+
+        @pl.when(core == half)
+        def _(half=half):
+            spread_half(
+                half, mine_ref, w_ref, w_out_ref, proj_ref, out_ref, wide_ref, sums_ref, sems
+            )
+
+    spread_wait(proj_ref, wide_ref, sems)
+
+
+def spread_other(
     own_ref,
-    mine_ref,
     other_ref,
+    w_ref,
+    w_out_ref,
+    gain_in_ref,
+    gain_attn_ref,
+    mine_sums_ref,
+    proj_in,
+    out_in,
     proj_ref,
     out_ref,
-    gain_in_ref,
-    gain_attn_ref,
+    grad_in_ref,
+    grad_attn_ref,
     wide_ref,
+    sums_ref,
     sems,
 ):
     core = own_ref[0] & 1
-
-    def copy(piece):
-        if piece < 16:
-            target = proj_ref.at[:, pl.ds(piece * LANES, LANES)]
-        else:
-            target = out_ref.at[:, pl.ds((piece - 16) * LANES, LANES)]
-        return pltpu.make_async_copy(wide_ref.at[piece], target, sems.at[piece])
-
-    def write(low_ref, high_ref):
-        for piece in range(20):
-            half, place = divmod(piece, 10)
-            wide_ref[piece] = (low_ref, high_ref)[half][place * D : (place + 1) * D, :].astype(F32)
-            copy(piece).start()
-        gain_in_ref[...] = low_ref[10 * D : 10 * D + 16, :].astype(F32)[:PAIRS]
-        gain_attn_ref[...] = high_ref[10 * D : 10 * D + 16, :].astype(F32)[:PAIRS]
-
-    @pl.when(core == 0)
-    def _():
-        write(mine_ref, other_ref)
-
-    @pl.when(core == 1)
-    def _():
-        write(other_ref, mine_ref)
-
-    for piece in range(20):
-        copy(piece).wait()
+    for half in range(2):
+
+        @pl.when(core != half)
+        def _(half=half):
+            spread_half(
+                half, other_ref, w_ref, w_out_ref, proj_ref, out_ref, wide_ref, sums_ref, sems
+            )
+
+    for n, (gain_ref, grad_ref) in enumerate(
+        ((gain_in_ref, grad_in_ref), (gain_attn_ref, grad_attn_ref))
+    ):
+        total = (sums_ref[n] + mine_sums_ref[n]).T
+        grad_ref[...] = jnp.sum(total, axis=0, keepdims=True) / gain_ref[...]
+    spread_wait(proj_ref, wide_ref, sems)
 
 
 def struct(shape, dtype):
@@ -683,10 +705,9 @@
             pltpu.HBM((4 * PAIRS, ROWS, LANES), BF),
             pltpu.HBM((D, ROWS), BF),
             pltpu.HBM((ROWS, D), BF),
-            struct((2, D), F32),
         ),
         in_specs=[SMEM_SPEC] * 2 + [VMEM_SPEC] * 2 + [ANY_SPEC] * 8 + [VMEM_SPEC] * 2,
-        out_specs=(VMEM_SPEC, HBM_SPEC, HBM_SPEC, HBM_SPEC, VMEM_SPEC),
+        out_specs=(VMEM_SPEC, HBM_SPEC, HBM_SPEC, HBM_SPEC),
         scratch_shapes=[
             pltpu.VMEM((PAIRS, ROWS, LANES), BF),
             pltpu.VMEM((4 * PAIRS, ROWS, LANES), BF),
@@ -708,12 +729,12 @@
     )(lens, own, got_rows, got_grads, *saved[:6], w_proj, w_out, gain_in, gain_attn)
 
 
-def gradient_terms(own, d_hidden, scaled, mixed, cot, gains):
+def gradient_terms(own, d_hidden, scaled, mixed, cot):
     half = struct((HALF, LANES), BF)
     return pl.pallas_call(
         terms_kernel,
         out_shape=(half, half),
-        in_specs=[SMEM_SPEC] + [HBM_SPEC] * 4 + [VMEM_SPEC],
+        in_specs=[SMEM_SPEC] + [HBM_SPEC] * 4,
         out_specs=(VMEM_SPEC, VMEM_SPEC),
         scratch_shapes=[
             pltpu.VMEM((4 * PAIRS, ROWS, LANES), BF),
@@ -727,7 +748,7 @@
             flops=10 * ROWS * D * D, transcendentals=0, bytes_accessed=10 * MIB
         ),
         name="gradient_terms",
-    )(own, d_hidden, scaled, mixed, cot, gains)
+    )(own, d_hidden, scaled, mixed, cot)
 
 
 def in_hbm(array):
@@ -740,13 +761,14 @@
     got_rows = lax.all_to_all(send_blocks(lens, own, events), ("chip", "core"), 0, 0, tiled=True)
     got_grads = lax.all_to_all(send_blocks(lens, own, cotangent), ("chip", "core"), 0, 0, tiled=True)
     gain_in = gain_in.reshape(1, D)
+    gain_attn = gain_attn.reshape(1, D)
     saved = [in_hbm(x) for x in forward_layer(lens, own, got_rows, w_proj, gain_in)]
-    send_back, *kept, gains = backward_layer(
-        lens, own, got_rows, got_grads, saved, w_proj, in_hbm(w_out), gain_in, gain_attn.reshape(1, D)
+    send_back, *kept = backward_layer(
+        lens, own, got_rows, got_grads, saved, w_proj, in_hbm(w_out), gain_in, gain_attn
     )
     came_back = lax.all_to_all(send_back, ("chip", "core"), 0, 0, tiled=True)
     d_hidden, mixed, cot = (in_hbm(x) for x in kept)
-    keep, send = gradient_terms(own, d_hidden, saved[6], mixed, cot, gains)
+    keep, send = gradient_terms(own, d_hidden, saved[6], mixed, cot)
     send, came_back = lax.optimization_barrier((send, came_back))
     swap = [(0, 1), (1, 0)]
     other = lax.ppermute(send, "core", swap)
@@ -755,7 +777,6 @@
     total = (jnp.sum(parts.astype(F32), axis=0) * (1.0 / DEVICES)).astype(BF)
     copies = jnp.broadcast_to(total[None], (64, PART, LANES))
     mine = lax.all_to_all(copies, ("grp", "chip"), 0, 0, tiled=True).reshape(HALF, LANES)
-    others = lax.ppermute(mine, "core", swap)
     d_rows = pl.pallas_call(
         home_kernel,
         out_shape=struct((LOCAL, BLOCK, D), BF),
@@ -763,16 +784,31 @@
         out_specs=VMEM_SPEC,
         name="take_home",
     )(lens, own, came_back)
-    gain = struct((PAIRS, LANES), F32)
+    mine, d_rows = lax.optimization_barrier((mine, d_rows))
+    others = lax.ppermute(mine, "core", swap)
+    grads = (struct((D, 4 * D), F32), struct((D, D), F32))
+    scratch = [pltpu.VMEM((10, D, LANES), F32), pltpu.SemaphoreType.DMA((10,))]
+    sums = (2, D, LANES)
+    grad_proj, grad_out, mine_sums = pl.pallas_call(
+        spread_mine,
+        out_shape=grads + (struct(sums, F32),),
+        in_specs=[SMEM_SPEC, VMEM_SPEC, VMEM_SPEC, VMEM_SPEC],
+        out_specs=(ANY_SPEC, ANY_SPEC, VMEM_SPEC),
+        scratch_shapes=scratch,
+        compiler_params=params(24),
+        name="spread_mine",
+    )(own, mine, w_proj, w_out)
+    gain = struct((1, D), F32)
     grad_proj, grad_out, grad_in, grad_attn = pl.pallas_call(
-        spread_kernel,
-        out_shape=(struct((D, 4 * D), F32), struct((D, D), F32), gain, gain),
-        in_specs=[SMEM_SPEC, VMEM_SPEC, VMEM_SPEC],
+        spread_other,
+        out_shape=grads + (gain, gain),
+        in_specs=[SMEM_SPEC] + [VMEM_SPEC] * 6 + [ANY_SPEC] * 2,
         out_specs=(ANY_SPEC, ANY_SPEC, VMEM_SPEC, VMEM_SPEC),
-        scratch_shapes=[pltpu.VMEM((20, D, LANES), F32), pltpu.SemaphoreType.DMA((20,))],
-        compiler_params=params(16),
-        name="spread_grads",
-    )(own, mine, others)
+        scratch_shapes=scratch[:1] + [pltpu.VMEM(sums, F32)] + scratch[1:],
+        input_output_aliases={7: 0, 8: 1},
+        compiler_params=params(24),
+        name="spread_other",
+    )(own, others, w_proj, w_out, gain_in, gain_attn, mine_sums, grad_proj, grad_out)
     return (
         d_rows.reshape(1, LOCAL * BLOCK, D),
         grad_proj,

time: 175 us -> 173 us (0.989)
  Pallas kernels: 42.3 us -> 69.6 us
  blocking collectives: 53.2 us -> 27.5 us
  starting transfers between devices: 41 us -> 28.4 us
  waiting for transfers between devices: 35.9 us -> 42 us
  local copies, waits for them, and re-layouts: 0.21 us -> 3.34 us
    all_to_all x1 -> x0, blocking collectives: 25.2 us -> none  [per_device(): lax.all_to_all(copies, ('grp', 'chip'), 0, 0, tiled=True)]
    pallas_call x1, Pallas kernels: 15.3 us -> 33 us  [backward_layer(): pl.pallas_call(backward_kernel, out_shape=(pltpu.HBM((PEERS, BLOCK, D), B...]
    all_to_all x1, starting transfers between devices: 22.5 us -> 4.88 us  [per_device(): came_back = lax.all_to_all(send_back, ('chip', 'core'), 0, 0, tiled=True)]
    all_to_all x0 -> x1, waiting for transfers between devices: none -> 16.7 us  [per_device(): lax.all_to_all(copies, ('grp', 'chip'), 0, 0, tiled=True)]
    pallas_call x1, Pallas kernels: 8.42 us -> 17.4 us  [forward_layer(): pl.pallas_call(forward_kernel, out_shape=[pltpu.HBM((PAIRS, ROWS, LANES),...]
    all_to_all x1, waiting for transfers between devices: 8.93 us -> 0.01 us  [per_device(): lax.all_to_all(send_blocks(lens, own, cotangent), ('chip', 'core'), 0, 0,...]
    all_to_all x0 -> x1, starting transfers between devices: none -> 4.96 us  [per_device(): lax.all_to_all(copies, ('grp', 'chip'), 0, 0, tiled=True)]
    unnamed x8 -> x12, local copies, waits for them, and re-layouts: 0.02 us -> 2.11 us
  transfers between devices with their start and end apart: 5 -> 6, of which waited for: 5 -> 4; matrix products, arithmetic and copies ran while one was open for 0% -> 0% of each run, Pallas kernels for 12% -> 19%
where the time goes in v7:
time: 173 us; the launch traced here: 172 us
  Pallas kernels  69.6 us (40%)
  waiting for transfers between devices  42 us (24%)
  starting transfers between devices  28.4 us (16%)
  blocking collectives  27.5 us (16%)
  local copies, waits for them, and re-layouts  3.34 us (2%)
    pallas_call x1, Pallas kernels, backward_layer(): pl.pallas_call(backward_kernel, out_shape=(pltpu.HBM((PEERS, BLOCK, D), B...  33 us
    all_to_all x1, blocking collectives, per_device(): lax.all_to_all(chip_sum.reshape(64, PART, LANES), ('grp', 'chip'), 0, 0,...  27.5 us
    pallas_call x1, Pallas kernels, forward_layer(): pl.pallas_call(forward_kernel, out_shape=[pltpu.HBM((PAIRS, ROWS, LANES),...  17.4 us
    all_to_all x1, waiting for transfers between devices, per_device(): lax.all_to_all(copies, ('grp', 'chip'), 0, 0, tiled=True)  16.7 us
    all_to_all x1, waiting for transfers between devices, per_device(): lax.all_to_all(send_blocks(lens, own, events), ('chip', 'core'), 0, 0, ti...  14.9 us
    all_to_all x1, starting transfers between devices, per_device(): lax.all_to_all(send_blocks(lens, own, events), ('chip', 'core'), 0, 0, ti...  9.29 us
    pallas_call x1, Pallas kernels, gradient_terms(): pl.pallas_call(terms_kernel, out_shape=(half, half), in_specs=[SMEM_SPEC]...  8.78 us
    all_to_all x1, waiting for transfers between devices, per_device(): came_back = lax.all_to_all(send_back, ('chip', 'core'), 0, 0, tiled=True)  7.46 us
  transfers between devices with their start and end apart: 6, of which 4 were waited for; matrix products, arithmetic and copies ran while one was open for 0% of the time, Pallas kernels for 19%

profile of v7, /device:TPU:1, one launch (start us, length us, event | category | flops | bytes accessed | tf_op | source)
XLA Modules:
  0.0 172.4 jit_solution(10973302413409345448)
XLA Ops:
  0.6 2.2 %send_blocks.2 = bf16[16,64,512]{2,1,0:T(8,128)(2,1)} custom-call(s32[16]{0:T(128)} %bitcast.16, s32[1]{0:T(128)} %bitcast.own_ref, bf16[8,64,512]{2,1,0:T(8,128)(2,1)} %bitcast.24), custom_call_target="tpu_custom_call" | custom-call | tf_op jit(solution)/shard_map/send_blocks/pallas_call | solution.py:667
  2.9 9.3 %all-to-all-start = ((bf16[16,64,512]{2,1,0:T(8,128)(2,1)}), bf16[16,64,512]{2,1,0:T(8,128)(2,1)S(1)}, u32[]{:S(2)}, u32[]{:S(2)}) async-start(bf16[16,64,512]{2,1,0:T(8,128)(2,1)} %send_blocks.2), calls=%async_computation | async-start | bytes 2097152 | tf_op jit(solution)/shard_map/all_to_all | solution.py:761
  12.2 0.0 copy-start.2
  12.2 2.3 %send_blocks.3 = bf16[16,64,512]{2,1,0:T(8,128)(2,1)} custom-call(s32[16]{0:T(128)} %bitcast.17, s32[1]{0:T(128)} %bitcast.own_ref, bf16[8,64,512]{2,1,0:T(8,128)(2,1)} %bitcast.25), custom_call_target="tpu_custom_call" | custom-call | tf_op jit(solution)/shard_map/send_blocks/pallas_call | solution.py:667
  14.4 0.0 copy-start
  14.4 0.0 copy-start.3
  14.4 14.9 %all-to-all-done.got_ref = bf16[16,64,512]{2,1,0:T(8,128)(2,1)S(1)} async-done(((bf16[16,64,512]{2,1,0:T(8,128)(2,1)}), bf16[16,64,512]{2,1,0:T(8,128)(2,1)S(1)}, u32[]{:S(2)}, u32[]{:S(2)}) %all-to-all-start) | async-done | bytes 1048608 | tf_op jit(solution)/shard_map/all_to_all | solution.py:761
  29.4 5.0 %all-to-all-start.1 = ((bf16[16,64,512]{2,1,0:T(8,128)(2,1)}), bf16[16,64,512]{2,1,0:T(8,128)(2,1)}, u32[]{:S(2)}, u32[]{:S(2)}) async-start(bf16[16,64,512]{2,1,0:T(8,128)(2,1)} %send_blocks.3), calls=%async_computation.1 | async-start | bytes 2097152 | tf_op jit(solution)/shard_map/all_to_all | solution.py:762
  34.4 0.0 copy-done.2
  34.4 0.0 copy-done
  34.4 0.0 copy-done.3
  34.4 0.0 copy-start.4
  34.4 17.4 %forward_layer.1 = (bf16[4,1024,128]{2,1,0:T(8,128)(2,1)}, bf16[1024,512]{1,0:T(8,128)(2,1)}, bf16[4,1024,128]{2,1,0:T(8,128)(2,1)}, bf16[4,1024,128]{2,1,0:T(8,...) custom-call(s32[16]{0:T(128)S(1)} %bitcast.19, ...), custom_call_target="tpu_custom_call" | custom-call | tf_op jit(solution)/shard_map/forward_layer/pallas_call | solution.py:684
  51.8 0.0 all-to-all-done.1.grads_ref
  51.8 0.0 copy-done.4
  51.8 33.0 %backward_layer.1 = (bf16[16,64,512]{2,1,0:T(8,128)(2,1)}, bf16[16,1024,128]{2,1,0:T(8,128)(2,1)}, bf16[512,1024]{1,0:T(8,128)(2,1)}, bf16[1024,512]{1,0:T(8,128)(2,1)}) custom-call(s32[16]{0:T(128)S(1)} %bitcast.20, s32[1]{0:T(128)} %bitcast.own_ref, bf16[16,64,512]{2,1,0:T(8,128)(2,1)S(1)} %all-to-all-done.got_ref, ...), custom_call_target="tpu_custom_call" | custom-call | tf_op jit(solution)/shard_map/backward_layer/pallas_call | solution.py:701
  84.8 4.9 %all-to-all-start.2 = ((bf16[16,64,512]{2,1,0:T(8,128)(2,1)}), bf16[16,64,512]{2,1,0:T(8,128)(2,1)}, u32[]{:S(2)}, u32[]{:S(2)}) async-start(bf16[16,64,512]{2,1,0:T(8,128)(2,1)} %get-tuple-element.41), calls=%async_computation.2 | async-start | bytes 2097152 | tf_op jit(solution)/shard_map/all_to_all | solution.py:769
  89.7 8.8 %gradient_terms.1 = (bf16[5120,128]{1,0:T(8,128)(2,1)S(1)}, bf16[5120,128]{1,0:T(8,128)(2,1)S(1)}) custom-call(s32[1]{0:T(128)} %bitcast.own_ref, bf16[16,1024,128]{2,1,0:T(8,128)(2,1)} %get-tuple-element.35.d_hidden_in, bf16[512,1024]{1,0:T(8,128)(2,1)} %get-tuple-element.36.scaled_in, bf16[512,1024]{1,0:T(8,128)(2,1)} %get-tuple-element.37.mixed_in, ...), custom_call_target="tpu_custom_call" | custom-call | flops 2684354560 | bytes 10485760 | tf_op jit(solution)/shard_map/gradient_terms/pallas_call | solution.py:734
  98.5 0.0 copy-start.5
  98.5 1.0 copy-done.5
  99.5 7.5 %all-to-all-done.2.back_ref = bf16[16,64,512]{2,1,0:T(8,128)(2,1)} async-done(((bf16[16,64,512]{2,1,0:T(8,128)(2,1)}), bf16[16,64,512]{2,1,0:T(8,128)(2,1)}, u32[]{:S(2)}, u32[]{:S(2)}) %all-to-all-start.2) | async-done | bytes 1048608 | tf_op jit(solution)/shard_map/all_to_all | solution.py:769
  107.0 0.9 collective-permute-start
  107.9 2.9 %collective-permute-done = bf16[5120,128]{1,0:T(8,128)(2,1)S(1)} collective-permute-done((bf16[5120,128]{1,0:T(8,128)(2,1)}, bf16[5120,128]{1,0:T(8,128)(2,1)S(1)}, u32[]{:S(2)}, u32[]{:S(2)}) %collective-permute-start) | collective-permute-done | bytes 1310752 | tf_op jit(solution)/shard_map/ppermute | solution.py:774
  110.8 0.3 add_convert_fusion
  111.1 27.5 %all_to_all.25 = bf16[64,80,128]{2,1,0:T(8,128)(2,1)S(1)} all-to-all(bf16[64,80,128]{2,1,0:T(8,128)(2,1)S(1)} %bitcast.23), channel_id=1, replica_groups=mesh['grp'=8,'chip'=8,'core'=2] {'grp','chip'}, dimensions={0} | all-to-all | bytes 2621440 | tf_op jit(solution)/shard_map/all_to_all | solution.py:776
  138.7 0.2 convert_reduce_fusion
  138.9 1.2 broadcast_in_dim.2
  140.1 5.0 %all-to-all-start.4 = ((bf16[64,80,128]{2,1,0:T(8,128)(2,1)}), bf16[64,80,128]{2,1,0:T(8,128)(2,1)S(1)}, u32[]{:S(2)}, u32[]{:S(2)}) async-start(bf16[64,80,128]{2,1,0:T(8,128)(2,1)} %broadcast_in_dim.2), calls=%async_computation.4 | async-start | bytes 2621440 | tf_op jit(solution)/shard_map/all_to_all | solution.py:779
  145.1 2.2 %take_home.1 = bf16[8,64,512]{2,1,0:T(8,128)(2,1)} custom-call(s32[16]{0:T(128)} %bitcast.18, s32[1]{0:T(128)} %bitcast.own_ref, bf16[16,64,512]{2,1,0:T(8,128)(2,1)} %all-to-all-done.2.back_ref), custom_call_target="tpu_custom_call" | custom-call | tf_op jit(solution)/shard_map/take_home/pallas_call | solution.py:780
  147.3 16.7 %all-to-all-done.4 = bf16[64,80,128]{2,1,0:T(8,128)(2,1)S(1)} async-done(((bf16[64,80,128]{2,1,0:T(8,128)(2,1)}), bf16[64,80,128]{2,1,0:T(8,128)(2,1)S(1)}, u32[]{:S(2)}, u32[]{:S(2)}) %all-to-all-start.4) | async-done | bytes 1310752 | tf_op jit(solution)/shard_map/all_to_all | solution.py:779
  164.0 3.4 %collective-permute-start.1 = (bf16[5120,128]{1,0:T(8,128)(2,1)S(1)}, bf16[5120,128]{1,0:T(8,128)(2,1)S(1)}, u32[]{:S(2)}, u32[]{:S(2)}) collective-permute-start(bf16[5120,128]{1,0:T(8,128)(2,1)S(1)} %bitcast.11), channel_id=1, source_target_pairs={{0,1},{1,0},{2,3},{3,2},{4,5},{5,4},{6,7},{7,6},{8,9},{9,8},{10,11... | collective-permute-start | bytes 3932168 | tf_op jit(solution)/shard_map/ppermute | solution.py:788
  167.4 0.0 copy-start.1
  167.4 1.0 copy-done.1
  168.4 1.6 spread_mine.1
  170.0 0.0 collective-permute-done.1.other_ref
  170.1 2.2 %spread_other.1 = (f32[512,2048]{1,0:T(8,128)}, f32[512,512]{1,0:T(8,128)}, f32[1,512]{1,0:T(1,128)}, f32[1,512]{1,0:T(1,128)}) custom-call(s32[1]{0:T(128)} %bitcast.own_ref, bf16[5120,128]{1,0:T(8,128)(2,1)S(1)} %collective-permute-done.1.other_ref, bf16[512,2048]{1,0:T(8,128)(2,1)S(1)} %copy-done, ...), custom_call_target="tpu_custom_call", output_to_operand_aliasing={{0}: (7, {}), {1}: (8, {})} | custom-call | tf_op jit(solution)/shard_map/spread_other/pallas_call | solution.py:802
  (1 shorter events, 0.0 us)
Async XLA Ops:
  2.9 26.5 %all-to-all-start = ((bf16[16,64,512]{2,1,0:T(8,128)(2,1)}), bf16[16,64,512]{2,1,0:T(8,128)(2,1)S(1)}, u32[]{:S(2)}, u32[]{:S(2)}) async-start(bf16[16,64,512]{2,1,0:T(8,128)(2,1)} %send_blocks.2), calls=%async_computation | async-start | bytes 2097152 | tf_op jit(solution)/shard_map/all_to_all | solution.py:761
  12.2 22.2 %copy-start.2 = (f32[512]{0:T(512)S(1)}, f32[512]{0:T(512)}, u32[]{:S(2)}) copy-start(f32[512]{0:T(512)} %param.10) | copy-start | bytes 6148
  14.4 20.0 %copy-start = (bf16[512,2048]{1,0:T(8,128)(2,1)S(1)}, bf16[512,2048]{1,0:T(8,128)(2,1)}, u32[]{:S(2)}) copy-start(bf16[512,2048]{1,0:T(8,128)(2,1)} %w_ref.5) | copy-start | bytes 6291460
  14.4 20.0 %copy-start.3 = (s32[1,16]{1,0:T(1,128)S(1)}, s32[1,16]{1,0:T(1,128)}, u32[]{:S(2)}) copy-start(s32[1,16]{1,0:T(1,128)} %param.9) | copy-start | bytes 196
  29.4 22.4 %all-to-all-start.1 = ((bf16[16,64,512]{2,1,0:T(8,128)(2,1)}), bf16[16,64,512]{2,1,0:T(8,128)(2,1)}, u32[]{:S(2)}, u32[]{:S(2)}) async-start(bf16[16,64,512]{2,1,0:T(8,128)(2,1)} %send_blocks.3), calls=%async_computation.1 | async-start | bytes 2097152 | tf_op jit(solution)/shard_map/all_to_all | solution.py:762
  34.4 17.4 %copy-start.4 = (f32[512]{0:T(512)S(1)}, f32[512]{0:T(512)}, u32[]{:S(2)}) copy-start(f32[512]{0:T(512)} %param.12) | copy-start | bytes 6148
  84.8 22.2 %all-to-all-start.2 = ((bf16[16,64,512]{2,1,0:T(8,128)(2,1)}), bf16[16,64,512]{2,1,0:T(8,128)(2,1)}, u32[]{:S(2)}, u32[]{:S(2)}) async-start(bf16[16,64,512]{2,1,0:T(8,128)(2,1)} %get-tuple-element.41), calls=%async_computation.2 | async-start | bytes 2097152 | tf_op jit(solution)/shard_map/all_to_all | solution.py:769
  98.5 1.1 copy-start.5
  107.0 3.8 %collective-permute-start = (bf16[5120,128]{1,0:T(8,128)(2,1)}, bf16[5120,128]{1,0:T(8,128)(2,1)S(1)}, u32[]{:S(2)}, u32[]{:S(2)}) collective-permute-start(bf16[5120,128]{1,0:T(8,128)(2,1)} %copy-done.5), channel_id=1, source_target_pairs={{0,1},{1,0},{2,3},{3,2},{4,5},{5,4},{6,7},{7,6},{8,9},{9,8},{10,11... | collective-permute-start | bytes 3932168 | tf_op jit(solution)/shard_map/ppermute | solution.py:774
  140.1 23.9 %all-to-all-start.4 = ((bf16[64,80,128]{2,1,0:T(8,128)(2,1)}), bf16[64,80,128]{2,1,0:T(8,128)(2,1)S(1)}, u32[]{:S(2)}, u32[]{:S(2)}) async-start(bf16[64,80,128]{2,1,0:T(8,128)(2,1)} %broadcast_in_dim.2), calls=%async_computation.4 | async-start | bytes 2621440 | tf_op jit(solution)/shard_map/all_to_all | solution.py:779
  164.0 6.0 %collective-permute-start.1 = (bf16[5120,128]{1,0:T(8,128)(2,1)S(1)}, bf16[5120,128]{1,0:T(8,128)(2,1)S(1)}, u32[]{:S(2)}, u32[]{:S(2)}) collective-permute-start(bf16[5120,128]{1,0:T(8,128)(2,1)S(1)} %bitcast.11), channel_id=1, source_target_pairs={{0,1},{1,0},{2,3},{3,2},{4,5},{5,4},{6,7},{7,6},{8,9},{9,8},{10,11... | collective-permute-start | bytes 3932168 | tf_op jit(solution)/shard_map/ppermute | solution.py:788
  167.4 1.0 copy-start.1

commit v8 on v7

--- a/solution.py
+++ b/solution.py
@@ -184,7 +184,7 @@
         normed, _ = normed_rows(tile_rows(got_ref, t, first, count))
         scaled = (normed * gain_ref[...]).astype(BF)
         rows = rows_at(t)
-        scaled_ref[:, rows] = scaled.T
+        scaled_ref[rows, :] = scaled
         for quarter in range(4):
             half = 0.5 * dot(scaled, w_ref[:, quarter * D : (quarter + 1) * D])
             swing = jnp.tanh(half)
@@ -206,7 +206,7 @@
     lax.fori_loop(0, live, project, 0)
 
     def clear(t, carry):
-        scaled_ref[:, rows_at(t)] = jnp.zeros((D, TILE), BF)
+        scaled_ref[rows_at(t), :] = jnp.zeros((TILE, D), BF)
         return carry
 
     lax.fori_loop(live, TILES, clear, 0)
@@ -370,7 +370,7 @@
         cot = tile_rows(grads_ref, t, first, count).astype(BF)
         d_mixed = dot_cols(cot, w_out_ref[...])
         gained = normed * gain_attn_ref[...]
-        mixed_ref[:, rows] = (gained * upper).astype(BF).T
+        mixed_ref[rows, :] = (gained * upper).astype(BF)
         cot_rows_ref[rows, :] = cot
         d_upper = d_mixed * gained
         pull = d_mixed * upper
@@ -391,7 +391,7 @@
 
     def clear(t, carry):
         d_hidden_ref[:, rows_at(t), :] = jnp.zeros((4 * PAIRS, TILE, LANES), BF)
-        mixed_ref[:, rows_at(t)] = jnp.zeros((D, TILE), BF)
+        mixed_ref[rows_at(t), :] = jnp.zeros((TILE, D), BF)
         cot_rows_ref[rows_at(t), :] = jnp.zeros((TILE, D), BF)
         return carry
 
@@ -530,11 +530,13 @@
     mixed_in,
     cot_in,
     keep_ref,
-    send_ref,
+    send_low_ref,
+    send_high_ref,
     d_hidden_ref,
     scaled_ref,
     mixed_ref,
     cot_ref,
+    turned_ref,
     sems,
 ):
     core = own_ref[0] & 1
@@ -551,32 +553,32 @@
     for load in loads:
         load.start()
 
-    def put(half, rows, values):
+    def put_piece(piece, values):
+        half, place = divmod(piece, 10)
         values = values.astype(BF)
 
         @pl.when(core == half)
         def _():
-            keep_ref[rows, :] = values
+            keep_ref[place * D : (place + 1) * D, :] = values
 
         @pl.when(core != half)
         def _():
-            send_ref[rows, :] = values
-
-    def put_piece(piece, values):
-        half, place = divmod(piece, 10)
-        put(half, pl.ds(place * D, D), values)
+            send_ref = (send_low_ref, send_high_ref)[place // 5]
+            send_ref[place % 5 * D : (place % 5 + 1) * D, :] = values
 
     loads[0].wait()
+    turned_ref[...] = mixed_ref[...].T
     loads[1].wait()
     for c in range(2):
-        term = dot(mixed_ref[...], cot_ref[:, c * 256 : (c + 1) * 256])
+        term = dot(turned_ref[...], cot_ref[:, c * 256 : (c + 1) * 256])
         put_piece(16 + 2 * c, term[:, :LANES])
         put_piece(17 + 2 * c, term[:, LANES:])
     loads[2].wait()
+    turned_ref[...] = scaled_ref[...].T
     for c in range(8):
         loads[3 + c].wait()
         part = jnp.concatenate([d_hidden_ref[2 * c], d_hidden_ref[2 * c + 1]], axis=1)
-        term = dot(scaled_ref[...], part)
+        term = dot(turned_ref[...], part)
         put_piece(2 * c, term[:, :LANES])
         put_piece(2 * c + 1, term[:, LANES:])
 
@@ -676,8 +678,7 @@
 def saved_shapes(make):
     pairs = make((PAIRS, ROWS, LANES), BF)
     wide = make((ROWS, D), BF)
-    tall = make((D, ROWS), BF)
-    return [wide, pairs, pairs, pairs, make((4 * PAIRS, ROWS, LANES), BF), tall]
+    return [wide, pairs, pairs, pairs, make((4 * PAIRS, ROWS, LANES), BF), wide]
 
 
 def forward_layer(lens, own, got_rows, w_proj, gain_in):
@@ -703,7 +704,7 @@
         out_shape=(
             pltpu.HBM((PEERS, BLOCK, D), BF),
             pltpu.HBM((4 * PAIRS, ROWS, LANES), BF),
-            pltpu.HBM((D, ROWS), BF),
+            pltpu.HBM((ROWS, D), BF),
             pltpu.HBM((ROWS, D), BF),
         ),
         in_specs=[SMEM_SPEC] * 2 + [VMEM_SPEC] * 2 + [ANY_SPEC] * 8 + [VMEM_SPEC] * 2,
@@ -711,7 +712,7 @@
         scratch_shapes=[
             pltpu.VMEM((PAIRS, ROWS, LANES), BF),
             pltpu.VMEM((4 * PAIRS, ROWS, LANES), BF),
-            pltpu.VMEM((D, ROWS), BF),
+            pltpu.VMEM((ROWS, D), BF),
             pltpu.VMEM((ROWS, D), BF),
             pltpu.VMEM((GROUP, LANES, TILE), F32),
             pltpu.VMEM((PAIRS, LANES, ROWS), BF),
@@ -731,16 +732,18 @@
 
 def gradient_terms(own, d_hidden, scaled, mixed, cot):
     half = struct((HALF, LANES), BF)
+    quarter = pltpu.HBM((HALF // 2, LANES), BF)
     return pl.pallas_call(
         terms_kernel,
-        out_shape=(half, half),
+        out_shape=(half, quarter, quarter),
         in_specs=[SMEM_SPEC] + [HBM_SPEC] * 4,
-        out_specs=(VMEM_SPEC, VMEM_SPEC),
+        out_specs=(VMEM_SPEC,) * 3,
         scratch_shapes=[
             pltpu.VMEM((4 * PAIRS, ROWS, LANES), BF),
+            pltpu.VMEM((ROWS, D), BF),
+            pltpu.VMEM((ROWS, D), BF),
+            pltpu.VMEM((ROWS, D), BF),
             pltpu.VMEM((D, ROWS), BF),
-            pltpu.VMEM((D, ROWS), BF),
-            pltpu.VMEM((ROWS, D), BF),
             pltpu.SemaphoreType.DMA((11,)),
         ],
         compiler_params=params(40),
@@ -768,10 +771,10 @@
     )
     came_back = lax.all_to_all(send_back, ("chip", "core"), 0, 0, tiled=True)
     d_hidden, mixed, cot = (in_hbm(x) for x in kept)
-    keep, send = gradient_terms(own, d_hidden, saved[6], mixed, cot)
-    send, came_back = lax.optimization_barrier((send, came_back))
+    keep, *send = gradient_terms(own, d_hidden, saved[6], mixed, cot)
     swap = [(0, 1), (1, 0)]
-    other = lax.ppermute(send, "core", swap)
+    send[0], came_back = lax.optimization_barrier((send[0], came_back))
+    other = jnp.concatenate([lax.ppermute(part, "core", swap) for part in send])
     chip_sum = (keep.astype(F32) + other.astype(F32)).astype(BF)
     parts = lax.all_to_all(chip_sum.reshape(64, PART, LANES), ("grp", "chip"), 0, 0, tiled=True)
     total = (jnp.sum(parts.astype(F32), axis=0) * (1.0 / DEVICES)).astype(BF)

time: 173 us -> 173 us (level)
  Pallas kernels: 69.6 us -> 44.7 us
  starting transfers between devices: 28.4 us -> 46.2 us
  waiting for transfers between devices: 42 us -> 49.3 us
    all_to_all x1, starting transfers between devices: 4.88 us -> 22.5 us  [per_device(): came_back = lax.all_to_all(send_back, ('chip', 'core'), 0, 0, tiled=True)]
    pallas_call x1, Pallas kernels: 33 us -> 15.4 us  [backward_layer(): pl.pallas_call(backward_kernel, out_shape=(pltpu.HBM((PEERS, BLOCK, D), B...]
    pallas_call x1, Pallas kernels: 17.4 us -> 8.35 us  [forward_layer(): pl.pallas_call(forward_kernel, out_shape=[pltpu.HBM((PAIRS, ROWS, LANES),...]
    all_to_all x1, waiting for transfers between devices: 0.01 us -> 9 us  [per_device(): lax.all_to_all(send_blocks(lens, own, cotangent), ('chip', 'core'), 0, 0,...]
  transfers between devices with their start and end apart: 6 -> 7, of which waited for: 4 -> 5; matrix products, arithmetic and copies ran while one was open for 0% -> 0% of each run, Pallas kernels for 19% -> 14%
where the time goes in v8:
time: 173 us; the launch traced here: 172 us
  waiting for transfers between devices  49.3 us (28%)
  starting transfers between devices  46.2 us (27%)
  Pallas kernels  44.7 us (26%)
  blocking collectives  26.9 us (16%)
  local copies, waits for them, and re-layouts  2.29 us (1%)
    all_to_all x1, blocking collectives, per_device(): lax.all_to_all(chip_sum.reshape(64, PART, LANES), ('grp', 'chip'), 0, 0,...  26.9 us
    all_to_all x1, starting transfers between devices, per_device(): came_back = lax.all_to_all(send_back, ('chip', 'core'), 0, 0, tiled=True)  22.5 us
    all_to_all x1, waiting for transfers between devices, per_device(): lax.all_to_all(copies, ('grp', 'chip'), 0, 0, tiled=True)  16.7 us
    pallas_call x1, Pallas kernels, backward_layer(): pl.pallas_call(backward_kernel, out_shape=(pltpu.HBM((PEERS, BLOCK, D), B...  15.4 us
    all_to_all x1, waiting for transfers between devices, per_device(): lax.all_to_all(send_blocks(lens, own, events), ('chip', 'core'), 0, 0, ti...  14.7 us
    pallas_call x1, Pallas kernels, gradient_terms(): pl.pallas_call(terms_kernel, out_shape=(half, quarter, quarter), in_specs...  10.2 us
    all_to_all x1, starting transfers between devices, per_device(): lax.all_to_all(send_blocks(lens, own, events), ('chip', 'core'), 0, 0, ti...  9.29 us
    all_to_all x1, waiting for transfers between devices, per_device(): lax.all_to_all(send_blocks(lens, own, cotangent), ('chip', 'core'), 0, 0,...  9 us
  transfers between devices with their start and end apart: 7, of which 5 were waited for; matrix products, arithmetic and copies ran while one was open for 0% of the time, Pallas kernels for 14%

profile of v8, /device:TPU:1, one launch (start us, length us, event | category | flops | bytes accessed | tf_op | source)
XLA Modules:
  0.0 172.0 jit_solution(17315316249567329809)
XLA Ops:
  0.6 2.2 %send_blocks.2 = bf16[16,64,512]{2,1,0:T(8,128)(2,1)} custom-call(s32[16]{0:T(128)} %bitcast.16, s32[1]{0:T(128)} %bitcast.own_ref, bf16[8,64,512]{2,1,0:T(8,128)(2,1)} %bitcast.24), custom_call_target="tpu_custom_call" | custom-call | tf_op jit(solution)/shard_map/send_blocks/pallas_call | solution.py:669
  2.9 9.3 %all-to-all-start = ((bf16[16,64,512]{2,1,0:T(8,128)(2,1)}), bf16[16,64,512]{2,1,0:T(8,128)(2,1)S(1)}, u32[]{:S(2)}, u32[]{:S(2)}) async-start(bf16[16,64,512]{2,1,0:T(8,128)(2,1)} %send_blocks.2), calls=%async_computation | async-start | bytes 2097152 | tf_op jit(solution)/shard_map/all_to_all | solution.py:764
  12.2 0.0 copy-start
  12.2 0.0 copy-start.2
  12.2 0.0 copy-start.3
  12.2 2.4 %send_blocks.3 = bf16[16,64,512]{2,1,0:T(8,128)(2,1)} custom-call(s32[16]{0:T(128)} %bitcast.17, s32[1]{0:T(128)} %bitcast.own_ref, bf16[8,64,512]{2,1,0:T(8,128)(2,1)} %bitcast.25), custom_call_target="tpu_custom_call" | custom-call | tf_op jit(solution)/shard_map/send_blocks/pallas_call | solution.py:669
  14.6 14.7 %all-to-all-done.got_ref = bf16[16,64,512]{2,1,0:T(8,128)(2,1)S(1)} async-done(((bf16[16,64,512]{2,1,0:T(8,128)(2,1)}), bf16[16,64,512]{2,1,0:T(8,128)(2,1)S(1)}, u32[]{:S(2)}, u32[]{:S(2)}) %all-to-all-start) | async-done | bytes 1048608 | tf_op jit(solution)/shard_map/all_to_all | solution.py:764
  29.4 5.0 %all-to-all-start.1 = ((bf16[16,64,512]{2,1,0:T(8,128)(2,1)}), bf16[16,64,512]{2,1,0:T(8,128)(2,1)}, u32[]{:S(2)}, u32[]{:S(2)}) async-start(bf16[16,64,512]{2,1,0:T(8,128)(2,1)} %send_blocks.3), calls=%async_computation.1 | async-start | bytes 2097152 | tf_op jit(solution)/shard_map/all_to_all | solution.py:765
  34.4 0.0 copy-start.4
  34.4 0.0 copy-done
  34.4 0.0 copy-done.2
  34.4 0.0 copy-done.3
  34.4 8.4 %forward_layer.1 = (bf16[4,1024,128]{2,1,0:T(8,128)(2,1)}, bf16[1024,512]{1,0:T(8,128)(2,1)}, bf16[4,1024,128]{2,1,0:T(8,128)(2,1)}, bf16[4,1024,128]{2,1,0:T(8,...) custom-call(s32[16]{0:T(128)S(1)} %bitcast.19, ...), custom_call_target="tpu_custom_call" | custom-call | tf_op jit(solution)/shard_map/forward_layer/pallas_call | solution.py:685
  42.8 9.0 %all-to-all-done.1.grads_ref = bf16[16,64,512]{2,1,0:T(8,128)(2,1)} async-done(((bf16[16,64,512]{2,1,0:T(8,128)(2,1)}), bf16[16,64,512]{2,1,0:T(8,128)(2,1)}, u32[]{:S(2)}, u32[]{:S(2)}) %all-to-all-start.1) | async-done | bytes 1048608 | tf_op jit(solution)/shard_map/all_to_all | solution.py:765
  51.8 0.0 copy-done.4
  51.8 15.4 %backward_layer.1 = (bf16[16,64,512]{2,1,0:T(8,128)(2,1)}, bf16[16,1024,128]{2,1,0:T(8,128)(2,1)}, bf16[1024,512]{1,0:T(8,128)(2,1)}, bf16[1024,512]{1,0:T(8,128)(2,1)}) custom-call(s32[16]{0:T(128)S(1)} %bitcast.20, s32[1]{0:T(128)} %bitcast.own_ref, bf16[16,64,512]{2,1,0:T(8,128)(2,1)S(1)} %all-to-all-done.got_ref, ...), custom_call_target="tpu_custom_call" | custom-call | tf_op jit(solution)/shard_map/backward_layer/pallas_call | solution.py:702
  67.2 22.5 %all-to-all-start.2 = ((bf16[16,64,512]{2,1,0:T(8,128)(2,1)}), bf16[16,64,512]{2,1,0:T(8,128)(2,1)}, u32[]{:S(2)}, u32[]{:S(2)}) async-start(bf16[16,64,512]{2,1,0:T(8,128)(2,1)} %get-tuple-element.42), calls=%async_computation.2 | async-start | bytes 2097152 | tf_op jit(solution)/shard_map/all_to_all | solution.py:772
  89.7 10.2 %gradient_terms.1 = (bf16[5120,128]{1,0:T(8,128)(2,1)S(1)}, bf16[2560,128]{1,0:T(8,128)(2,1)}, bf16[2560,128]{1,0:T(8,128)(2,1)}) custom-call(s32[1]{0:T(128)} %bitcast.own_ref, bf16[16,1024,128]{2,1,0:T(8,128)(2,1)} %get-tuple-element.36.d_hidden_in, bf16[1024,512]{1,0:T(8,128)(2,1)} %get-tuple-element.37.scaled_in, ...), custom_call_target="tpu_custom_call" | custom-call | flops 2684354560 | bytes 10485760 | tf_op jit(solution)/shard_map/gradient_terms/pallas_call | solution.py:736
  99.9 0.2 collective-permute-start.1
  100.1 6.9 %all-to-all-done.2.back_ref = bf16[16,64,512]{2,1,0:T(8,128)(2,1)} async-done(((bf16[16,64,512]{2,1,0:T(8,128)(2,1)}), bf16[16,64,512]{2,1,0:T(8,128)(2,1)}, u32[]{:S(2)}, u32[]{:S(2)}) %all-to-all-start.2) | async-done | bytes 1048608 | tf_op jit(solution)/shard_map/all_to_all | solution.py:772
  107.0 0.9 collective-permute-start
  107.9 0.0 collective-permute-done.1
  107.9 1.9 %collective-permute-done = bf16[2560,128]{1,0:T(8,128)(2,1)S(1)} collective-permute-done((bf16[2560,128]{1,0:T(8,128)(2,1)}, bf16[2560,128]{1,0:T(8,128)(2,1)S(1)}, u32[]{:S(2)}, u32[]{:S(2)}) %collective-permute-start) | collective-permute-done | bytes 655392 | tf_op jit(solution)/shard_map/ppermute | solution.py:777
  109.8 1.5 add_convert_fusion
  111.3 26.9 %all_to_all.25 = bf16[64,80,128]{2,1,0:T(8,128)(2,1)S(1)} all-to-all(bf16[64,80,128]{2,1,0:T(8,128)(2,1)S(1)} %bitcast.23), channel_id=1, replica_groups=mesh['grp'=8,'chip'=8,'core'=2] {'grp','chip'}, dimensions={0} | all-to-all | bytes 2621440 | tf_op jit(solution)/shard_map/all_to_all | solution.py:779
  138.2 0.2 convert_reduce_fusion
  138.4 1.2 broadcast_in_dim.2
  139.7 5.0 %all-to-all-start.4 = ((bf16[64,80,128]{2,1,0:T(8,128)(2,1)}), bf16[64,80,128]{2,1,0:T(8,128)(2,1)S(1)}, u32[]{:S(2)}, u32[]{:S(2)}) async-start(bf16[64,80,128]{2,1,0:T(8,128)(2,1)} %broadcast_in_dim.2), calls=%async_computation.4 | async-start | bytes 2621440 | tf_op jit(solution)/shard_map/all_to_all | solution.py:782
  144.6 2.2 %take_home.1 = bf16[8,64,512]{2,1,0:T(8,128)(2,1)} custom-call(s32[16]{0:T(128)} %bitcast.18, s32[1]{0:T(128)} %bitcast.own_ref, bf16[16,64,512]{2,1,0:T(8,128)(2,1)} %all-to-all-done.2.back_ref), custom_call_target="tpu_custom_call" | custom-call | tf_op jit(solution)/shard_map/take_home/pallas_call | solution.py:783
  146.8 16.7 %all-to-all-done.4 = bf16[64,80,128]{2,1,0:T(8,128)(2,1)S(1)} async-done(((bf16[64,80,128]{2,1,0:T(8,128)(2,1)}), bf16[64,80,128]{2,1,0:T(8,128)(2,1)S(1)}, u32[]{:S(2)}, u32[]{:S(2)}) %all-to-all-start.4) | async-done | bytes 1310752 | tf_op jit(solution)/shard_map/all_to_all | solution.py:782
  163.6 3.4 %collective-permute-start.2 = (bf16[5120,128]{1,0:T(8,128)(2,1)S(1)}, bf16[5120,128]{1,0:T(8,128)(2,1)S(1)}, u32[]{:S(2)}, u32[]{:S(2)}) collective-permute-start(bf16[5120,128]{1,0:T(8,128)(2,1)S(1)} %bitcast.11), channel_id=1, source_target_pairs={{0,1},{1,0},{2,3},{3,2},{4,5},{5,4},{6,7},{7,6},{8,9},{9,8},{10,11... | collective-permute-start | bytes 3932168 | tf_op jit(solution)/shard_map/ppermute | solution.py:791
  166.9 0.0 copy-start.1
  166.9 1.0 copy-done.1
  168.0 1.6 spread_mine.1
  169.6 0.0 collective-permute-done.2.other_ref
  169.6 2.2 %spread_other.1 = (f32[512,2048]{1,0:T(8,128)}, f32[512,512]{1,0:T(8,128)}, f32[1,512]{1,0:T(1,128)}, f32[1,512]{1,0:T(1,128)}) custom-call(s32[1]{0:T(128)} %bitcast.own_ref, bf16[5120,128]{1,0:T(8,128)(2,1)S(1)} %collective-permute-done.2.other_ref, bf16[512,2048]{1,0:T(8,128)(2,1)S(1)} %copy-done, ...), custom_call_target="tpu_custom_call", output_to_operand_aliasing={{0}: (7, {}), {1}: (8, {})} | custom-call | tf_op jit(solution)/shard_map/spread_other/pallas_call | solution.py:805
  (1 shorter events, 0.0 us)
Async XLA Ops:
  2.9 26.5 %all-to-all-start = ((bf16[16,64,512]{2,1,0:T(8,128)(2,1)}), bf16[16,64,512]{2,1,0:T(8,128)(2,1)S(1)}, u32[]{:S(2)}, u32[]{:S(2)}) async-start(bf16[16,64,512]{2,1,0:T(8,128)(2,1)} %send_blocks.2), calls=%async_computation | async-start | bytes 2097152 | tf_op jit(solution)/shard_map/all_to_all | solution.py:764
  12.2 22.2 %copy-start = (bf16[512,2048]{1,0:T(8,128)(2,1)S(1)}, bf16[512,2048]{1,0:T(8,128)(2,1)}, u32[]{:S(2)}) copy-start(bf16[512,2048]{1,0:T(8,128)(2,1)} %w_ref.5) | copy-start | bytes 6291460
  12.2 22.2 %copy-start.2 = (f32[512]{0:T(512)S(1)}, f32[512]{0:T(512)}, u32[]{:S(2)}) copy-start(f32[512]{0:T(512)} %param.10) | copy-start | bytes 6148
  12.2 22.2 %copy-start.3 = (s32[1,16]{1,0:T(1,128)S(1)}, s32[1,16]{1,0:T(1,128)}, u32[]{:S(2)}) copy-start(s32[1,16]{1,0:T(1,128)} %param.9) | copy-start | bytes 196
  29.4 22.4 %all-to-all-start.1 = ((bf16[16,64,512]{2,1,0:T(8,128)(2,1)}), bf16[16,64,512]{2,1,0:T(8,128)(2,1)}, u32[]{:S(2)}, u32[]{:S(2)}) async-start(bf16[16,64,512]{2,1,0:T(8,128)(2,1)} %send_blocks.3), calls=%async_computation.1 | async-start | bytes 2097152 | tf_op jit(solution)/shard_map/all_to_all | solution.py:765
  34.4 17.4 %copy-start.4 = (f32[512]{0:T(512)S(1)}, f32[512]{0:T(512)}, u32[]{:S(2)}) copy-start(f32[512]{0:T(512)} %param.12) | copy-start | bytes 6148
  67.2 39.8 %all-to-all-start.2 = ((bf16[16,64,512]{2,1,0:T(8,128)(2,1)}), bf16[16,64,512]{2,1,0:T(8,128)(2,1)}, u32[]{:S(2)}, u32[]{:S(2)}) async-start(bf16[16,64,512]{2,1,0:T(8,128)(2,1)} %get-tuple-element.42), calls=%async_computation.2 | async-start | bytes 2097152 | tf_op jit(solution)/shard_map/all_to_all | solution.py:772
  99.9 8.0 %collective-permute-start.1 = (bf16[2560,128]{1,0:T(8,128)(2,1)}, bf16[2560,128]{1,0:T(8,128)(2,1)}, u32[]{:S(2)}, u32[]{:S(2)}) collective-permute-start(bf16[2560,128]{1,0:T(8,128)(2,1)} %get-tuple-element.44), channel_id=1, source_target_pairs={{0,1},{1,0},{2,3},{3,2},{4,5},{5,4},{6,7},{7,6},{8,9},{9,8},{10,11... | collective-permute-start | bytes 1966088 | tf_op jit(solution)/shard_map/ppermute | solution.py:777
  107.0 2.8 %collective-permute-start = (bf16[2560,128]{1,0:T(8,128)(2,1)}, bf16[2560,128]{1,0:T(8,128)(2,1)S(1)}, u32[]{:S(2)}, u32[]{:S(2)}) collective-permute-start(bf16[2560,128]{1,0:T(8,128)(2,1)} %get-tuple-element.43), channel_id=1, source_target_pairs={{0,1},{1,0},{2,3},{3,2},{4,5},{5,4},{6,7},{7,6},{8,9},{9,8},{10,11... | collective-permute-start | bytes 1966088 | tf_op jit(solution)/shard_map/ppermute | solution.py:777
  139.7 23.9 %all-to-all-start.4 = ((bf16[64,80,128]{2,1,0:T(8,128)(2,1)}), bf16[64,80,128]{2,1,0:T(8,128)(2,1)S(1)}, u32[]{:S(2)}, u32[]{:S(2)}) async-start(bf16[64,80,128]{2,1,0:T(8,128)(2,1)} %broadcast_in_dim.2), calls=%async_computation.4 | async-start | bytes 2621440 | tf_op jit(solution)/shard_map/all_to_all | solution.py:782
  163.6 6.0 %collective-permute-start.2 = (bf16[5120,128]{1,0:T(8,128)(2,1)S(1)}, bf16[5120,128]{1,0:T(8,128)(2,1)S(1)}, u32[]{:S(2)}, u32[]{:S(2)}) collective-permute-start(bf16[5120,128]{1,0:T(8,128)(2,1)S(1)} %bitcast.11), channel_id=1, source_target_pairs={{0,1},{1,0},{2,3},{3,2},{4,5},{5,4},{6,7},{7,6},{8,9},{9,8},{10,11... | collective-permute-start | bytes 3932168 | tf_op jit(solution)/shard_map/ppermute | solution.py:791
  166.9 1.0 copy-start.1

commit v9 on v8

--- a/solution.py
+++ b/solution.py
@@ -280,8 +280,8 @@
 def backward_kernel(
     len_ref,
     own_ref,
-    got_ref,
-    grads_ref,
+    got_in,
+    grads_in,
     attn_in,
     upper_in,
     values_in,
@@ -315,8 +315,13 @@
     slope_ref,
     w_ref,
     w_out_ref,
+    got_ref,
+    grads_ref,
 ):
     own = own_ref[0]
+    load_grads = pltpu.make_async_copy(grads_in, grads_ref, load_sems.at[9])
+    load_grads.start()
+    load_got = pltpu.make_async_copy(got_in, got_ref, load_sems.at[10])
     starts, sizes, ranks, first, count = holdings(len_ref, own)
     live = (count + 3) // 4
     early = pl.ds(0, PAIRS)
@@ -357,8 +362,10 @@
     lax.fori_loop(0, live, request, 0)
     for load in loads[1:]:
         load.start()
+    load_got.start()
     history_starts(hist_ref, own, starts, sizes, ranks, first)
     loads[0].wait()
+    load_grads.wait()
 
     def middle(t, carry):
         rows = rows_at(t)
@@ -495,6 +502,7 @@
     saves.append(pltpu.make_async_copy(d_hidden_ref, d_hidden_out, load_sems.at[6]))
     saves[-1].start()
     loads[5].wait()
+    load_got.wait()
 
     def final(t, carry):
         rows = rows_at(t)
@@ -707,7 +715,7 @@
             pltpu.HBM((ROWS, D), BF),
             pltpu.HBM((ROWS, D), BF),
         ),
-        in_specs=[SMEM_SPEC] * 2 + [VMEM_SPEC] * 2 + [ANY_SPEC] * 8 + [VMEM_SPEC] * 2,
+        in_specs=[SMEM_SPEC] * 2 + [ANY_SPEC] * 10 + [VMEM_SPEC] * 2,
         out_specs=(VMEM_SPEC, HBM_SPEC, HBM_SPEC, HBM_SPEC),
         scratch_shapes=[
             pltpu.VMEM((PAIRS, ROWS, LANES), BF),
@@ -720,11 +728,12 @@
             pltpu.VMEM((GROUP, ROWS, LANES), F32),
             pltpu.SMEM((LEN_BLK,), jnp.int32),
             pltpu.SemaphoreType.DMA((3, TILES)),
-            pltpu.SemaphoreType.DMA((9,)),
+            pltpu.SemaphoreType.DMA((11,)),
             pltpu.VMEM((PAIRS, ROWS, LANES), BF),
         ]
         + saved_shapes(pltpu.VMEM)[:5]
-        + [pltpu.VMEM((D, 4 * D), BF), pltpu.VMEM((D, D), BF)],
+        + [pltpu.VMEM((D, 4 * D), BF), pltpu.VMEM((D, D), BF)]
+        + [pltpu.VMEM((PEERS, BLOCK, D), BF)] * 2,
         compiler_params=params(44),
         name="backward_layer",
     )(lens, own, got_rows, got_grads, *saved[:6], w_proj, w_out, gain_in, gain_attn)

time: 173 us -> 173 us (level)
  Pallas kernels: 44.7 us -> 55.6 us
  starting transfers between devices: 46.2 us -> 38.6 us
  waiting for transfers between devices: 49.3 us -> 45.6 us
    all_to_all x1, starting transfers between devices: 22.5 us -> 14.8 us  [per_device(): came_back = lax.all_to_all(send_back, ('chip', 'core'), 0, 0, tiled=True)]
    pallas_call x1, Pallas kernels: 15.4 us -> 22.6 us  [backward_layer(): pl.pallas_call(backward_kernel, out_shape=(pltpu.HBM((PEERS, BLOCK, D), B...]
    pallas_call x1, Pallas kernels: 8.35 us -> 12 us  [forward_layer(): pl.pallas_call(forward_kernel, out_shape=[pltpu.HBM((PAIRS, ROWS, LANES),...]
    all_to_all x1, waiting for transfers between devices: 9 us -> 5.31 us  [per_device(): lax.all_to_all(send_blocks(lens, own, cotangent), ('chip', 'core'), 0, 0,...]
  transfers between devices with their start and end apart: 7 -> 7, of which waited for: 5 -> 5; matrix products, arithmetic and copies ran while one was open for 0% -> 0% of each run, Pallas kernels for 14% -> 17%
where the time goes in v9:
time: 173 us; the launch traced here: 172 us
  Pallas kernels  55.6 us (32%)
  waiting for transfers between devices  45.6 us (26%)
  starting transfers between devices  38.6 us (22%)
  blocking collectives  27.6 us (16%)
  local copies, waits for them, and re-layouts  2.29 us (1%)
    all_to_all x1, blocking collectives, per_device(): lax.all_to_all(chip_sum.reshape(64, PART, LANES), ('grp', 'chip'), 0, 0,...  27.6 us
    pallas_call x1, Pallas kernels, backward_layer(): pl.pallas_call(backward_kernel, out_shape=(pltpu.HBM((PEERS, BLOCK, D), B...  22.6 us
    all_to_all x1, waiting for transfers between devices, per_device(): lax.all_to_all(copies, ('grp', 'chip'), 0, 0, tiled=True)  16.7 us
    all_to_all x1, starting transfers between devices, per_device(): came_back = lax.all_to_all(send_back, ('chip', 'core'), 0, 0, tiled=True)  14.8 us
    all_to_all x1, waiting for transfers between devices, per_device(): lax.all_to_all(send_blocks(lens, own, events), ('chip', 'core'), 0, 0, ti...  14.7 us
    pallas_call x1, Pallas kernels, forward_layer(): pl.pallas_call(forward_kernel, out_shape=[pltpu.HBM((PAIRS, ROWS, LANES),...  12 us
    pallas_call x1, Pallas kernels, gradient_terms(): pl.pallas_call(terms_kernel, out_shape=(half, quarter, quarter), in_specs...  10.2 us
    all_to_all x1, starting transfers between devices, per_device(): lax.all_to_all(send_blocks(lens, own, events), ('chip', 'core'), 0, 0, ti...  9.29 us
  transfers between devices with their start and end apart: 7, of which 5 were waited for; matrix products, arithmetic and copies ran while one was open for 0% of the time, Pallas kernels for 17%

profile of v9, /device:TPU:1, one launch (start us, length us, event | category | flops | bytes accessed | tf_op | source)
XLA Modules:
  0.0 172.2 jit_solution(5205188693703195183)
XLA Ops:
  0.6 2.2 %send_blocks.2 = bf16[16,64,512]{2,1,0:T(8,128)(2,1)} custom-call(s32[16]{0:T(128)} %bitcast.16, s32[1]{0:T(128)} %bitcast.own_ref, bf16[8,64,512]{2,1,0:T(8,128)(2,1)} %bitcast.24), custom_call_target="tpu_custom_call" | custom-call | tf_op jit(solution)/shard_map/send_blocks/pallas_call | solution.py:677
  2.9 9.3 %all-to-all-start = ((bf16[16,64,512]{2,1,0:T(8,128)(2,1)}), bf16[16,64,512]{2,1,0:T(8,128)(2,1)S(1)}, u32[]{:S(2)}, u32[]{:S(2)}) async-start(bf16[16,64,512]{2,1,0:T(8,128)(2,1)} %send_blocks.2), calls=%async_computation | async-start | bytes 2097152 | tf_op jit(solution)/shard_map/all_to_all | solution.py:773
  12.2 0.0 copy-start
  12.2 0.0 copy-start.2
  12.2 0.0 copy-start.3
  12.2 2.4 %send_blocks.3 = bf16[16,64,512]{2,1,0:T(8,128)(2,1)} custom-call(s32[16]{0:T(128)} %bitcast.17, s32[1]{0:T(128)} %bitcast.own_ref, bf16[8,64,512]{2,1,0:T(8,128)(2,1)} %bitcast.25), custom_call_target="tpu_custom_call" | custom-call | tf_op jit(solution)/shard_map/send_blocks/pallas_call | solution.py:677
  14.6 14.7 %all-to-all-done.got_ref.got_in = bf16[16,64,512]{2,1,0:T(8,128)(2,1)S(1)} async-done(((bf16[16,64,512]{2,1,0:T(8,128)(2,1)}), bf16[16,64,512]{2,1,0:T(8,128)(2,1)S(1)}, u32[]{:S(2)}, u32[]{:S(2)}) %all-to-all-start) | async-done | bytes 1048608 | tf_op jit(solution)/shard_map/all_to_all | solution.py:773
  29.4 5.0 %all-to-all-start.1 = ((bf16[16,64,512]{2,1,0:T(8,128)(2,1)}), bf16[16,64,512]{2,1,0:T(8,128)(2,1)}, u32[]{:S(2)}, u32[]{:S(2)}) async-start(bf16[16,64,512]{2,1,0:T(8,128)(2,1)} %send_blocks.3), calls=%async_computation.1 | async-start | bytes 2097152 | tf_op jit(solution)/shard_map/all_to_all | solution.py:774
  34.4 0.0 copy-start.4
  34.4 0.0 copy-done
  34.4 0.0 copy-done.2
  34.4 0.0 copy-done.3
  34.4 12.0 %forward_layer.1 = (bf16[4,1024,128]{2,1,0:T(8,128)(2,1)}, bf16[1024,512]{1,0:T(8,128)(2,1)}, bf16[4,1024,128]{2,1,0:T(8,128)(2,1)}, bf16[4,1024,128]{2,1,0:T(8,...) custom-call(s32[16]{0:T(128)S(1)} %bitcast.19, ...), custom_call_target="tpu_custom_call" | custom-call | tf_op jit(solution)/shard_map/forward_layer/pallas_call | solution.py:693
  46.4 5.3 %all-to-all-done.1.grads_in = bf16[16,64,512]{2,1,0:T(8,128)(2,1)} async-done(((bf16[16,64,512]{2,1,0:T(8,128)(2,1)}), bf16[16,64,512]{2,1,0:T(8,128)(2,1)}, u32[]{:S(2)}, u32[]{:S(2)}) %all-to-all-start.1) | async-done | bytes 1048608 | tf_op jit(solution)/shard_map/all_to_all | solution.py:774
  51.8 0.0 copy-done.4
  51.8 22.6 %backward_layer.1 = (bf16[16,64,512]{2,1,0:T(8,128)(2,1)}, bf16[16,1024,128]{2,1,0:T(8,128)(2,1)}, bf16[1024,512]{1,0:T(8,128)(2,1)}, bf16[1024,512]{1,0:T(8,128)(2,1)}) custom-call(s32[16]{0:T(128)S(1)} %bitcast.20, s32[1]{0:T(128)} %bitcast.own_ref, bf16[16,64,512]{2,1,0:T(8,128)(2,1)S(1)} %all-to-all-done.got_ref.got_in, ...), custom_call_target="tpu_custom_call" | custom-call | tf_op jit(solution)/shard_map/backward_layer/pallas_call | solution.py:710
  74.4 14.8 %all-to-all-start.2 = ((bf16[16,64,512]{2,1,0:T(8,128)(2,1)}), bf16[16,64,512]{2,1,0:T(8,128)(2,1)}, u32[]{:S(2)}, u32[]{:S(2)}) async-start(bf16[16,64,512]{2,1,0:T(8,128)(2,1)} %get-tuple-element.42), calls=%async_computation.2 | async-start | bytes 2097152 | tf_op jit(solution)/shard_map/all_to_all | solution.py:781
  89.2 10.2 %gradient_terms.1 = (bf16[5120,128]{1,0:T(8,128)(2,1)S(1)}, bf16[2560,128]{1,0:T(8,128)(2,1)}, bf16[2560,128]{1,0:T(8,128)(2,1)}) custom-call(s32[1]{0:T(128)} %bitcast.own_ref, bf16[16,1024,128]{2,1,0:T(8,128)(2,1)} %get-tuple-element.36.d_hidden_in, bf16[1024,512]{1,0:T(8,128)(2,1)} %get-tuple-element.37.scaled_in, ...), custom_call_target="tpu_custom_call" | custom-call | flops 2684354560 | bytes 10485760 | tf_op jit(solution)/shard_map/gradient_terms/pallas_call | solution.py:745
  99.4 0.2 collective-permute-start.1
  99.7 6.9 %all-to-all-done.2.back_ref = bf16[16,64,512]{2,1,0:T(8,128)(2,1)} async-done(((bf16[16,64,512]{2,1,0:T(8,128)(2,1)}), bf16[16,64,512]{2,1,0:T(8,128)(2,1)}, u32[]{:S(2)}, u32[]{:S(2)}) %all-to-all-start.2) | async-done | bytes 1048608 | tf_op jit(solution)/shard_map/all_to_all | solution.py:781
  106.5 0.9 collective-permute-start
  107.5 0.0 collective-permute-done.1
  107.5 1.9 %collective-permute-done = bf16[2560,128]{1,0:T(8,128)(2,1)S(1)} collective-permute-done((bf16[2560,128]{1,0:T(8,128)(2,1)}, bf16[2560,128]{1,0:T(8,128)(2,1)S(1)}, u32[]{:S(2)}, u32[]{:S(2)}) %collective-permute-start) | collective-permute-done | bytes 655392 | tf_op jit(solution)/shard_map/ppermute | solution.py:786
  109.4 1.5 add_convert_fusion
  110.9 27.6 %all_to_all.25 = bf16[64,80,128]{2,1,0:T(8,128)(2,1)S(1)} all-to-all(bf16[64,80,128]{2,1,0:T(8,128)(2,1)S(1)} %bitcast.23), channel_id=1, replica_groups=mesh['grp'=8,'chip'=8,'core'=2] {'grp','chip'}, dimensions={0} | all-to-all | bytes 2621440 | tf_op jit(solution)/shard_map/all_to_all | solution.py:788
  138.5 0.2 convert_reduce_fusion
  138.7 1.2 broadcast_in_dim.2
  139.9 5.0 %all-to-all-start.4 = ((bf16[64,80,128]{2,1,0:T(8,128)(2,1)}), bf16[64,80,128]{2,1,0:T(8,128)(2,1)S(1)}, u32[]{:S(2)}, u32[]{:S(2)}) async-start(bf16[64,80,128]{2,1,0:T(8,128)(2,1)} %broadcast_in_dim.2), calls=%async_computation.4 | async-start | bytes 2621440 | tf_op jit(solution)/shard_map/all_to_all | solution.py:791
  144.9 2.2 %take_home.1 = bf16[8,64,512]{2,1,0:T(8,128)(2,1)} custom-call(s32[16]{0:T(128)} %bitcast.18, s32[1]{0:T(128)} %bitcast.own_ref, bf16[16,64,512]{2,1,0:T(8,128)(2,1)} %all-to-all-done.2.back_ref), custom_call_target="tpu_custom_call" | custom-call | tf_op jit(solution)/shard_map/take_home/pallas_call | solution.py:792
  147.1 16.7 %all-to-all-done.4 = bf16[64,80,128]{2,1,0:T(8,128)(2,1)S(1)} async-done(((bf16[64,80,128]{2,1,0:T(8,128)(2,1)}), bf16[64,80,128]{2,1,0:T(8,128)(2,1)S(1)}, u32[]{:S(2)}, u32[]{:S(2)}) %all-to-all-start.4) | async-done | bytes 1310752 | tf_op jit(solution)/shard_map/all_to_all | solution.py:791
  163.8 3.4 %collective-permute-start.2 = (bf16[5120,128]{1,0:T(8,128)(2,1)S(1)}, bf16[5120,128]{1,0:T(8,128)(2,1)S(1)}, u32[]{:S(2)}, u32[]{:S(2)}) collective-permute-start(bf16[5120,128]{1,0:T(8,128)(2,1)S(1)} %bitcast.11), channel_id=1, source_target_pairs={{0,1},{1,0},{2,3},{3,2},{4,5},{5,4},{6,7},{7,6},{8,9},{9,8},{10,11... | collective-permute-start | bytes 3932168 | tf_op jit(solution)/shard_map/ppermute | solution.py:800
  167.2 0.0 copy-start.1
  167.2 1.0 copy-done.1
  168.2 1.6 spread_mine.1
  169.8 0.0 collective-permute-done.2.other_ref
  169.9 2.2 %spread_other.1 = (f32[512,2048]{1,0:T(8,128)}, f32[512,512]{1,0:T(8,128)}, f32[1,512]{1,0:T(1,128)}, f32[1,512]{1,0:T(1,128)}) custom-call(s32[1]{0:T(128)} %bitcast.own_ref, bf16[5120,128]{1,0:T(8,128)(2,1)S(1)} %collective-permute-done.2.other_ref, bf16[512,2048]{1,0:T(8,128)(2,1)S(1)} %copy-done, ...), custom_call_target="tpu_custom_call", output_to_operand_aliasing={{0}: (7, {}), {1}: (8, {})} | custom-call | tf_op jit(solution)/shard_map/spread_other/pallas_call | solution.py:814
  (1 shorter events, 0.0 us)
Async XLA Ops:
  2.9 26.5 %all-to-all-start = ((bf16[16,64,512]{2,1,0:T(8,128)(2,1)}), bf16[16,64,512]{2,1,0:T(8,128)(2,1)S(1)}, u32[]{:S(2)}, u32[]{:S(2)}) async-start(bf16[16,64,512]{2,1,0:T(8,128)(2,1)} %send_blocks.2), calls=%async_computation | async-start | bytes 2097152 | tf_op jit(solution)/shard_map/all_to_all | solution.py:773
  12.2 22.2 %copy-start = (bf16[512,2048]{1,0:T(8,128)(2,1)S(1)}, bf16[512,2048]{1,0:T(8,128)(2,1)}, u32[]{:S(2)}) copy-start(bf16[512,2048]{1,0:T(8,128)(2,1)} %w_ref.5) | copy-start | bytes 6291460
  12.2 22.2 %copy-start.2 = (f32[512]{0:T(512)S(1)}, f32[512]{0:T(512)}, u32[]{:S(2)}) copy-start(f32[512]{0:T(512)} %param.10) | copy-start | bytes 6148
  12.2 22.2 %copy-start.3 = (s32[1,16]{1,0:T(1,128)S(1)}, s32[1,16]{1,0:T(1,128)}, u32[]{:S(2)}) copy-start(s32[1,16]{1,0:T(1,128)} %param.9) | copy-start | bytes 196
  29.4 22.4 %all-to-all-start.1 = ((bf16[16,64,512]{2,1,0:T(8,128)(2,1)}), bf16[16,64,512]{2,1,0:T(8,128)(2,1)}, u32[]{:S(2)}, u32[]{:S(2)}) async-start(bf16[16,64,512]{2,1,0:T(8,128)(2,1)} %send_blocks.3), calls=%async_computation.1 | async-start | bytes 2097152 | tf_op jit(solution)/shard_map/all_to_all | solution.py:774
  34.4 17.4 %copy-start.4 = (f32[512]{0:T(512)S(1)}, f32[512]{0:T(512)}, u32[]{:S(2)}) copy-start(f32[512]{0:T(512)} %param.12) | copy-start | bytes 6148
  74.4 32.1 %all-to-all-start.2 = ((bf16[16,64,512]{2,1,0:T(8,128)(2,1)}), bf16[16,64,512]{2,1,0:T(8,128)(2,1)}, u32[]{:S(2)}, u32[]{:S(2)}) async-start(bf16[16,64,512]{2,1,0:T(8,128)(2,1)} %get-tuple-element.42), calls=%async_computation.2 | async-start | bytes 2097152 | tf_op jit(solution)/shard_map/all_to_all | solution.py:781
  99.4 8.0 %collective-permute-start.1 = (bf16[2560,128]{1,0:T(8,128)(2,1)}, bf16[2560,128]{1,0:T(8,128)(2,1)}, u32[]{:S(2)}, u32[]{:S(2)}) collective-permute-start(bf16[2560,128]{1,0:T(8,128)(2,1)} %get-tuple-element.44), channel_id=1, source_target_pairs={{0,1},{1,0},{2,3},{3,2},{4,5},{5,4},{6,7},{7,6},{8,9},{9,8},{10,11... | collective-permute-start | bytes 1966088 | tf_op jit(solution)/shard_map/ppermute | solution.py:786
  106.5 2.8 %collective-permute-start = (bf16[2560,128]{1,0:T(8,128)(2,1)}, bf16[2560,128]{1,0:T(8,128)(2,1)S(1)}, u32[]{:S(2)}, u32[]{:S(2)}) collective-permute-start(bf16[2560,128]{1,0:T(8,128)(2,1)} %get-tuple-element.43), channel_id=1, source_target_pairs={{0,1},{1,0},{2,3},{3,2},{4,5},{5,4},{6,7},{7,6},{8,9},{9,8},{10,11... | collective-permute-start | bytes 1966088 | tf_op jit(solution)/shard_map/ppermute | solution.py:786
  139.9 23.9 %all-to-all-start.4 = ((bf16[64,80,128]{2,1,0:T(8,128)(2,1)}), bf16[64,80,128]{2,1,0:T(8,128)(2,1)S(1)}, u32[]{:S(2)}, u32[]{:S(2)}) async-start(bf16[64,80,128]{2,1,0:T(8,128)(2,1)} %broadcast_in_dim.2), calls=%async_computation.4 | async-start | bytes 2621440 | tf_op jit(solution)/shard_map/all_to_all | solution.py:791
  163.8 6.0 %collective-permute-start.2 = (bf16[5120,128]{1,0:T(8,128)(2,1)S(1)}, bf16[5120,128]{1,0:T(8,128)(2,1)S(1)}, u32[]{:S(2)}, u32[]{:S(2)}) collective-permute-start(bf16[5120,128]{1,0:T(8,128)(2,1)S(1)} %bitcast.11), channel_id=1, source_target_pairs={{0,1},{1,0},{2,3},{3,2},{4,5},{5,4},{6,7},{7,6},{8,9},{9,8},{10,11... | collective-permute-start | bytes 3932168 | tf_op jit(solution)/shard_map/ppermute | solution.py:800
  167.2 1.0 copy-start.1

commit v10 on v9

--- a/solution.py
+++ b/solution.py
@@ -783,8 +783,12 @@
     keep, *send = gradient_terms(own, d_hidden, saved[6], mixed, cot)
     swap = [(0, 1), (1, 0)]
     send[0], came_back = lax.optimization_barrier((send[0], came_back))
-    other = jnp.concatenate([lax.ppermute(part, "core", swap) for part in send])
-    chip_sum = (keep.astype(F32) + other.astype(F32)).astype(BF)
+    chip_sum = keep
+    for n in (1, 0):
+        other = lax.ppermute(send[n], "core", swap)
+        rows = slice(n * HALF // 2, (n + 1) * HALF // 2)
+        pair_sum = (keep[rows].astype(F32) + other.astype(F32)).astype(BF)
+        chip_sum = lax.dynamic_update_slice(chip_sum, pair_sum, (n * HALF // 2, 0))
     parts = lax.all_to_all(chip_sum.reshape(64, PART, LANES), ("grp", "chip"), 0, 0, tiled=True)
     total = (jnp.sum(parts.astype(F32), axis=0) * (1.0 / DEVICES)).astype(BF)
     copies = jnp.broadcast_to(total[None], (64, PART, LANES))

time: 173 us -> 172 us (level)
  Pallas kernels: 55.6 us -> 70.7 us
  starting transfers between devices: 38.6 us -> 30 us
  waiting for transfers between devices: 45.6 us -> 37.4 us
  other arithmetic: 1.68 us -> 3.52 us
    pallas_call x1, Pallas kernels: 22.6 us -> 32.5 us  [backward_layer(): pl.pallas_call(backward_kernel, out_shape=(pltpu.HBM((PEERS, BLOCK, D), B...]
    all_to_all x1, starting transfers between devices: 14.8 us -> 5.79 us  [per_device(): came_back = lax.all_to_all(send_back, ('chip', 'core'), 0, 0, tiled=True)]
    pallas_call x1, Pallas kernels: 12 us -> 17.4 us  [forward_layer(): pl.pallas_call(forward_kernel, out_shape=[pltpu.HBM((PAIRS, ROWS, LANES),...]
    all_to_all x1, waiting for transfers between devices: 5.31 us -> 0.01 us  [per_device(): lax.all_to_all(send_blocks(lens, own, cotangent), ('chip', 'core'), 0, 0,...]
    dynamic_update_slice x0 -> x2, other arithmetic: none -> 3.3 us  [per_device(): chip_sum = lax.dynamic_update_slice(chip_sum, pair_sum, (n * HALF // 2, 0))]
    ppermute x2, waiting for transfers between devices: 1.93 us -> 0.01 us  [per_device(): other = lax.ppermute(send[n], 'core', swap)]
  transfers between devices with their start and end apart: 7 -> 7, of which waited for: 5 -> 3; matrix products, arithmetic and copies ran while one was open for 0% -> 2% of each run, Pallas kernels for 17% -> 20%
where the time goes in v10:
time: 172 us
  Pallas kernels  70.7 us (41%)
  waiting for transfers between devices  37.4 us (22%)
  starting transfers between devices  30 us (17%)
  blocking collectives  26.1 us (15%)
  other arithmetic  3.52 us (2%)
  local copies, waits for them, and re-layouts  3.34 us (2%)
    pallas_call x1, Pallas kernels, backward_layer(): pl.pallas_call(backward_kernel, out_shape=(pltpu.HBM((PEERS, BLOCK, D), B...  32.5 us
    all_to_all x1, blocking collectives, per_device(): lax.all_to_all(chip_sum.reshape(64, PART, LANES), ('grp', 'chip'), 0, 0,...  26.1 us
    pallas_call x1, Pallas kernels, forward_layer(): pl.pallas_call(forward_kernel, out_shape=[pltpu.HBM((PAIRS, ROWS, LANES),...  17.4 us
    all_to_all x1, waiting for transfers between devices, per_device(): lax.all_to_all(copies, ('grp', 'chip'), 0, 0, tiled=True)  16.7 us
    all_to_all x1, waiting for transfers between devices, per_device(): lax.all_to_all(send_blocks(lens, own, events), ('chip', 'core'), 0, 0, ti...  14.9 us
    pallas_call x1, Pallas kernels, gradient_terms(): pl.pallas_call(terms_kernel, out_shape=(half, quarter, quarter), in_specs...  10.2 us
    all_to_all x1, starting transfers between devices, per_device(): lax.all_to_all(send_blocks(lens, own, events), ('chip', 'core'), 0, 0, ti...  9.29 us
    all_to_all x1, starting transfers between devices, per_device(): came_back = lax.all_to_all(send_back, ('chip', 'core'), 0, 0, tiled=True)  5.79 us
  transfers between devices with their start and end apart: 7, of which 3 were waited for; matrix products, arithmetic and copies ran while one was open for 2% of the time, Pallas kernels for 20%

profile of v10, /device:TPU:1, one launch (start us, length us, event | category | flops | bytes accessed | tf_op | source)
XLA Modules:
  0.0 172.0 jit_solution(255268653647926184)
XLA Ops:
  0.6 2.2 %send_blocks.2 = bf16[16,64,512]{2,1,0:T(8,128)(2,1)} custom-call(s32[16]{0:T(128)} %bitcast.16, s32[1]{0:T(128)} %bitcast.own_ref, bf16[8,64,512]{2,1,0:T(8,128)(2,1)} %bitcast.24), custom_call_target="tpu_custom_call" | custom-call | tf_op jit(solution)/shard_map/send_blocks/pallas_call | solution.py:677
  2.9 9.3 %all-to-all-start = ((bf16[16,64,512]{2,1,0:T(8,128)(2,1)}), bf16[16,64,512]{2,1,0:T(8,128)(2,1)S(1)}, u32[]{:S(2)}, u32[]{:S(2)}) async-start(bf16[16,64,512]{2,1,0:T(8,128)(2,1)} %send_blocks.2), calls=%async_computation | async-start | bytes 2097152 | tf_op jit(solution)/shard_map/all_to_all | solution.py:773
  12.2 0.0 copy-start.2
  12.2 2.3 %send_blocks.3 = bf16[16,64,512]{2,1,0:T(8,128)(2,1)} custom-call(s32[16]{0:T(128)} %bitcast.17, s32[1]{0:T(128)} %bitcast.own_ref, bf16[8,64,512]{2,1,0:T(8,128)(2,1)} %bitcast.25), custom_call_target="tpu_custom_call" | custom-call | tf_op jit(solution)/shard_map/send_blocks/pallas_call | solution.py:677
  14.5 0.0 copy-start
  14.5 0.0 copy-start.3
  14.5 14.9 %all-to-all-done.got_ref.got_in = bf16[16,64,512]{2,1,0:T(8,128)(2,1)S(1)} async-done(((bf16[16,64,512]{2,1,0:T(8,128)(2,1)}), bf16[16,64,512]{2,1,0:T(8,128)(2,1)S(1)}, u32[]{:S(2)}, u32[]{:S(2)}) %all-to-all-start) | async-done | bytes 1048608 | tf_op jit(solution)/shard_map/all_to_all | solution.py:773
  29.4 5.0 %all-to-all-start.1 = ((bf16[16,64,512]{2,1,0:T(8,128)(2,1)}), bf16[16,64,512]{2,1,0:T(8,128)(2,1)}, u32[]{:S(2)}, u32[]{:S(2)}) async-start(bf16[16,64,512]{2,1,0:T(8,128)(2,1)} %send_blocks.3), calls=%async_computation.1 | async-start | bytes 2097152 | tf_op jit(solution)/shard_map/all_to_all | solution.py:774
  34.4 0.0 copy-done.2
  34.4 0.0 copy-done
  34.4 0.0 copy-done.3
  34.4 0.0 copy-start.4
  34.4 17.4 %forward_layer.1 = (bf16[4,1024,128]{2,1,0:T(8,128)(2,1)}, bf16[1024,512]{1,0:T(8,128)(2,1)}, bf16[4,1024,128]{2,1,0:T(8,128)(2,1)}, bf16[4,1024,128]{2,1,0:T(8,...) custom-call(s32[16]{0:T(128)S(1)} %bitcast.19, ...), custom_call_target="tpu_custom_call" | custom-call | tf_op jit(solution)/shard_map/forward_layer/pallas_call | solution.py:693
  51.8 0.0 all-to-all-done.1.grads_in
  51.8 0.0 copy-done.4
  51.8 32.5 %backward_layer.1 = (bf16[16,64,512]{2,1,0:T(8,128)(2,1)}, bf16[16,1024,128]{2,1,0:T(8,128)(2,1)}, bf16[1024,512]{1,0:T(8,128)(2,1)}, bf16[1024,512]{1,0:T(8,128)(2,1)}) custom-call(s32[16]{0:T(128)S(1)} %bitcast.20, s32[1]{0:T(128)} %bitcast.own_ref, bf16[16,64,512]{2,1,0:T(8,128)(2,1)S(1)} %all-to-all-done.got_ref.got_in, ...), custom_call_target="tpu_custom_call" | custom-call | tf_op jit(solution)/shard_map/backward_layer/pallas_call | solution.py:710
  84.4 5.8 %all-to-all-start.2 = ((bf16[16,64,512]{2,1,0:T(8,128)(2,1)}), bf16[16,64,512]{2,1,0:T(8,128)(2,1)}, u32[]{:S(2)}, u32[]{:S(2)}) async-start(bf16[16,64,512]{2,1,0:T(8,128)(2,1)} %get-tuple-element.43), calls=%async_computation.2 | async-start | bytes 2097152 | tf_op jit(solution)/shard_map/all_to_all | solution.py:781
  90.2 10.2 %gradient_terms.1 = (bf16[5120,128]{1,0:T(8,128)(2,1)S(1)}, bf16[2560,128]{1,0:T(8,128)(2,1)}, bf16[2560,128]{1,0:T(8,128)(2,1)}) custom-call(s32[1]{0:T(128)} %bitcast.own_ref, bf16[16,1024,128]{2,1,0:T(8,128)(2,1)} %get-tuple-element.36.d_hidden_in, bf16[1024,512]{1,0:T(8,128)(2,1)} %get-tuple-element.37.scaled_in, ...), custom_call_target="tpu_custom_call" | custom-call | flops 2684354560 | bytes 10485760 | tf_op jit(solution)/shard_map/gradient_terms/pallas_call | solution.py:745
  100.4 0.2 collective-permute-start
  100.6 1.1 copy.14
  101.7 5.8 %all-to-all-done.2.back_ref = bf16[16,64,512]{2,1,0:T(8,128)(2,1)} async-done(((bf16[16,64,512]{2,1,0:T(8,128)(2,1)}), bf16[16,64,512]{2,1,0:T(8,128)(2,1)}, u32[]{:S(2)}, u32[]{:S(2)}) %all-to-all-start.2) | async-done | bytes 1048608 | tf_op jit(solution)/shard_map/all_to_all | solution.py:781
  107.5 0.9 collective-permute-start.1
  108.4 0.0 collective-permute-done
  108.4 2.3 %fusion = bf16[5120,128]{1,0:T(8,128)(2,1)} fusion(bf16[5120,128]{1,0:T(8,128)(2,1)} %copy.14, bf16[2560,128]{1,0:T(8,128)(2,1)} %collective-permute-done), kind=kLoop, calls=%fused_computation.3 | loop fusion | flops 1310720 | bytes 1966080 | tf_op jit(solution)/shard_map/dynamic_update_slice | solution.py:791
  110.7 0.0 collective-permute-done.1
  110.7 1.0 fusion.1
  111.7 26.1 %all_to_all.25 = bf16[64,80,128]{2,1,0:T(8,128)(2,1)S(1)} all-to-all(bf16[64,80,128]{2,1,0:T(8,128)(2,1)} %bitcast.23), channel_id=1, replica_groups=mesh['grp'=8,'chip'=8,'core'=2] {'grp','chip'}, dimensions={0} | all-to-all | bytes 2621440 | tf_op jit(solution)/shard_map/all_to_all | solution.py:792
  137.8 0.2 convert_reduce_fusion
  138.0 1.2 broadcast_in_dim.2
  139.2 5.4 %all-to-all-start.4 = ((bf16[64,80,128]{2,1,0:T(8,128)(2,1)}), bf16[64,80,128]{2,1,0:T(8,128)(2,1)S(1)}, u32[]{:S(2)}, u32[]{:S(2)}) async-start(bf16[64,80,128]{2,1,0:T(8,128)(2,1)} %broadcast_in_dim.2), calls=%async_computation.4 | async-start | bytes 2621440 | tf_op jit(solution)/shard_map/all_to_all | solution.py:795
  144.6 2.2 %take_home.1 = bf16[8,64,512]{2,1,0:T(8,128)(2,1)} custom-call(s32[16]{0:T(128)} %bitcast.18, s32[1]{0:T(128)} %bitcast.own_ref, bf16[16,64,512]{2,1,0:T(8,128)(2,1)} %all-to-all-done.2.back_ref), custom_call_target="tpu_custom_call" | custom-call | tf_op jit(solution)/shard_map/take_home/pallas_call | solution.py:796
  146.8 16.7 %all-to-all-done.4 = bf16[64,80,128]{2,1,0:T(8,128)(2,1)S(1)} async-done(((bf16[64,80,128]{2,1,0:T(8,128)(2,1)}), bf16[64,80,128]{2,1,0:T(8,128)(2,1)S(1)}, u32[]{:S(2)}, u32[]{:S(2)}) %all-to-all-start.4) | async-done | bytes 1310752 | tf_op jit(solution)/shard_map/all_to_all | solution.py:795
  163.6 3.4 %collective-permute-start.2 = (bf16[5120,128]{1,0:T(8,128)(2,1)S(1)}, bf16[5120,128]{1,0:T(8,128)(2,1)S(1)}, u32[]{:S(2)}, u32[]{:S(2)}) collective-permute-start(bf16[5120,128]{1,0:T(8,128)(2,1)S(1)} %bitcast.11), channel_id=1, source_target_pairs={{0,1},{1,0},{2,3},{3,2},{4,5},{5,4},{6,7},{7,6},{8,9},{9,8},{10,11... | collective-permute-start | bytes 3932168 | tf_op jit(solution)/shard_map/ppermute | solution.py:804
  166.9 0.0 copy-start.1
  166.9 1.0 copy-done.1
  168.0 1.6 spread_mine.1
  169.6 0.0 collective-permute-done.2.other_ref
  169.6 2.2 %spread_other.1 = (f32[512,2048]{1,0:T(8,128)}, f32[512,512]{1,0:T(8,128)}, f32[1,512]{1,0:T(1,128)}, f32[1,512]{1,0:T(1,128)}) custom-call(s32[1]{0:T(128)} %bitcast.own_ref, bf16[5120,128]{1,0:T(8,128)(2,1)S(1)} %collective-permute-done.2.other_ref, bf16[512,2048]{1,0:T(8,128)(2,1)S(1)} %copy-done, ...), custom_call_target="tpu_custom_call", output_to_operand_aliasing={{0}: (7, {}), {1}: (8, {})} | custom-call | tf_op jit(solution)/shard_map/spread_other/pallas_call | solution.py:818
  (1 shorter events, 0.0 us)
Async XLA Ops:
  2.9 26.5 %all-to-all-start = ((bf16[16,64,512]{2,1,0:T(8,128)(2,1)}), bf16[16,64,512]{2,1,0:T(8,128)(2,1)S(1)}, u32[]{:S(2)}, u32[]{:S(2)}) async-start(bf16[16,64,512]{2,1,0:T(8,128)(2,1)} %send_blocks.2), calls=%async_computation | async-start | bytes 2097152 | tf_op jit(solution)/shard_map/all_to_all | solution.py:773
  12.2 22.2 %copy-start.2 = (f32[512]{0:T(512)S(1)}, f32[512]{0:T(512)}, u32[]{:S(2)}) copy-start(f32[512]{0:T(512)} %param.10) | copy-start | bytes 6148
  14.5 19.9 %copy-start = (bf16[512,2048]{1,0:T(8,128)(2,1)S(1)}, bf16[512,2048]{1,0:T(8,128)(2,1)}, u32[]{:S(2)}) copy-start(bf16[512,2048]{1,0:T(8,128)(2,1)} %w_ref.5) | copy-start | bytes 6291460
  14.5 19.9 %copy-start.3 = (s32[1,16]{1,0:T(1,128)S(1)}, s32[1,16]{1,0:T(1,128)}, u32[]{:S(2)}) copy-start(s32[1,16]{1,0:T(1,128)} %param.9) | copy-start | bytes 196
  29.4 22.4 %all-to-all-start.1 = ((bf16[16,64,512]{2,1,0:T(8,128)(2,1)}), bf16[16,64,512]{2,1,0:T(8,128)(2,1)}, u32[]{:S(2)}, u32[]{:S(2)}) async-start(bf16[16,64,512]{2,1,0:T(8,128)(2,1)} %send_blocks.3), calls=%async_computation.1 | async-start | bytes 2097152 | tf_op jit(solution)/shard_map/all_to_all | solution.py:774
  34.4 17.4 %copy-start.4 = (f32[512]{0:T(512)S(1)}, f32[512]{0:T(512)}, u32[]{:S(2)}) copy-start(f32[512]{0:T(512)} %param.12) | copy-start | bytes 6148
  84.4 23.1 %all-to-all-start.2 = ((bf16[16,64,512]{2,1,0:T(8,128)(2,1)}), bf16[16,64,512]{2,1,0:T(8,128)(2,1)}, u32[]{:S(2)}, u32[]{:S(2)}) async-start(bf16[16,64,512]{2,1,0:T(8,128)(2,1)} %get-tuple-element.43), calls=%async_computation.2 | async-start | bytes 2097152 | tf_op jit(solution)/shard_map/all_to_all | solution.py:781
  100.4 8.0 %collective-permute-start = (bf16[2560,128]{1,0:T(8,128)(2,1)}, bf16[2560,128]{1,0:T(8,128)(2,1)}, u32[]{:S(2)}, u32[]{:S(2)}) collective-permute-start(bf16[2560,128]{1,0:T(8,128)(2,1)} %get-tuple-element.41), channel_id=1, source_target_pairs={{0,1},{1,0},{2,3},{3,2},{4,5},{5,4},{6,7},{7,6},{8,9},{9,8},{10,11... | collective-permute-start | bytes 1966088 | tf_op jit(solution)/shard_map/ppermute | solution.py:788
  107.5 3.2 %collective-permute-start.1 = (bf16[2560,128]{1,0:T(8,128)(2,1)}, bf16[2560,128]{1,0:T(8,128)(2,1)S(1)}, u32[]{:S(2)}, u32[]{:S(2)}) collective-permute-start(bf16[2560,128]{1,0:T(8,128)(2,1)} %get-tuple-element.44), channel_id=1, source_target_pairs={{0,1},{1,0},{2,3},{3,2},{4,5},{5,4},{6,7},{7,6},{8,9},{9,8},{10,11... | collective-permute-start | bytes 1966088 | tf_op jit(solution)/shard_map/ppermute | solution.py:788
  139.2 24.4 %all-to-all-start.4 = ((bf16[64,80,128]{2,1,0:T(8,128)(2,1)}), bf16[64,80,128]{2,1,0:T(8,128)(2,1)S(1)}, u32[]{:S(2)}, u32[]{:S(2)}) async-start(bf16[64,80,128]{2,1,0:T(8,128)(2,1)} %broadcast_in_dim.2), calls=%async_computation.4 | async-start | bytes 2621440 | tf_op jit(solution)/shard_map/all_to_all | solution.py:795
  163.6 6.0 %collective-permute-start.2 = (bf16[5120,128]{1,0:T(8,128)(2,1)S(1)}, bf16[5120,128]{1,0:T(8,128)(2,1)S(1)}, u32[]{:S(2)}, u32[]{:S(2)}) collective-permute-start(bf16[5120,128]{1,0:T(8,128)(2,1)S(1)} %bitcast.11), channel_id=1, source_target_pairs={{0,1},{1,0},{2,3},{3,2},{4,5},{5,4},{6,7},{7,6},{8,9},{9,8},{10,11... | collective-permute-start | bytes 3932168 | tf_op jit(solution)/shard_map/ppermute | solution.py:804
  166.9 1.0 copy-start.1
